TPU v7x, 32 devices: a whole 2x2x4 slice. The times are simulated.
32 devices in a mesh: group: 8 (over z, core), dev: 4 (over y, x).
Axes of the slice: x: 2, y: 2, z: 4, core: 2. Of those that a mesh axis runs over, the one named last changes fastest.
Arguments:
- tiles: bfloat16 [2304, 5, 128, 128], P(('group', 'dev')), may hold values from 0.00029945374 to 0.029907227
- tile_col: int32 [2304, 5], P(('group', 'dev')), may hold values from 0 to 15
- strip_group: int32 [2304], P(('group', 'dev')), may hold values from 0 to 7, as said below
- strip_slot: int32 [2304], P(('group', 'dev')), may hold values from 0 to 15
- live_count: int32 [32], P(('group', 'dev')), may hold values from 36 to 72, as said below
- omega: bfloat16 [16384, 128], P(('group', 'dev')), may hold values from -40 to 40
- idf: float32 [65536], P(('group', 'dev')), may hold values from 0.4 to 20
Outputs:
- q_basis: float32 [65536, 128], P(('group', 'dev'))
- doc_factor: bfloat16 [128, 16384], P(None, ('group', 'dev'))
Inputs may be any that keep to these rules, and one draw needn't show every extreme that they name: `strip_group`: among the 72 strips of one device at most 12 name one group; in every draw one group is named by exactly 12 strips of every device. `live_count`: some device has all 72 strips live.
All inputs are finite; a program needn't handle non-finite values.
Results may differ from a plain program's by a relative error of at most 0.0034.
Values may be sent and summed in bfloat16 or wider, within the bound.
No kernel may reach another device: no remote copies, remote signals or barrier semaphores. Data moves between devices by JAX's collectives and lax.ppermute only.
A program may use at most 128 MiB of HBM per device.

v0:
```python
import jax
import jax.numpy as jnp
from jax import lax
from jax.sharding import PartitionSpec as P


def on_device(tiles, tile_col, strip_group, strip_slot, live_count, omega, idf):
    n_group = lax.axis_size("group")
    n_dev = lax.axis_size("dev")
    strips = tiles.shape[0]
    tile_edge = tiles.shape[2]
    sketch_cols = omega.shape[1]
    owned_blocks = idf.shape[0] // tile_edge
    capacity = max(2, (4 * strips + 3 * n_group - 1) // (3 * n_group))
    alive_mask = (jnp.arange(strips) < live_count[0]).astype(jnp.float32)
    group_omega = lax.all_gather(omega, "dev", axis=0, tiled=True)
    omega_blocks = group_omega.reshape(-1, tile_edge, sketch_cols)
    picked = omega_blocks[tile_col]
    partial_value = jnp.einsum("stij,stjk->sik", tiles, picked, preferred_element_type=jnp.float32)
    partial_value = partial_value * alive_mask[:, None, None]
    member = (strip_group[:, None] == jnp.arange(n_group)[None, :]).astype(jnp.int32)
    rank_in = jnp.sum((jnp.cumsum(member, axis=0) - member) * member, axis=1)
    position = strip_group * capacity + rank_in
    labels = jnp.where(alive_mask > 0, strip_slot, -1).astype(jnp.float32)
    outgoing = (
        jnp.zeros((n_group * capacity, tile_edge, sketch_cols), jnp.float32)
        .at[position]
        .set(partial_value)
    )
    out_labels = jnp.full((n_group * capacity,), -1.0, jnp.float32).at[position].set(labels)
    arrived, arrived_labels = (
        lax.all_to_all(
            outgoing.reshape(n_group, capacity, tile_edge, sketch_cols),
            "group",
            split_axis=0,
            concat_axis=0,
            tiled=True,
        ),
        lax.all_to_all(
            out_labels.reshape(n_group, capacity), "group", split_axis=0, concat_axis=0, tiled=True
        ),
    )
    slot_ids = arrived_labels.reshape(-1).astype(jnp.int32)
    chooser = (jnp.arange(owned_blocks)[:, None] == slot_ids[None, :]).astype(jnp.float32)
    owned_rows = jnp.einsum(
        "rs,sik->rik",
        chooser,
        arrived.reshape(-1, tile_edge, sketch_cols),
        precision=lax.Precision.HIGHEST,
        preferred_element_type=jnp.float32,
    )
    sketch = owned_rows.reshape(-1, sketch_cols) * idf[:, None]
    total_terms = idf.shape[0] * n_group * n_dev
    local_gram = lax.dot_general(
        sketch,
        sketch,
        (((0,), (0,)), ((), ())),
        precision=lax.Precision.HIGHEST,
        preferred_element_type=jnp.float32,
    )
    gram_matrix = lax.psum(local_gram, ("group", "dev")) / total_terms
    lower_factor = jnp.linalg.cholesky(gram_matrix)
    q_basis = jax.scipy.linalg.solve_triangular(lower_factor, sketch.T, lower=True).T
    weighted = (
        (idf[:, None] * q_basis).astype(jnp.bfloat16).reshape(owned_blocks, tile_edge, sketch_cols)
    )
    band_rows = lax.all_gather(weighted, "group", axis=0, tiled=True)
    strip_q = band_rows[strip_group * owned_blocks + strip_slot]
    strip_q = strip_q * alive_mask.astype(jnp.bfloat16)[:, None, None]
    contrib = jnp.einsum("sik,stij->stkj", strip_q, tiles, preferred_element_type=jnp.float32)
    col_blocks = n_dev * (omega.shape[0] // tile_edge)
    doc_part = jax.ops.segment_sum(
        contrib.reshape(-1, sketch_cols, tile_edge), tile_col.reshape(-1), num_segments=col_blocks
    )
    my_docs = lax.psum_scatter(doc_part, "dev", scatter_dimension=0, tiled=True)
    doc_factor = jnp.transpose(my_docs, (1, 0, 2)).reshape(sketch_cols, -1).astype(jnp.bfloat16)
    return (q_basis, doc_factor)


def solution(mesh):
    placed = (
        P(("group", "dev"), None, None, None),
        P(("group", "dev"), None),
        P(("group", "dev")),
        P(("group", "dev")),
        P(("group", "dev")),
        P(("group", "dev"), None),
        P(("group", "dev")),
    )
    return jax.shard_map(
        on_device,
        mesh=mesh,
        in_specs=placed,
        out_specs=(P(("group", "dev"), None), P(None, ("group", "dev"))),
        check_vma=False,
    )
```

profile of v0, /device:TPU:0, one launch (start us, length us, event | category | flops | bytes accessed | tf_op | source)
XLA Modules:
  0.0 527.5 jit_solution(2830530185264732526)
XLA Ops:
  7.8 0.7 fusion.14
  8.5 0.1 reduce_window_sum.11
  8.7 0.8 select_reduce_fusion.1
  9.5 0.7 compare_select_fusion.1
  10.2 0.8 scatter_custom_fusion
  11.0 0.7 all_to_all.9
  11.7 6.4 %all-to-all-start = ((f32[8,1,12]{2,1,0:T(1,128)}), f32[8,1,12]{2,1,0:T(1,128)S(1)}, u32[]{:S(2)}, u32[]{:S(2)}) async-start(f32[8,1,12]{2,1,0:T(1,128)} %bitcast.1), calls=%async_computation | async-start | bytes 8192 | tf_op jit(solution)/shard_map/all_to_all | solution.py:39
  18.0 11.5 %all_gather.6 = bf16[2048,128]{1,0:T(8,128)(2,1)S(1)} all-gather(bf16[512,128]{1,0:T(8,128)(2,1)} %param.12), channel_id=1, replica_groups=mesh['group'=8,'dev'=4] {'dev'}, dimensions={0}, use_global_device_ids=true | all-gather | bytes 655360 | tf_op jit(solution)/shard_map/all_gather | solution.py:16
  29.5 0.7 compare_select_fusion
  30.2 0.1 copy.41
  30.3 0.1 reshape.77
  30.5 11.1 %gather_fusion = bf16[360,128,128]{2,1,0:T(8,128)(2,1)} fusion(bf16[16,128,128]{2,1,0:T(8,128)(2,1)S(1)} %bitcast.53, s32[1024]{0:T(1024)S(1)} %pad_clamp_fusion.1), kind=kCustom, calls=%fused_computation | custom fusion | bytes 23594400 | tf_op jit(solution)/shard_map/gather | solution.py:18
  41.6 11.8 %fusion.2 = f32[72,128,128]{1,2,0:T(8,128)} fusion(f32[72]{0:T(128)S(1)} %compare_convert_fusion, bf16[72,5,128,128]{3,2,1,0:T(8,128)(2,1)} %bitcast.55, bf16[72,5,128,128]{3,2,1,0:T(8,128)(2,1)} %param.7), kind=kOutput, calls=%fused_computation.8 | convolution fusion | flops 1511129088 | bytes 28311840 | tf_op jit(solution)/shard_map/stij,stjk->sik/dot_general | solution.py:19
  53.4 6.1 %copy.43 = f32[72,128,128]{2,1,0:T(8,128)} copy(f32[72,128,128]{1,2,0:T(8,128)} %fusion.2) | data formatting | bytes 9437184 | tf_op jit(solution)/shard_map/mul | solution.py:20
  59.4 3.4 broadcast_in_dim.36
  62.9 14.5 %scatter_fusion = f32[96,128,128]{2,1,0:T(8,128)} fusion(f32[96,128,128]{2,1,0:T(8,128)} %broadcast_in_dim.36, s32[72]{0:T(128)S(1)} %get-tuple-element.7, f32[72,128,128]{2,1,0:T(8,128)} %copy.43), kind=kCustom, calls=%fused_computation.3 | custom fusion | bytes 14156064 | tf_op jit(solution)/shard_map/scatter | solution.py:28
  77.4 4.9 all-to-all-start.1
  82.2 0.2 all-reduce.2.cloned.1.call-start
  82.5 0.1 copy.45
  82.6 0.1 convert_element_type.50
  82.7 138.5 %all-to-all-done.1 = f32[8,12,128,128]{3,2,1,0:T(8,128)} async-done(((f32[8,12,128,128]{3,2,1,0:T(8,128)}), f32[8,12,128,128]{3,2,1,0:T(8,128)}, u32[]{:S(2)}, u32[]{:S(2)}) %all-to-all-start.1) | async-done | bytes 6291488 | tf_op jit(solution)/shard_map/all_to_all | solution.py:32
  221.2 8.3 %fusion.6 = f32[16,128,128]{2,0,1:T(8,128)S(1)} fusion(f32[96,128,128]{2,1,0:T(8,128)} %bitcast.9, f32[16,128]{0,1:T(8,128)S(1)} %copy.45, s32[96]{0:T(128)S(1)} %convert_element_type.50), kind=kOutput, calls=%fused_computation.12 | convolution fusion | flops 302253568 | bytes 7348608 | tf_op jit(solution)/shard_map/rs,sik->rik/dot_general | solution.py:45
  229.5 2.4 convolution_bitcast_fusion
  231.9 0.0 all-reduce.2.cloned.1.call-update
  232.0 0.3 all-gather.2.cloned.1.call-start
  232.2 0.3 copy.46
  232.6 116.8 %all-reduce.2.cloned.1.call-done = f32[128,128]{0,1:T(8,128)} async-done(((f32[128,128]{0,1:T(8,128)}), f32[128,128]{0,1:T(8,128)}) %all-reduce.2.cloned.1.call-update) | async-done | bytes 65552 | tf_op jit(solution)/shard_map/psum | solution.py:61
  349.3 0.8 broadcast_multiply_fusion
  350.2 0.1 copy.48
  350.3 0.9 fusion.13
  351.1 11.7 %cholesky.16 = f32[128,128]{1,0:T(8,128)S(1)} custom-call(f32[128,128]{1,0:T(8,128)S(1)} %fusion.13), custom_call_target="Cholesky" | custom-call | tf_op jit(solution)/shard_map/jit(cholesky)/cholesky | solution.py:62
  362.9 0.6 compare_reduce_fusion
  363.5 0.7 fusion.10
  364.2 9.8 %custom-call.7 = f32[1,128,128]{1,2,0:T(8,128)S(1)} custom-call(f32[1,128,128]{2,1,0:T(8,128)S(1)} %fusion.10), custom_call_target="InvertDiagBlocksLowerTriangular" | custom-call | tf_op jit(solution)/shard_map/jit(_solve_triangular)/triangular_solve | solution.py:63
  374.0 2.1 multiply_convert_fusion
  376.2 0.3 reduce-scatter.2.cloned.1.call-start
  376.5 0.1 copy.49
  376.6 0.1 reshape.109
  376.7 47.7 %all-gather.2.cloned.1.call-done = bf16[128,128,128]{2,1,0:T(8,128)(2,1)} async-done(((bf16[16,128,128]{2,1,0:T(8,128)(2,1)}), bf16[128,128,128]{2,1,0:T(8,128)(2,1)}) %all-gather.2.cloned.1.call-update) | async-done | bytes 4194320 | tf_op jit(solution)/shard_map/all_gather | solution.py:67
  424.4 3.2 gather_fusion.1
  427.6 15.5 %fusion.3 = f32[72,128,5,128]{3,1,2,0:T(8,128)} fusion(bf16[72,5,128,128]{3,2,1,0:T(8,128)(2,1)} %param.7, bf16[72,128,128]{2,1,0:T(8,128)(2,1)S(1)} %gather_fusion.1, bf16[72]{0:T(256)(128)(2,1)S(1)} %fusion.21), kind=kOutput, calls=%fused_computation.9 | convolution fusion | flops 1514668032 | bytes 37748880 | tf_op jit(solution)/shard_map/sik,stij->stkj/dot_general | solution.py:70
  443.1 0.1 broadcast_in_dim.38
  443.2 47.9 %scatter_fusion.1 = f32[16,128,128]{2,1,0:T(8,128)S(1)} fusion(f32[16,128,128]{2,1,0:T(8,128)S(1)} %broadcast_in_dim.38, s32[360]{0:T(512)S(1)} %reshape.109, f32[360,128,128]{2,1,0:T(8,128)} %bitcast.54), kind=kCustom, calls=%fused_computation.4 | custom fusion | flops 5898240 | bytes 70780320 | tf_op jit(solution)/shard_map/scatter-add | solution.py:72
  491.1 1.0 copy-done
  492.2 26.9 %reduce-scatter.2.cloned.1.call-done = f32[4,128,128]{2,1,0:T(8,128)} async-done(((f32[16,128,128]{2,1,0:T(8,128)}), f32[4,128,128]{2,1,0:T(8,128)}) %reduce-scatter.2.cloned.1.call-update) | async-done | bytes 262160 | tf_op jit(solution)/shard_map/reduce_scatter | solution.py:75
  519.1 1.0 convert_bitcast_fusion
  520.0 0.1 copy.51
  520.2 0.8 copy.52
  (14 shorter events, 0.1 us)
Async XLA Ops:
  11.7 65.7 %all-to-all-start = ((f32[8,1,12]{2,1,0:T(1,128)}), f32[8,1,12]{2,1,0:T(1,128)S(1)}, u32[]{:S(2)}, u32[]{:S(2)}) async-start(f32[8,1,12]{2,1,0:T(1,128)} %bitcast.1), calls=%async_computation | async-start | bytes 8192 | tf_op jit(solution)/shard_map/all_to_all | solution.py:39
  77.4 5.1 copy-start.1
  77.4 143.8 %all-to-all-start.1 = ((f32[8,12,128,128]{3,2,1,0:T(8,128)}), f32[8,12,128,128]{3,2,1,0:T(8,128)}, u32[]{:S(2)}, u32[]{:S(2)}) async-start(f32[8,12,128,128]{3,2,1,0:T(8,128)} %bitcast.56), calls=%async_computation.1 | async-start | bytes 12582912 | tf_op jit(solution)/shard_map/all_to_all | solution.py:32
  82.2 267.1 %all-reduce.2.cloned.1.call-start = ((), (), s32[]{:S(2)}) async-start(), calls=%async_computation.3 | async-start | bytes 131072 | tf_op jit(solution)/shard_map/psum | solution.py:61
  221.2 155.3 %copy-start.2 = (s32[72,5]{0,1:T(8,128)S(1)}, s32[72,5]{0,1:T(8,128)}, u32[]{:S(2)}) copy-start(s32[72,5]{0,1:T(8,128)} %param.8) | copy-start | bytes 4324
  232.0 192.5 %all-gather.2.cloned.1.call-start = ((), (), s32[]{:S(2)}) async-start(), calls=%async_computation.4 | async-start | bytes 4718592 | tf_op jit(solution)/shard_map/all_gather | solution.py:67
  376.2 142.9 %reduce-scatter.2.cloned.1.call-start = ((), (), s32[]{:S(2)}) async-start(), calls=%async_computation.5 | async-start | bytes 1310720 | tf_op jit(solution)/shard_map/reduce_scatter | solution.py:75
  491.1 1.0 copy-start
Sparse Core Ops, SparseCore 0:
  232.1 117.2 all-reduce.1
  376.3 48.0 all-gather.1
  492.3 26.7 reduce-scatter.1
where the time goes:
time: 529 us; the launch traced here: 527 us
  waiting for transfers between devices  330 us (62%)
  other arithmetic  76.6 us (14%)
  local copies, waits for them, and re-layouts  42.8 us (8%)
  matrix products  40.1 us (8%)
  between operations  14.6 us (3%)
  starting transfers between devices  12 us (2%)
  blocking collectives  11.5 us (2%)
    all_to_all x1, waiting for transfers between devices, on_device(): lax.all_to_all(outgoing.reshape(n_group, capacity, tile_edge, sketch_cols...  138 us
    psum x1, waiting for transfers between devices, on_device(): gram_matrix = lax.psum(local_gram, ('group', 'dev')) / total_terms  117 us
    scatter-add x1, other arithmetic, on_device(): jax.ops.segment_sum(contrib.reshape(-1, sketch_cols, tile_edge), tile_col...  47.9 us
    all_gather x1, waiting for transfers between devices, on_device(): band_rows = lax.all_gather(weighted, 'group', axis=0, tiled=True)  47.7 us
    reduce_scatter x1, waiting for transfers between devices, on_device(): my_docs = lax.psum_scatter(doc_part, 'dev', scatter_dimension=0, tiled=True)  26.9 us
    dot_general x1, matrix products, on_device(): jnp.einsum('sik,stij->stkj', strip_q, tiles, preferred_element_type=jnp.f...  15.5 us
    scatter x1, local copies, waits for them, and re-layouts, on_device(): outgoing = jnp.zeros((n_group * capacity, tile_edge, sketch_cols), jnp.fl...  14.5 us
    another operation x3, other arithmetic, on_device(): lower_factor = jnp.linalg.cholesky(gram_matrix)  12.4 us
  transfers between devices with their start and end apart: 5, of which 4 were waited for; matrix products, arithmetic and copies ran while one was open for 9% of the time, Pallas kernels for 0%

commit v1 on v0

v1 whole, which is shorter than its diff:
```python
import functools
import jax
import jax.numpy as jnp
from jax import lax
from jax.experimental import pallas as pl
from jax.experimental.pallas import tpu as pltpu
from jax.sharding import PartitionSpec as P

F32 = jnp.float32
BF16 = jnp.bfloat16
HIGHEST = lax.Precision.HIGHEST


def strips_per_step(strips, most=8):
    return max(s for s in range(1, most + 1) if strips % s == 0)


def sketch_kernel(owned, step_strips, group_ref, slot_ref, col_ref, live_ref, place_ref,
                  tiles_ref, omega_ref, mine_ref, theirs_ref, acc_ref, out_ref, sems):
    step = pl.program_id(0)
    tpi = tiles_ref.shape[1]
    half = mine_ref.shape[0]
    core = place_ref[0] % 2

    @pl.when(step == 0)
    def _():
        acc_ref[...] = jnp.zeros_like(acc_ref)

    for i in range(step_strips):
        strip = step * step_strips + i

        @pl.when(strip < live_ref[0])
        def _():
            owner = group_ref[strip]
            side = jnp.where(owner % 2 == core, 0, 1)
            block = side * half + (owner // 2) * owned + slot_ref[strip]
            left = jnp.concatenate([tiles_ref[i, j] for j in range(tpi)], axis=1)
            right = jnp.concatenate([omega_ref[col_ref[strip, j]] for j in range(tpi)], axis=0)
            acc_ref[block] += jnp.dot(left, right, preferred_element_type=F32)

    @pl.when(step == pl.num_programs(0) - 1)
    def _():
        keep = pltpu.make_async_copy(acc_ref.at[pl.ds(0, half)], mine_ref, sems.at[0])
        keep.start()
        out_ref[...] = acc_ref[pl.ds(half, half)].astype(BF16)
        give = pltpu.make_async_copy(out_ref, theirs_ref, sems.at[1])
        give.start()
        keep.wait()
        give.wait()


def partial_sketch(group, slot, col, live, place, tiles, omega_blocks, n_group, owned):
    strips, tpi, edge, _ = tiles.shape
    cols = omega_blocks.shape[-1]
    per = strips_per_step(strips)
    half = n_group // 2 * owned
    return pl.pallas_call(
        functools.partial(sketch_kernel, owned, per),
        out_shape=(
            jax.ShapeDtypeStruct((half, edge, cols), F32),
            jax.ShapeDtypeStruct((half, edge, cols), BF16),
        ),
        grid_spec=pltpu.PrefetchScalarGridSpec(
            num_scalar_prefetch=5,
            grid=(strips // per,),
            in_specs=[
                pl.BlockSpec((per, tpi, edge, edge), lambda s, *_: (s, 0, 0, 0)),
                pl.BlockSpec(omega_blocks.shape, lambda s, *_: (0, 0, 0)),
            ],
            out_specs=(pl.BlockSpec(memory_space=pl.ANY), pl.BlockSpec(memory_space=pl.ANY)),
            scratch_shapes=[
                pltpu.VMEM((2 * half, edge, cols), F32),
                pltpu.VMEM((half, edge, cols), BF16),
                pltpu.SemaphoreType.DMA((2,)),
            ],
        ),
        name="partial_sketch",
    )(group, slot, col, live, place, tiles, omega_blocks)


def combine_kernel(place_ref, mine_ref, pair_ref, up_ref, down_ref, idf_ref,
                   sketch_ref, weight_ref, gram_ref):
    step = pl.program_id(0)
    blocks = sketch_ref.shape[0]
    total = mine_ref[0] + pair_ref[0].astype(F32) + up_ref[...].astype(F32) + down_ref[...].astype(F32)
    gram = jnp.zeros(gram_ref.shape, F32)
    for b in range(blocks):
        row = idf_ref[b]
        scale = jnp.transpose(jnp.broadcast_to(row, (total.shape[2], total.shape[1])))
        sk = total[b] * scale
        sketch_ref[b] = sk
        weight_ref[b] = jnp.transpose(sk * scale).astype(BF16)
        gram += lax.dot_general(sk, sk, (((0,), (0,)), ((), ())), precision=HIGHEST,
                                preferred_element_type=F32)

    @pl.when(step == 0)
    def _():
        gram_ref[...] = gram

    @pl.when(step > 0)
    def _():
        gram_ref[...] += gram


def combine(place, mine, pair, up, down, idf):
    chips, owned, edge, cols = mine.shape
    per = max(s for s in (1, 2, 4) if owned % s == 0)
    part = pl.BlockSpec((1, per, edge, cols), lambda s, place: (place[0] // 2, s, 0, 0))
    plain = pl.BlockSpec((per, edge, cols), lambda s, place: (s, 0, 0))
    return pl.pallas_call(
        combine_kernel,
        out_shape=(
            jax.ShapeDtypeStruct((owned, edge, cols), F32),
            jax.ShapeDtypeStruct((owned, cols, edge), BF16),
            jax.ShapeDtypeStruct((cols, cols), F32),
        ),
        grid_spec=pltpu.PrefetchScalarGridSpec(
            num_scalar_prefetch=1,
            grid=(owned // per,),
            in_specs=[part, part, plain, plain,
                      pl.BlockSpec((per, 1, edge), lambda s, place: (s, 0, 0))],
            out_specs=(plain, pl.BlockSpec((per, cols, edge), lambda s, place: (s, 0, 0)),
                       pl.BlockSpec((cols, cols), lambda s, place: (0, 0))),
        ),
        name="combine",
    )(place, mine, pair, up, down, idf.reshape(owned, 1, edge))


def project_kernel(owned, step_strips, chips, group_ref, slot_ref, col_ref, live_ref, place_ref,
                   tiles_ref, *rest):
    n_src = 2 + 4 * (chips - 1)
    sources = rest[:n_src]
    doc_ref, weights_ref, sems = rest[n_src:]
    step = pl.program_id(0)
    tpi, edge = tiles_ref.shape[1], tiles_ref.shape[3]
    chip, core = place_ref[0] // 2, place_ref[0] % 2

    away = [(0, 0), (0, 1)]
    for t in range(1, chips):
        away += [(-t, 0), (-t, 1), (t, 0), (t, 1)]

    @pl.when(step == 0)
    def _():
        doc_ref[...] = jnp.zeros_like(doc_ref)
        for wait in (False, True):
            for n, (far, other) in enumerate(away):
                there = chip + far

                @pl.when((there >= 0) & (there < chips))
                def _():
                    owner = there * 2 + (core if other == 0 else 1 - core)
                    copy = pltpu.make_async_copy(
                        sources[n], weights_ref.at[pl.ds(owner * owned, owned)], sems.at[n])
                    copy.wait() if wait else copy.start()

    for i in range(step_strips):
        strip = step * step_strips + i

        @pl.when(strip < live_ref[0])
        def _():
            left = weights_ref[group_ref[strip] * owned + slot_ref[strip]]
            right = jnp.concatenate([tiles_ref[i, j] for j in range(tpi)], axis=1)
            out = jnp.dot(left, right, preferred_element_type=F32)
            for j in range(tpi):
                doc_ref[col_ref[strip, j]] += out[:, j * edge:(j + 1) * edge]


def project(group, slot, col, live, place, tiles, sources, n_group, owned, col_blocks):
    strips, tpi, edge, _ = tiles.shape
    cols = sources[0].shape[1]
    per = strips_per_step(strips)
    chips = n_group // 2
    return pl.pallas_call(
        functools.partial(project_kernel, owned, per, chips),
        out_shape=jax.ShapeDtypeStruct((col_blocks, cols, edge), F32),
        grid_spec=pltpu.PrefetchScalarGridSpec(
            num_scalar_prefetch=5,
            grid=(strips // per,),
            in_specs=[pl.BlockSpec((per, tpi, edge, edge), lambda s, *_: (s, 0, 0, 0))]
            + [pl.BlockSpec(memory_space=pl.ANY)] * len(sources),
            out_specs=pl.BlockSpec((col_blocks, cols, edge), lambda s, *_: (0, 0, 0)),
            scratch_shapes=[
                pltpu.VMEM((n_group * owned, cols, edge), BF16),
                pltpu.SemaphoreType.DMA((len(sources),)),
            ],
        ),
        name="project",
    )(group, slot, col, live, place, tiles, *sources)


def finish_kernel(place_ref, own_ref, inverse_ref, *rest):
    arrived, out_ref = rest[:-1], rest[-1]
    blocks, _, edge = own_ref.shape[1:]
    for b in range(blocks):
        total = own_ref[0, b]
        for r in arrived:
            total += r[b].astype(F32)
        out_ref[:, b * edge:(b + 1) * edge] = jnp.dot(
            inverse_ref[...], total, precision=HIGHEST, preferred_element_type=F32).astype(BF16)


def finish(place, own, inverse, arrived):
    n_dev, blocks, cols, edge = own.shape
    return pl.pallas_call(
        finish_kernel,
        out_shape=jax.ShapeDtypeStruct((cols, blocks * edge), BF16),
        grid_spec=pltpu.PrefetchScalarGridSpec(
            num_scalar_prefetch=1,
            grid=(1,),
            in_specs=[pl.BlockSpec((1, blocks, cols, edge), lambda s, place: (place[1], 0, 0, 0)),
                      pl.BlockSpec((cols, cols), lambda s, place: (0, 0))]
            + [pl.BlockSpec((blocks, cols, edge), lambda s, place: (0, 0, 0))] * len(arrived),
            out_specs=pl.BlockSpec((cols, blocks * edge), lambda s, place: (0, 0)),
        ),
        name="finish",
    )(place, own, inverse, *arrived)


def partners(n, s):
    if n & (n - 1) == 0:
        return [(i, i ^ s) for i in range(n)]
    return [(i, (i + s) % n) for i in range(n)]


def partner_of(n, me, s):
    return me ^ s if n & (n - 1) == 0 else (me + s) % n


def sum_over(x, axis, n):
    if n & (n - 1):
        return lax.psum(x, axis)
    s = 1
    while s < n:
        x = x + lax.ppermute(x, axis, partners(n, s))
        s *= 2
    return x


def on_device(tiles, tile_col, strip_group, strip_slot, live_count, omega, idf):
    n_group = lax.axis_size("group")
    n_dev = lax.axis_size("dev")
    chips = n_group // 2
    edge = tiles.shape[2]
    cols = omega.shape[1]
    owned = idf.shape[0] // edge
    me, band = lax.axis_index("group"), lax.axis_index("dev")
    chip = me // 2
    place = jnp.stack([me, band]).astype(jnp.int32)

    col_own = omega.shape[0] // edge
    own_omega = omega.reshape(col_own, edge, cols)
    group_omega = jnp.zeros((n_dev,) + own_omega.shape, BF16)
    group_omega = lax.dynamic_update_slice(group_omega, own_omega[None], (band, 0, 0, 0))
    for s in range(1, n_dev):
        sent = lax.ppermute(own_omega, "dev", partners(n_dev, s))
        source = partner_of(n_dev, band, s if n_dev & (n_dev - 1) == 0 else n_dev - s)
        group_omega = lax.dynamic_update_slice(group_omega, sent[None], (source, 0, 0, 0))
    omega_blocks = group_omega.reshape(n_dev * col_own, edge, cols)

    mine, theirs = partial_sketch(strip_group, strip_slot, tile_col, live_count, place,
                                  tiles, omega_blocks, n_group, owned)
    pair = lax.ppermute(theirs, "group", [(i, i ^ 1) for i in range(n_group)])
    mine = mine.reshape(chips, owned, edge, cols)
    pair = pair.reshape(chips, owned, edge, cols)

    up = jnp.zeros((owned, edge, cols), BF16)
    down = up
    for t in range(1, chips):
        up_unit = jnp.clip(chips - t + chip, 0, chips - 1)
        down_unit = jnp.clip(t - chips + chip, 0, chips - 1)

        def outgoing(unit, carried):
            total = (lax.dynamic_index_in_dim(mine, unit, 0, False)
                     + lax.dynamic_index_in_dim(pair, unit, 0, False).astype(F32))
            if t > 1:
                total = total + carried.astype(F32)
            return total.astype(BF16)

        to_up, to_down = outgoing(up_unit, up), outgoing(down_unit, down)
        up_links = [(c, c + 1) for c in range(min(t, chips - 1))]
        down_links = [(chips - 1 - a, chips - 1 - b) for a, b in up_links]
        both = lambda links: [(2 * a + k, 2 * b + k) for a, b in links for k in (0, 1)]
        up = lax.ppermute(to_up, "group", both(up_links))
        down = lax.ppermute(to_down, "group", both(down_links))

    sketch, weight, local_gram = combine(place, mine, pair, up, down, idf)

    swap = lambda x: lax.ppermute(x, "group", [(i, i ^ 1) for i in range(n_group)])
    sources = [weight, swap(weight)]
    below = above = weight
    for t in range(1, chips):
        below = lax.ppermute(below, "group", [(i, i + 2) for i in range(n_group - 2)])
        above = lax.ppermute(above, "group", [(i + 2, i) for i in range(n_group - 2)])
        sources += [below, swap(below), above, swap(above)]

    gram_matrix = sum_over(sum_over(local_gram, "dev", n_dev), "group", n_group)
    gram_matrix = gram_matrix / (idf.shape[0] * n_group * n_dev)
    lower_factor = jnp.linalg.cholesky(gram_matrix)
    inverse = jax.scipy.linalg.solve_triangular(lower_factor, jnp.eye(cols, dtype=F32), lower=True)
    q_basis = lax.dot_general(sketch.reshape(-1, cols), inverse, (((1,), (1,)), ((), ())),
                              precision=HIGHEST, preferred_element_type=F32)

    doc_part = project(strip_group, strip_slot, tile_col, live_count, place, tiles, sources,
                       n_group, owned, n_dev * col_own)
    doc_part = doc_part.reshape(n_dev, col_own, cols, edge)
    arrived = []
    for s in range(1, n_dev):
        unit = lax.dynamic_index_in_dim(doc_part, partner_of(n_dev, band, s), 0, False)
        arrived.append(lax.ppermute(unit.astype(BF16), "dev", partners(n_dev, s)))
    doc_factor = finish(place, doc_part, inverse, arrived)
    return (q_basis, doc_factor)


def solution(mesh):
    placed = (
        P(("group", "dev"), None, None, None),
        P(("group", "dev"), None),
        P(("group", "dev")),
        P(("group", "dev")),
        P(("group", "dev")),
        P(("group", "dev"), None),
        P(("group", "dev")),
    )
    return jax.shard_map(
        on_device,
        mesh=mesh,
        in_specs=placed,
        out_specs=(P(("group", "dev"), None), P(None, ("group", "dev"))),
        check_vma=False,
    )
```

time: 529 us -> 215 us (0.41)
  waiting for transfers between devices: 330 us -> 53.1 us
  starting transfers between devices: 12 us -> 67.2 us
  Pallas kernels: 0 us -> 50.3 us
  other arithmetic: 76.6 us -> 32.4 us
  matrix products: 40.1 us -> 2.2 us
  local copies, waits for them, and re-layouts: 42.8 us -> 7.58 us
  between operations: 14.6 us -> 1.77 us
  blocking collectives: 11.5 us -> 0 us
    all_to_all x2 -> x0, waiting for transfers between devices: 138 us -> none  [the longest x1 138 us: on_device(): lax.all_to_all(outgoing.reshape(n_group, capacity, tile_edge, sketch_cols...]
    psum x1 -> x0, waiting for transfers between devices: 117 us -> none  [on_device(): gram_matrix = lax.psum(local_gram, ('group', 'dev')) / total_terms]
    ppermute x0 -> x31, starting transfers between devices: none -> 67.2 us  [the longest x3 25.5 us: on_device(): up = lax.ppermute(to_up, 'group', both(up_links))]
    ppermute x0 -> x31, waiting for transfers between devices: none -> 53.1 us  [the longest x3 27 us: on_device(): up = lax.ppermute(to_up, 'group', both(up_links))]
    pallas_call x0 -> x4, Pallas kernels: none -> 50.3 us  [the longest x1 21.6 us: project(): pl.pallas_call(functools.partial(project_kernel, owned, per, chips), out_...]
    scatter-add x1 -> x0, other arithmetic: 47.9 us -> none  [on_device(): jax.ops.segment_sum(contrib.reshape(-1, sketch_cols, tile_edge), tile_col...]
    all_gather x1 -> x0, waiting for transfers between devices: 47.7 us -> none  [on_device(): band_rows = lax.all_gather(weighted, 'group', axis=0, tiled=True)]
    dot_general x4 -> x1, matrix products: 38 us -> 1.96 us  [on_device(): lax.dot_general(sketch.reshape(-1, cols), inverse, (((1,), (1,)), ((), ()...]
  transfers between devices with their start and end apart: 5 -> 31, of which waited for: 4 -> 12; matrix products, arithmetic and copies ran while one was open for 9% -> 15% of each run, Pallas kernels for 0% -> 0%
where the time goes in v1:
time: 215 us
  starting transfers between devices  67.2 us (31%)
  waiting for transfers between devices  53.1 us (25%)
  Pallas kernels  50.3 us (23%)
  other arithmetic  32.4 us (15%)
  local copies, waits for them, and re-layouts  7.58 us (4%)
  matrix products  2.2 us (1%)
    ppermute x3, waiting for transfers between devices, on_device(): up = lax.ppermute(to_up, 'group', both(up_links))  27 us
    ppermute x3, starting transfers between devices, on_device(): up = lax.ppermute(to_up, 'group', both(up_links))  25.5 us
    pallas_call x1, Pallas kernels, project(): pl.pallas_call(functools.partial(project_kernel, owned, per, chips), out_...  21.6 us
    pallas_call x1, Pallas kernels, partial_sketch(): pl.pallas_call(functools.partial(sketch_kernel, owned, per), out_shape=(j...  20.4 us
    ppermute x3, starting transfers between devices, on_device(): lax.ppermute(below, 'group', [(i, i + 2) for i in range(n_group - 2)])  15 us
    another operation x3, other arithmetic, on_device(): lower_factor = jnp.linalg.cholesky(gram_matrix)  12.4 us
    another operation x2, other arithmetic, on_device(): jax.scipy.linalg.solve_triangular(lower_factor, jnp.eye(cols, dtype=F32),...  10.5 us
    convert_element_type x4, other arithmetic, outgoing(): return total.astype(BF16)  8.89 us
  transfers between devices with their start and end apart: 31, of which 12 were waited for; matrix products, arithmetic and copies ran while one was open for 15% of the time, Pallas kernels for 0%

profile of v1, /device:TPU:0, one launch (start us, length us, event | category | flops | bytes accessed | tf_op | source)
XLA Modules:
  0.0 214.6 jit_solution(3754360472147449993)
XLA Ops:
  0.6 4.0 %collective-permute-start.2 = (bf16[4,128,128]{2,1,0:T(8,128)(2,1)}, bf16[4,128,128]{2,1,0:T(8,128)(2,1)S(1)}, u32[]{:S(2)}, u32[]{:S(2)}) collective-permute-start(bf16[4,128,128]{2,1,0:T(8,128)(2,1)} %bitcast.67), channel_id=1, source_target_pairs={{0,3},{1,2},{2,1},{3,0},{4,7},{5,6},{6,5},{7,4},{8,11},{9,10},{10,... | collective-permute-start | bytes 393224 | tf_op jit(solution)/shard_map/ppermute | solution.py:255
  6.5 1.4 copy.9.col_ref
  8.0 0.9 constant_dynamic-update-slice_fusion
  8.9 2.4 %collective-permute-done = bf16[4,128,128]{2,1,0:T(8,128)(2,1)S(1)} collective-permute-done((bf16[4,128,128]{2,1,0:T(8,128)(2,1)}, bf16[4,128,128]{2,1,0:T(8,128)(2,1)S(1)}, u32[]{:S(2)}, u32[]{:S(2)}) %collective-permute-start) | collective-permute-done | bytes 131104 | tf_op jit(solution)/shard_map/ppermute | solution.py:255
  11.5 0.8 copy-done.1
  12.3 20.4 %partial_sketch.1 = (f32[64,128,128]{2,1,0:T(8,128)}, bf16[64,128,128]{2,1,0:T(8,128)(2,1)}) custom-call(s32[72]{0:T(128)} %group_ref.3, s32[72]{0:T(128)} %slot_ref.3, s32[72,5]{1,0:T(8,128)} %copy.9.col_ref, s32[1]{0:T(128)S(6)} %copy.18.live_ref, s32[2]{0:T(128)} %pad_add_fusion.place_ref, bf16[72,5,128,128]{3,2,1,0:T(8,128)(2,1)} %tiles_ref.3, ...), custom_call_target="tpu_custom_call" | custom-call | tf_op jit(solution)/shard_map/partial_sketch/pallas_call | solution.py:57
  32.8 4.3 %collective-permute-done.3 = bf16[64,128,128]{2,1,0:T(8,128)(2,1)S(1)} collective-permute-done((bf16[64,128,128]{2,1,0:T(8,128)(2,1)}, bf16[64,128,128]{2,1,0:T(8,128)(2,1)S(1)}, u32[]{:S(2)}, u32[]{:S(2)}) %collective-permute-start.3) | collective-permute-done | bytes 2097184 | tf_op jit(solution)/shard_map/ppermute | solution.py:262
  37.1 2.6 %fusion.5 = (bf16[16,128,128]{2,1,0:T(8,128)(2,1)S(1)}, bf16[16,128,128]{2,1,0:T(8,128)(2,1)S(1)}) fusion(f32[4,16,128,128]{3,2,1,0:T(8,128)} %bitcast.53, s32[]{:T(128)S(6)} %min.24, bf16[4,16,128,128]{3,2,1,0:T(8,128)(2,1)S(1)} %bitcast.58, s32[]{:T(128)S(6)} %min.21), kind=kLoop, calls=%fused_computation.11 | loop fusion | flops 1572864 | bytes 4194312 | tf_op jit(solution)/shard_map/convert_element_type | solution.py:277
  39.8 1.5 collective-permute-start.7
  41.2 2.4 %collective-permute-start.4 = (bf16[16,128,128]{2,1,0:T(8,128)(2,1)S(1)}, bf16[16,128,128]{2,1,0:T(8,128)(2,1)}, u32[]{:S(2)}, u32[]{:S(2)}) collective-permute-start(bf16[16,128,128]{2,1,0:T(8,128)(2,1)S(1)} %get-tuple-element.15), channel_id=1, source_target_pairs={{0,8},{4,12},{1,9},{5,13},{2,10},{6,14},{3,11},{7,15}} | collective-permute-start | bytes 1572872 | tf_op jit(solution)/shard_map/ppermute | solution.py:283
  43.7 1.6 fusion
  45.3 1.5 collective-permute-start.8
  46.7 7.9 %collective-permute-done.4 = bf16[16,128,128]{2,1,0:T(8,128)(2,1)} collective-permute-done((bf16[16,128,128]{2,1,0:T(8,128)(2,1)S(1)}, bf16[16,128,128]{2,1,0:T(8,128)(2,1)}, u32[]{:S(2)}, u32[]{:S(2)}) %collective-permute-start.4) | collective-permute-done | bytes 524320 | tf_op jit(solution)/shard_map/ppermute | solution.py:283
  54.6 3.3 %fusion.1 = (bf16[16,128,128]{2,1,0:T(8,128)(2,1)}, bf16[16,128,128]{2,1,0:T(8,128)(2,1)}) fusion(bf16[16,128,128]{2,1,0:T(8,128)(2,1)} %collective-permute-done.8, f32[4,16,128,128]{3,2,1,0:T(8,128)} %bitcast.55, s32[]{:T(128)S(6)} %min.22, bf16[4,16,128,128]{3,2,1,0:T(8,128)(2,1)S(1)} %bitcast.60, bf16[16,128,128]{2,1,0:T(8,128)(2,1)} %collective-permute-done.4, ...), kind=kLoop, calls=%fused_computation.3 | loop fusion | flops 2621440 | bytes 5242888 | tf_op jit(solution)/shard_map/convert_element_type | solution.py:277
  57.9 18.8 %collective-permute-start.5 = (bf16[16,128,128]{2,1,0:T(8,128)(2,1)}, bf16[16,128,128]{2,1,0:T(8,128)(2,1)S(1)}, u32[]{:S(2)}, u32[]{:S(2)}) collective-permute-start(bf16[16,128,128]{2,1,0:T(8,128)(2,1)} %get-tuple-element.13), channel_id=1, source_target_pairs={{0,8},{4,12},{8,16},{12,20},{1,9},{5,13},{9,17},{13,21},{2,10},{6,... | collective-permute-start | bytes 1572872 | tf_op jit(solution)/shard_map/ppermute | solution.py:283
  76.7 1.3 collective-permute-start.9
  78.0 9.5 %collective-permute-done.5 = bf16[16,128,128]{2,1,0:T(8,128)(2,1)S(1)} collective-permute-done((bf16[16,128,128]{2,1,0:T(8,128)(2,1)}, bf16[16,128,128]{2,1,0:T(8,128)(2,1)S(1)}, u32[]{:S(2)}, u32[]{:S(2)}) %collective-permute-start.5) | collective-permute-done | bytes 524320 | tf_op jit(solution)/shard_map/ppermute | solution.py:283
  87.5 1.4 fusion.3
  88.9 4.3 %collective-permute-start.6 = (bf16[16,128,128]{2,1,0:T(8,128)(2,1)S(1)}, bf16[16,128,128]{2,1,0:T(8,128)(2,1)S(1)}, u32[]{:S(2)}, u32[]{:S(2)}) collective-permute-start(bf16[16,128,128]{2,1,0:T(8,128)(2,1)S(1)} %fusion.3), channel_id=1, source_target_pairs={{0,8},{4,12},{8,16},{12,20},{16,24},{20,28},{1,9},{5,13},{9,17},{1... | collective-permute-start | bytes 1572872 | tf_op jit(solution)/shard_map/ppermute | solution.py:283
  93.3 9.6 %collective-permute-done.6.up_ref = bf16[16,128,128]{2,1,0:T(8,128)(2,1)S(1)} collective-permute-done((bf16[16,128,128]{2,1,0:T(8,128)(2,1)S(1)}, bf16[16,128,128]{2,1,0:T(8,128)(2,1)S(1)}, u32[]{:S(2)}, u32[]{:S(2)}) %collective-permute-start.6) | collective-permute-done | bytes 524320 | tf_op jit(solution)/shard_map/ppermute | solution.py:283
  102.9 0.8 copy-done.11
  103.7 5.5 %combine.1 = (f32[16,128,128]{2,1,0:T(8,128)}, bf16[16,128,128]{2,1,0:T(8,128)(2,1)}, f32[128,128]{1,0:T(8,128)}) custom-call(s32[2]{0:T(128)} %pad_add_fusion.place_ref, f32[4,16,128,128]{3,2,1,0:T(8,128)} %bitcast.57, bf16[4,16,128,128]{3,2,1,0:T(8,128)(2,1)} %bitcast.62, bf16[16,128,128]{2,1,0:T(8,128)(2,1)} %copy-done.11, ...), custom_call_target="tpu_custom_call" | custom-call | tf_op jit(solution)/shard_map/combine/pallas_call | solution.py:110
  109.2 1.3 collective-permute-start.18
  110.5 5.0 %collective-permute-start.16 = (bf16[16,128,128]{2,1,0:T(8,128)(2,1)}, bf16[16,128,128]{2,1,0:T(8,128)(2,1)S(1)}, u32[]{:S(2)}, u32[]{:S(2)}) collective-permute-start(bf16[16,128,128]{2,1,0:T(8,128)(2,1)} %get-tuple-element.11.rest_0_), channel_id=1, source_target_pairs={{0,8},{4,12},{8,16},{12,20},{16,24},{20,28},{1,9},{5,13},{9,17},{1... | collective-permute-start | bytes 1572872 | tf_op jit(solution)/shard_map/ppermute | solution.py:292
  115.5 7.8 %collective-permute-done.18.rest_4_ = bf16[16,128,128]{2,1,0:T(8,128)(2,1)S(1)} collective-permute-done((bf16[16,128,128]{2,1,0:T(8,128)(2,1)}, bf16[16,128,128]{2,1,0:T(8,128)(2,1)S(1)}, u32[]{:S(2)}, u32[]{:S(2)}) %collective-permute-start.18) | collective-permute-done | bytes 524320 | tf_op jit(solution)/shard_map/ppermute | solution.py:293
  123.4 1.3 collective-permute-start.22
  124.7 4.6 %collective-permute-start.20 = (bf16[16,128,128]{2,1,0:T(8,128)(2,1)S(1)}, bf16[16,128,128]{2,1,0:T(8,128)(2,1)S(1)}, u32[]{:S(2)}, u32[]{:S(2)}) collective-permute-start(bf16[16,128,128]{2,1,0:T(8,128)(2,1)S(1)} %collective-permute-done.16.rest_2_), channel_id=1, source_target_pairs={{0,8},{4,12},{8,16},{12,20},{16,24},{20,28},{1,9},{5,13},{9,17},{1... | collective-permute-start | bytes 1572872 | tf_op jit(solution)/shard_map/ppermute | solution.py:292
  129.3 0.9 copy.11
  130.2 2.2 %collective-permute-start.10 = (f32[128,128]{0,1:T(8,128)S(1)}, f32[128,128]{0,1:T(8,128)S(1)}, u32[]{:S(2)}, u32[]{:S(2)}) collective-permute-start(f32[128,128]{0,1:T(8,128)S(1)} %copy.11), channel_id=1, source_target_pairs={{0,1},{1,0},{2,3},{3,2},{4,5},{5,4},{6,7},{7,6},{8,9},{9,8},{10,11... | collective-permute-start | bytes 196616 | tf_op jit(solution)/shard_map/ppermute | solution.py:234
  132.4 2.2 %collective-permute-done.10 = f32[128,128]{0,1:T(8,128)S(1)} collective-permute-done((f32[128,128]{0,1:T(8,128)S(1)}, f32[128,128]{0,1:T(8,128)S(1)}, u32[]{:S(2)}, u32[]{:S(2)}) %collective-permute-start.10) | collective-permute-done | bytes 65568 | tf_op jit(solution)/shard_map/ppermute | solution.py:234
  134.7 2.5 %collective-permute-start.11 = (f32[128,128]{0,1:T(8,128)S(1)}, f32[128,128]{0,1:T(8,128)S(1)}, u32[]{:S(2)}, u32[]{:S(2)}) collective-permute-start(f32[128,128]{0,1:T(8,128)S(1)} %add.132), channel_id=1, source_target_pairs={{0,2},{1,3},{2,0},{3,1},{4,6},{5,7},{6,4},{7,5},{8,10},{9,11},{10,... | collective-permute-start | bytes 196616 | tf_op jit(solution)/shard_map/ppermute | solution.py:234
  137.2 2.2 %collective-permute-done.11 = f32[128,128]{0,1:T(8,128)S(1)} collective-permute-done((f32[128,128]{0,1:T(8,128)S(1)}, f32[128,128]{0,1:T(8,128)S(1)}, u32[]{:S(2)}, u32[]{:S(2)}) %collective-permute-start.11) | collective-permute-done | bytes 65568 | tf_op jit(solution)/shard_map/ppermute | solution.py:234
  139.6 1.2 collective-permute-done.12
  140.8 1.8 collective-permute-start.13
  142.6 2.6 %collective-permute-done.13 = f32[128,128]{0,1:T(8,128)S(1)} collective-permute-done((f32[128,128]{0,1:T(8,128)S(1)}, f32[128,128]{0,1:T(8,128)S(1)}, u32[]{:S(2)}, u32[]{:S(2)}) %collective-permute-start.13) | collective-permute-done | bytes 65568 | tf_op jit(solution)/shard_map/ppermute | solution.py:234
  145.2 2.1 collective-permute-start.14
  147.8 1.3 collective-permute-start.26
  149.1 5.4 %collective-permute-start.24 = (bf16[16,128,128]{2,1,0:T(8,128)(2,1)S(1)}, bf16[16,128,128]{2,1,0:T(8,128)(2,1)}, u32[]{:S(2)}, u32[]{:S(2)}) collective-permute-start(bf16[16,128,128]{2,1,0:T(8,128)(2,1)S(1)} %collective-permute-done.20.rest_6_), channel_id=1, source_target_pairs={{0,8},{4,12},{8,16},{12,20},{16,24},{20,28},{1,9},{5,13},{9,17},{1... | collective-permute-start | bytes 1572872 | tf_op jit(solution)/shard_map/ppermute | solution.py:292
  154.6 11.7 %cholesky.17 = f32[128,128]{1,0:T(8,128)S(1)} custom-call(f32[128,128]{1,0:T(8,128)S(1)} %fusion.12), custom_call_target="Cholesky" | custom-call | tf_op jit(solution)/shard_map/jit(cholesky)/cholesky | solution.py:298
  168.9 9.8 %custom-call.7 = f32[1,128,128]{1,2,0:T(8,128)S(1)} custom-call(f32[1,128,128]{2,1,0:T(8,128)S(1)} %fusion.9), custom_call_target="InvertDiagBlocksLowerTriangular" | custom-call | tf_op jit(solution)/shard_map/jit(_solve_triangular)/triangular_solve | solution.py:299
  179.1 21.6 %project.1 = f32[16,128,128]{2,1,0:T(8,128)} custom-call(s32[72]{0:T(128)} %group_ref.3, s32[72]{0:T(128)} %slot_ref.3, s32[72,5]{1,0:T(8,128)} %copy.9.col_ref, s32[1]{0:T(128)S(6)} %copy.18.live_ref, s32[2]{0:T(128)} %pad_add_fusion.place_ref, bf16[72,5,128,128]{3,2,1,0:T(8,128)(2,1)} %tiles_ref.3, bf16[16,128,128]{2,1,0:T(8,128)(2,1)} %get-tuple-element.11.rest_0_, ...), custom_call_target="tpu_custom_call" | custom-call | tf_op jit(solution)/shard_map/project/pallas_call | solution.py:173
  200.6 1.2 fusion.8
  201.9 1.8 collective-permute-start.29
  203.7 1.7 collective-permute-start.28
  205.4 2.0 fusion.13
  207.3 1.9 collective-permute-done.30.rest_2_
  209.2 1.3 collective-permute-done.29.rest_1_
  211.8 2.8 %finish.1 = bf16[128,512]{1,0:T(8,128)(2,1)} custom-call(s32[2]{0:T(128)} %pad_add_fusion.place_ref, f32[4,4,128,128]{3,2,1,0:T(8,128)} %bitcast.64, f32[128,128]{1,0:T(8,128)} %copy-done.3, bf16[4,128,128]{2,1,0:T(8,128)(2,1)} %copy-done.14, bf16[4,128,128]{2,1,0:T(8,128)(2,1)} %copy-done.13, bf16[4,128,128]{2,1,0:T(8,128)(2,1)} %copy-done.12), custom_call_target="tpu_custom_call" | custom-call | tf_op jit(solution)/shard_map/finish/pallas_call | solution.py:204
  (75 shorter events, 6.4 us)
Async XLA Ops:
  0.6 10.8 %collective-permute-start.2 = (bf16[4,128,128]{2,1,0:T(8,128)(2,1)}, bf16[4,128,128]{2,1,0:T(8,128)(2,1)S(1)}, u32[]{:S(2)}, u32[]{:S(2)}) collective-permute-start(bf16[4,128,128]{2,1,0:T(8,128)(2,1)} %bitcast.67), channel_id=1, source_target_pairs={{0,3},{1,2},{2,1},{3,0},{4,7},{5,6},{6,5},{7,4},{8,11},{9,10},{10,... | collective-permute-start | bytes 393224 | tf_op jit(solution)/shard_map/ppermute | solution.py:255
  4.6 6.8 %collective-permute-start.1 = (bf16[4,128,128]{2,1,0:T(8,128)(2,1)}, bf16[4,128,128]{2,1,0:T(8,128)(2,1)S(1)}, u32[]{:S(2)}, u32[]{:S(2)}) collective-permute-start(bf16[4,128,128]{2,1,0:T(8,128)(2,1)} %bitcast.68), channel_id=1, source_target_pairs={{0,2},{1,3},{2,0},{3,1},{4,6},{5,7},{6,4},{7,5},{8,10},{9,11},{10,... | collective-permute-start | bytes 393224 | tf_op jit(solution)/shard_map/ppermute | solution.py:255
  5.1 6.3 %collective-permute-start = (bf16[4,128,128]{2,1,0:T(8,128)(2,1)}, bf16[4,128,128]{2,1,0:T(8,128)(2,1)S(1)}, u32[]{:S(2)}, u32[]{:S(2)}) collective-permute-start(bf16[4,128,128]{2,1,0:T(8,128)(2,1)} %bitcast.69), channel_id=1, source_target_pairs={{0,1},{1,0},{2,3},{3,2},{4,5},{5,4},{6,7},{7,6},{8,9},{9,8},{10,11... | collective-permute-start | bytes 393224 | tf_op jit(solution)/shard_map/ppermute | solution.py:255
  11.5 0.8 copy-start.1
  32.7 4.4 %collective-permute-start.3 = (bf16[64,128,128]{2,1,0:T(8,128)(2,1)}, bf16[64,128,128]{2,1,0:T(8,128)(2,1)S(1)}, u32[]{:S(2)}, u32[]{:S(2)}) collective-permute-start(bf16[64,128,128]{2,1,0:T(8,128)(2,1)} %get-tuple-element.8), channel_id=1, source_target_pairs={{0,4},{4,0},{8,12},{12,8},{16,20},{20,16},{24,28},{28,24},{1,5},{5... | collective-permute-start | bytes 6291464 | tf_op jit(solution)/shard_map/ppermute | solution.py:262
  37.1 50.3 %copy-start = (bf16[64,128,128]{2,1,0:T(8,128)(2,1)}, bf16[64,128,128]{2,1,0:T(8,128)(2,1)S(1)}, u32[]{:S(2)}) copy-start(bf16[64,128,128]{2,1,0:T(8,128)(2,1)S(1)} %collective-permute-done.3) | copy-start | bytes 6291460
  39.8 3.9 %collective-permute-start.7 = (bf16[16,128,128]{2,1,0:T(8,128)(2,1)S(1)}, bf16[16,128,128]{2,1,0:T(8,128)(2,1)}, u32[]{:S(2)}, u32[]{:S(2)}) collective-permute-start(bf16[16,128,128]{2,1,0:T(8,128)(2,1)S(1)} %get-tuple-element.14), channel_id=1, source_target_pairs={{24,16},{28,20},{25,17},{29,21},{26,18},{30,22},{27,19},{31,23}} | collective-permute-start | bytes 1572872 | tf_op jit(solution)/shard_map/ppermute | solution.py:284
  41.2 13.4 %collective-permute-start.4 = (bf16[16,128,128]{2,1,0:T(8,128)(2,1)S(1)}, bf16[16,128,128]{2,1,0:T(8,128)(2,1)}, u32[]{:S(2)}, u32[]{:S(2)}) collective-permute-start(bf16[16,128,128]{2,1,0:T(8,128)(2,1)S(1)} %get-tuple-element.15), channel_id=1, source_target_pairs={{0,8},{4,12},{1,9},{5,13},{2,10},{6,14},{3,11},{7,15}} | collective-permute-start | bytes 1572872 | tf_op jit(solution)/shard_map/ppermute | solution.py:283
  45.3 9.3 %collective-permute-start.8 = (bf16[16,128,128]{2,1,0:T(8,128)(2,1)S(1)}, bf16[16,128,128]{2,1,0:T(8,128)(2,1)}, u32[]{:S(2)}, u32[]{:S(2)}) collective-permute-start(bf16[16,128,128]{2,1,0:T(8,128)(2,1)S(1)} %fusion), channel_id=1, source_target_pairs={{24,16},{28,20},{16,8},{20,12},{25,17},{29,21},{17,9},{21,13},{26,... | collective-permute-start | bytes 1572872 | tf_op jit(solution)/shard_map/ppermute | solution.py:284
  57.9 29.6 %collective-permute-start.5 = (bf16[16,128,128]{2,1,0:T(8,128)(2,1)}, bf16[16,128,128]{2,1,0:T(8,128)(2,1)S(1)}, u32[]{:S(2)}, u32[]{:S(2)}) collective-permute-start(bf16[16,128,128]{2,1,0:T(8,128)(2,1)} %get-tuple-element.13), channel_id=1, source_target_pairs={{0,8},{4,12},{8,16},{12,20},{1,9},{5,13},{9,17},{13,21},{2,10},{6,... | collective-permute-start | bytes 1572872 | tf_op jit(solution)/shard_map/ppermute | solution.py:283
  76.7 16.6 %collective-permute-start.9 = (bf16[16,128,128]{2,1,0:T(8,128)(2,1)}, bf16[16,128,128]{2,1,0:T(8,128)(2,1)S(1)}, u32[]{:S(2)}, u32[]{:S(2)}) collective-permute-start(bf16[16,128,128]{2,1,0:T(8,128)(2,1)} %get-tuple-element.12), channel_id=1, source_target_pairs={{24,16},{28,20},{16,8},{20,12},{8,0},{12,4},{25,17},{29,21},{17,9}... | collective-permute-start | bytes 1572872 | tf_op jit(solution)/shard_map/ppermute | solution.py:284
  88.9 14.0 %collective-permute-start.6 = (bf16[16,128,128]{2,1,0:T(8,128)(2,1)S(1)}, bf16[16,128,128]{2,1,0:T(8,128)(2,1)S(1)}, u32[]{:S(2)}, u32[]{:S(2)}) collective-permute-start(bf16[16,128,128]{2,1,0:T(8,128)(2,1)S(1)} %fusion.3), channel_id=1, source_target_pairs={{0,8},{4,12},{8,16},{12,20},{16,24},{20,28},{1,9},{5,13},{9,17},{1... | collective-permute-start | bytes 1572872 | tf_op jit(solution)/shard_map/ppermute | solution.py:283
  93.2 9.7 %copy-start.10 = (bf16[16,128,128]{2,1,0:T(8,128)(2,1)}, bf16[16,128,128]{2,1,0:T(8,128)(2,1)S(1)}, u32[]{:S(2)}) copy-start(bf16[16,128,128]{2,1,0:T(8,128)(2,1)S(1)} %collective-permute-done.9.down_ref) | copy-start | bytes 1572868
  102.9 0.8 copy-start.11
  109.2 14.2 %collective-permute-start.18 = (bf16[16,128,128]{2,1,0:T(8,128)(2,1)}, bf16[16,128,128]{2,1,0:T(8,128)(2,1)S(1)}, u32[]{:S(2)}, u32[]{:S(2)}) collective-permute-start(bf16[16,128,128]{2,1,0:T(8,128)(2,1)} %get-tuple-element.11.rest_0_), channel_id=1, source_target_pairs={{8,0},{12,4},{16,8},{20,12},{24,16},{28,20},{9,1},{13,5},{17,9},{2... | collective-permute-start | bytes 1572872 | tf_op jit(solution)/shard_map/ppermute | solution.py:293
  110.5 14.2 %collective-permute-start.16 = (bf16[16,128,128]{2,1,0:T(8,128)(2,1)}, bf16[16,128,128]{2,1,0:T(8,128)(2,1)S(1)}, u32[]{:S(2)}, u32[]{:S(2)}) collective-permute-start(bf16[16,128,128]{2,1,0:T(8,128)(2,1)} %get-tuple-element.11.rest_0_), channel_id=1, source_target_pairs={{0,8},{4,12},{8,16},{12,20},{16,24},{20,28},{1,9},{5,13},{9,17},{1... | collective-permute-start | bytes 1572872 | tf_op jit(solution)/shard_map/ppermute | solution.py:292
  123.4 55.6 %copy-start.4 = (bf16[16,128,128]{2,1,0:T(8,128)(2,1)}, bf16[16,128,128]{2,1,0:T(8,128)(2,1)S(1)}, u32[]{:S(2)}) copy-start(bf16[16,128,128]{2,1,0:T(8,128)(2,1)S(1)} %collective-permute-done.18.rest_4_) | copy-start | bytes 1572868
  123.4 24.4 %collective-permute-start.22 = (bf16[16,128,128]{2,1,0:T(8,128)(2,1)S(1)}, bf16[16,128,128]{2,1,0:T(8,128)(2,1)S(1)}, u32[]{:S(2)}, u32[]{:S(2)}) collective-permute-start(bf16[16,128,128]{2,1,0:T(8,128)(2,1)S(1)} %collective-permute-done.18.rest_4_), channel_id=1, source_target_pairs={{8,0},{12,4},{16,8},{20,12},{24,16},{28,20},{9,1},{13,5},{17,9},{2... | collective-permute-start | bytes 1572872 | tf_op jit(solution)/shard_map/ppermute | solution.py:293
  124.7 54.4 %copy-start.5 = (bf16[16,128,128]{2,1,0:T(8,128)(2,1)}, bf16[16,128,128]{2,1,0:T(8,128)(2,1)S(1)}, u32[]{:S(2)}) copy-start(bf16[16,128,128]{2,1,0:T(8,128)(2,1)S(1)} %collective-permute-done.16.rest_2_) | copy-start | bytes 1572868
  124.7 24.4 %collective-permute-start.20 = (bf16[16,128,128]{2,1,0:T(8,128)(2,1)S(1)}, bf16[16,128,128]{2,1,0:T(8,128)(2,1)S(1)}, u32[]{:S(2)}, u32[]{:S(2)}) collective-permute-start(bf16[16,128,128]{2,1,0:T(8,128)(2,1)S(1)} %collective-permute-done.16.rest_2_), channel_id=1, source_target_pairs={{0,8},{4,12},{8,16},{12,20},{16,24},{20,28},{1,9},{5,13},{9,17},{1... | collective-permute-start | bytes 1572872 | tf_op jit(solution)/shard_map/ppermute | solution.py:292
  130.2 4.5 %collective-permute-start.10 = (f32[128,128]{0,1:T(8,128)S(1)}, f32[128,128]{0,1:T(8,128)S(1)}, u32[]{:S(2)}, u32[]{:S(2)}) collective-permute-start(f32[128,128]{0,1:T(8,128)S(1)} %copy.11), channel_id=1, source_target_pairs={{0,1},{1,0},{2,3},{3,2},{4,5},{5,4},{6,7},{7,6},{8,9},{9,8},{10,11... | collective-permute-start | bytes 196616 | tf_op jit(solution)/shard_map/ppermute | solution.py:234
  134.7 4.8 %collective-permute-start.11 = (f32[128,128]{0,1:T(8,128)S(1)}, f32[128,128]{0,1:T(8,128)S(1)}, u32[]{:S(2)}, u32[]{:S(2)}) collective-permute-start(f32[128,128]{0,1:T(8,128)S(1)} %add.132), channel_id=1, source_target_pairs={{0,2},{1,3},{2,0},{3,1},{4,6},{5,7},{6,4},{7,5},{8,10},{9,11},{10,... | collective-permute-start | bytes 196616 | tf_op jit(solution)/shard_map/ppermute | solution.py:234
  139.5 1.3 collective-permute-start.12
  140.8 4.3 %collective-permute-start.13 = (f32[128,128]{0,1:T(8,128)S(1)}, f32[128,128]{0,1:T(8,128)S(1)}, u32[]{:S(2)}, u32[]{:S(2)}) collective-permute-start(f32[128,128]{0,1:T(8,128)S(1)} %add.134), channel_id=1, source_target_pairs={{0,8},{4,12},{8,0},{12,4},{16,24},{20,28},{24,16},{28,20},{1,9},{5... | collective-permute-start | bytes 196616 | tf_op jit(solution)/shard_map/ppermute | solution.py:234
  145.2 9.3 %collective-permute-start.14 = (f32[128,128]{0,1:T(8,128)S(1)}, f32[128,128]{0,1:T(8,128)S(1)}, u32[]{:S(2)}, u32[]{:S(2)}) collective-permute-start(f32[128,128]{0,1:T(8,128)S(1)} %add.135), channel_id=1, source_target_pairs={{0,16},{4,20},{8,24},{12,28},{16,0},{20,4},{24,8},{28,12},{1,17},{... | collective-permute-start | bytes 196616 | tf_op jit(solution)/shard_map/ppermute | solution.py:234
  147.3 19.1 %collective-permute-start.15 = (bf16[16,128,128]{2,1,0:T(8,128)(2,1)}, bf16[16,128,128]{2,1,0:T(8,128)(2,1)S(1)}, u32[]{:S(2)}, u32[]{:S(2)}) collective-permute-start(bf16[16,128,128]{2,1,0:T(8,128)(2,1)} %get-tuple-element.11.rest_0_), channel_id=1, source_target_pairs={{0,4},{4,0},{8,12},{12,8},{16,20},{20,16},{24,28},{28,24},{1,5},{5... | collective-permute-start | bytes 1572872 | tf_op jit(solution)/shard_map/ppermute | solution.py:288
  147.3 19.6 %collective-permute-start.19 = (bf16[16,128,128]{2,1,0:T(8,128)(2,1)S(1)}, bf16[16,128,128]{2,1,0:T(8,128)(2,1)S(1)}, u32[]{:S(2)}, u32[]{:S(2)}) collective-permute-start(bf16[16,128,128]{2,1,0:T(8,128)(2,1)S(1)} %collective-permute-done.18.rest_4_), channel_id=1, source_target_pairs={{0,4},{4,0},{8,12},{12,8},{16,20},{20,16},{24,28},{28,24},{1,5},{5... | collective-permute-start | bytes 1572872 | tf_op jit(solution)/shard_map/ppermute | solution.py:288
  147.8 31.2 %copy-start.6 = (bf16[16,128,128]{2,1,0:T(8,128)(2,1)}, bf16[16,128,128]{2,1,0:T(8,128)(2,1)S(1)}, u32[]{:S(2)}) copy-start(bf16[16,128,128]{2,1,0:T(8,128)(2,1)S(1)} %collective-permute-done.22.rest_8_) | copy-start | bytes 1572868
  147.8 19.2 %collective-permute-start.26 = (bf16[16,128,128]{2,1,0:T(8,128)(2,1)S(1)}, bf16[16,128,128]{2,1,0:T(8,128)(2,1)}, u32[]{:S(2)}, u32[]{:S(2)}) collective-permute-start(bf16[16,128,128]{2,1,0:T(8,128)(2,1)S(1)} %collective-permute-done.22.rest_8_), channel_id=1, source_target_pairs={{8,0},{12,4},{16,8},{20,12},{24,16},{28,20},{9,1},{13,5},{17,9},{2... | collective-permute-start | bytes 1572872 | tf_op jit(solution)/shard_map/ppermute | solution.py:293
  149.1 29.9 %copy-start.7 = (bf16[16,128,128]{2,1,0:T(8,128)(2,1)}, bf16[16,128,128]{2,1,0:T(8,128)(2,1)S(1)}, u32[]{:S(2)}) copy-start(bf16[16,128,128]{2,1,0:T(8,128)(2,1)S(1)} %collective-permute-done.20.rest_6_) | copy-start | bytes 1572868
  149.1 18.3 %collective-permute-start.24 = (bf16[16,128,128]{2,1,0:T(8,128)(2,1)S(1)}, bf16[16,128,128]{2,1,0:T(8,128)(2,1)}, u32[]{:S(2)}, u32[]{:S(2)}) collective-permute-start(bf16[16,128,128]{2,1,0:T(8,128)(2,1)S(1)} %collective-permute-done.20.rest_6_), channel_id=1, source_target_pairs={{0,8},{4,12},{8,16},{12,20},{16,24},{20,28},{1,9},{5,13},{9,17},{1... | collective-permute-start | bytes 1572872 | tf_op jit(solution)/shard_map/ppermute | solution.py:292
  166.4 12.6 %collective-permute-start.17 = (bf16[16,128,128]{2,1,0:T(8,128)(2,1)S(1)}, bf16[16,128,128]{2,1,0:T(8,128)(2,1)}, u32[]{:S(2)}, u32[]{:S(2)}) collective-permute-start(bf16[16,128,128]{2,1,0:T(8,128)(2,1)S(1)} %collective-permute-done.16.rest_2_), channel_id=1, source_target_pairs={{0,4},{4,0},{8,12},{12,8},{16,20},{20,16},{24,28},{28,24},{1,5},{5... | collective-permute-start | bytes 1572872 | tf_op jit(solution)/shard_map/ppermute | solution.py:288
  166.5 12.2 %copy-start.8 = (bf16[16,128,128]{2,1,0:T(8,128)(2,1)}, bf16[16,128,128]{2,1,0:T(8,128)(2,1)S(1)}, u32[]{:S(2)}) copy-start(bf16[16,128,128]{2,1,0:T(8,128)(2,1)S(1)} %collective-permute-done.15.rest_1_) | copy-start | bytes 1572868
  166.5 12.5 %collective-permute-start.23 = (bf16[16,128,128]{2,1,0:T(8,128)(2,1)S(1)}, bf16[16,128,128]{2,1,0:T(8,128)(2,1)}, u32[]{:S(2)}, u32[]{:S(2)}) collective-permute-start(bf16[16,128,128]{2,1,0:T(8,128)(2,1)S(1)} %collective-permute-done.22.rest_8_), channel_id=1, source_target_pairs={{0,4},{4,0},{8,12},{12,8},{16,20},{20,16},{24,28},{28,24},{1,5},{5... | collective-permute-start | bytes 1572872 | tf_op jit(solution)/shard_map/ppermute | solution.py:288
  166.9 1.9 copy-start.9
  166.9 12.0 %collective-permute-start.21 = (bf16[16,128,128]{2,1,0:T(8,128)(2,1)S(1)}, bf16[16,128,128]{2,1,0:T(8,128)(2,1)}, u32[]{:S(2)}, u32[]{:S(2)}) collective-permute-start(bf16[16,128,128]{2,1,0:T(8,128)(2,1)S(1)} %collective-permute-done.20.rest_6_), channel_id=1, source_target_pairs={{0,4},{4,0},{8,12},{12,8},{16,20},{20,16},{24,28},{28,24},{1,5},{5... | collective-permute-start | bytes 1572872 | tf_op jit(solution)/shard_map/ppermute | solution.py:288
  167.0 12.0 %collective-permute-start.27 = (bf16[16,128,128]{2,1,0:T(8,128)(2,1)}, bf16[16,128,128]{2,1,0:T(8,128)(2,1)}, u32[]{:S(2)}, u32[]{:S(2)}) collective-permute-start(bf16[16,128,128]{2,1,0:T(8,128)(2,1)} %collective-permute-done.26.rest_12_), channel_id=1, source_target_pairs={{0,4},{4,0},{8,12},{12,8},{16,20},{20,16},{24,28},{28,24},{1,5},{5... | collective-permute-start | bytes 1572872 | tf_op jit(solution)/shard_map/ppermute | solution.py:288
  167.5 11.5 %collective-permute-start.25 = (bf16[16,128,128]{2,1,0:T(8,128)(2,1)}, bf16[16,128,128]{2,1,0:T(8,128)(2,1)}, u32[]{:S(2)}, u32[]{:S(2)}) collective-permute-start(bf16[16,128,128]{2,1,0:T(8,128)(2,1)} %collective-permute-done.24.rest_10_), channel_id=1, source_target_pairs={{0,4},{4,0},{8,12},{12,8},{16,20},{20,16},{24,28},{28,24},{1,5},{5... | collective-permute-start | bytes 1572872 | tf_op jit(solution)/shard_map/ppermute | solution.py:288
  178.9 26.4 %copy-start.3 = (f32[128,128]{1,0:T(8,128)}, f32[128,128]{1,0:T(8,128)S(1)}, u32[]{:S(2)}) copy-start(f32[128,128]{1,0:T(8,128)S(1)} %fusion.10.inverse_ref) | copy-start | bytes 196612
  179.0 26.4 %copy-start.2 = (f32[16,128,128]{2,1,0:T(8,128)S(1)}, f32[16,128,128]{2,1,0:T(8,128)}, u32[]{:S(2)}) copy-start(f32[16,128,128]{2,1,0:T(8,128)} %get-tuple-element.9) | copy-start | bytes 3145732
  201.8 7.4 %collective-permute-start.30 = (bf16[4,128,128]{2,1,0:T(8,128)(2,1)S(1)}, bf16[4,128,128]{2,1,0:T(8,128)(2,1)S(1)}, u32[]{:S(2)}, u32[]{:S(2)}) collective-permute-start(bf16[4,128,128]{2,1,0:T(8,128)(2,1)S(1)} %get-tuple-element.16), channel_id=1, source_target_pairs={{0,3},{1,2},{2,1},{3,0},{4,7},{5,6},{6,5},{7,4},{8,11},{9,10},{10,... | collective-permute-start | bytes 393224 | tf_op jit(solution)/shard_map/ppermute | solution.py:309
  201.9 8.6 %collective-permute-start.29 = (bf16[4,128,128]{2,1,0:T(8,128)(2,1)S(1)}, bf16[4,128,128]{2,1,0:T(8,128)(2,1)S(1)}, u32[]{:S(2)}, u32[]{:S(2)}) collective-permute-start(bf16[4,128,128]{2,1,0:T(8,128)(2,1)S(1)} %get-tuple-element.17), channel_id=1, source_target_pairs={{0,2},{1,3},{2,0},{3,1},{4,6},{5,7},{6,4},{7,5},{8,10},{9,11},{10,... | collective-permute-start | bytes 393224 | tf_op jit(solution)/shard_map/ppermute | solution.py:309
  203.7 6.8 %collective-permute-start.28 = (bf16[4,128,128]{2,1,0:T(8,128)(2,1)S(1)}, bf16[4,128,128]{2,1,0:T(8,128)(2,1)S(1)}, u32[]{:S(2)}, u32[]{:S(2)}) collective-permute-start(bf16[4,128,128]{2,1,0:T(8,128)(2,1)S(1)} %get-tuple-element.18), channel_id=1, source_target_pairs={{0,1},{1,0},{2,3},{3,2},{4,5},{5,4},{6,7},{7,6},{8,9},{9,8},{10,11... | collective-permute-start | bytes 393224 | tf_op jit(solution)/shard_map/ppermute | solution.py:309
  209.2 1.3 copy-start.12
  210.5 0.7 copy-start.13
  211.1 0.6 copy-start.14

commit v2 on v0

v2 whole, which is shorter than its diff:
```python
import functools
import jax
import jax.numpy as jnp
from jax import lax
from jax.experimental import pallas as pl
from jax.experimental.pallas import tpu as pltpu
from jax.sharding import PartitionSpec as P

F32 = jnp.float32
BF16 = jnp.bfloat16
HIGHEST = lax.Precision.HIGHEST
BATCH = 4

VM = pl.BlockSpec(memory_space=pltpu.VMEM)
SM = pl.BlockSpec(memory_space=pltpu.SMEM)
HB = pl.BlockSpec(memory_space=pltpu.HBM)


def near(x):
    return pltpu.with_memory_space_constraint(x, pltpu.VMEM)


def far_off(x):
    return pltpu.with_memory_space_constraint(x, pltpu.HBM)


def cost(strips):
    return pl.CostEstimate(flops=strips << 28, bytes_accessed=strips << 19, transcendentals=0)


def params(mib):
    return pltpu.CompilerParams(vmem_limit_bytes=mib << 20)


def far_chip(chip, chips):
    return jnp.where(chip < chips // 2, chips - 1, 0)


def collect(keep, group_ref, live_ref, list_ref, tiles_ref, buf_ref, sems):
    def scan(strip, count):
        hit = keep(group_ref[strip])

        @pl.when(hit)
        def _():
            list_ref[count] = strip
            pltpu.make_async_copy(tiles_ref.at[strip], buf_ref.at[count], sems.at[count]).start()

        return count + hit.astype(jnp.int32)

    return lax.fori_loop(0, live_ref[0], scan, jnp.int32(0))


def in_batches(count, list_ref, tiles_ref, buf_ref, sems, work):
    def trip(b, carry):
        for i in range(BATCH):
            at = b * BATCH + i

            @pl.when(at < count)
            def _():
                pltpu.make_async_copy(tiles_ref.at[0], buf_ref.at[at], sems.at[at]).wait()

        for i in range(BATCH):
            at = jnp.minimum(b * BATCH + i, count - 1)
            work(list_ref[at], at, (b * BATCH + i < count).astype(F32))
        return carry

    lax.fori_loop(0, (count + BATCH - 1) // BATCH, trip, jnp.int32(0))


def sketch_kernel(far_only, chips, owned, n_src, group_ref, slot_ref, col_ref, live_ref, place_ref,
                  tiles_ref, *rest):
    sources = rest[:n_src]
    both_ref, theirs_ref, omega_ref, list_ref, buf_ref, sems = rest[-6:]
    half = theirs_ref.shape[0]
    tpi = buf_ref.shape[1]
    strips = buf_ref.shape[0]
    me, band = place_ref[0], place_ref[1]
    chip, core = me // 2, me % 2
    far = far_chip(chip, chips)
    held = sources[0].shape[0]
    own = pltpu.make_async_copy(sources[0], omega_ref.at[pl.ds(band * held, held)],
                                sems.at[strips])
    own.start()
    count = collect(lambda g: (g // 2 == far) == far_only, group_ref, live_ref, list_ref,
                    tiles_ref, buf_ref, sems)
    both_ref[...] = jnp.zeros_like(both_ref)
    for s in range(1, n_src):
        omega_ref[pl.ds(partner_of(n_src, band, s, back=True) * held, held)] = sources[s][...]
    own.wait()

    def work(strip, at, valid):
        owner = group_ref[strip]
        unit = jnp.int32(0) if far_only else owner // 2 - (far == 0).astype(jnp.int32)
        side = jnp.where(owner % 2 == core, 0, half)
        block = side + unit * owned + slot_ref[strip]
        left = jnp.concatenate([buf_ref[at, j] for j in range(tpi)], axis=1)
        right = jnp.concatenate([omega_ref[col_ref[strip, j]] for j in range(tpi)], axis=0)
        both_ref[block] += jnp.dot(left, right, preferred_element_type=F32) * valid

    in_batches(count, list_ref, tiles_ref, buf_ref, sems, work)
    theirs_ref[...] = both_ref[pl.ds(half, half)].astype(BF16)


def partial_sketch(far_only, scalars, tiles, sources, chips, owned, after=()):
    strips, tpi, edge, _ = tiles.shape
    col_own, _, cols = sources[0].shape
    blocks = owned * (1 if far_only else chips - 1)
    return pl.pallas_call(
        functools.partial(sketch_kernel, far_only, chips, owned, len(sources)),
        out_shape=(pltpu.VMEM((2 * blocks, edge, cols), F32),
                   pltpu.VMEM((blocks, edge, cols), BF16)),
        in_specs=[SM] * 5 + [HB] * 2 + [VM] * (len(sources) - 1 + len(after)),
        out_specs=(VM, VM),
        scratch_shapes=[
            pltpu.VMEM((col_own * len(sources), edge, cols), BF16),
            pltpu.SMEM((strips,), jnp.int32),
            pltpu.VMEM((strips, tpi, edge, edge), BF16),
            pltpu.SemaphoreType.DMA((strips + 1,)),
        ],
        compiler_params=params(16),
        cost_estimate=cost(strips // 4 if far_only else strips),
        name="sketch_far" if far_only else "sketch_rest",
    )(*scalars, far_off(tiles), far_off(sources[0]), *[near(s) for s in (*sources[1:], *after)])


def first_kernel(blocks, piece, mine_ref, pair_ref, out_ref):
    rows = pl.ds(piece * blocks, blocks)
    out_ref[...] = (mine_ref[rows] + pair_ref[rows].astype(F32)).astype(BF16)


def relay_kernel(t, chips, owned, blocks, piece, place_ref, far_mine, far_pair, rest_mine,
                 rest_pair, up_ref, down_ref, to_up, to_down):
    chip = place_ref[0] // 2
    far = far_chip(chip, chips)
    for unit, carried, out in ((chips - t + chip, up_ref, to_up),
                               (t - chips + chip, down_ref, to_down)):
        unit = jnp.clip(unit, 0, chips - 1)

        @pl.when(unit == far)
        def _():
            rows = pl.ds(piece * blocks, blocks)
            out[...] = (far_mine[rows] + far_pair[rows].astype(F32)
                        + carried[...].astype(F32)).astype(BF16)

        @pl.when(unit != far)
        def _():
            unit_at = unit - (far == 0).astype(jnp.int32)
            rows = pl.ds(unit_at * owned + piece * blocks, blocks)
            out[...] = (rest_mine[rows] + rest_pair[rows].astype(F32)
                        + carried[...].astype(F32)).astype(BF16)


def combine_kernel(chips, owned, piece, place_ref, rest_mine, rest_pair, up_ref, down_ref,
                   idf_ref, gram_in, sketch_ref, weight_ref, gram_ref):
    blocks = sketch_ref.shape[0]
    chip = place_ref[0] // 2
    unit_at = chip - (far_chip(chip, chips) == 0).astype(jnp.int32)
    gram = gram_in[...]
    for b in range(blocks):
        at = unit_at * owned + piece * blocks + b
        total = (rest_mine[at] + rest_pair[at].astype(F32)
                 + up_ref[b].astype(F32) + down_ref[b].astype(F32))
        row = idf_ref[pl.ds(piece * blocks + b, 1), :]
        scale = jnp.transpose(jnp.broadcast_to(row, total.shape[::-1]))
        sk = total * scale
        sketch_ref[b] = sk
        weight_ref[b] = jnp.transpose(sk * scale).astype(BF16)
        gram += lax.dot_general(sk, sk, (((0,), (0,)), ((), ())), precision=HIGHEST,
                                preferred_element_type=F32)
    gram_ref[...] = gram


def factor_kernel(total_terms, gram_ref, inverse_ref, x_ref):
    n = gram_ref.shape[0]
    x_ref[...] = gram_ref[...] * (1.0 / total_terms)
    rows = lax.broadcasted_iota(jnp.int32, (n, n), 0)
    columns = lax.broadcasted_iota(jnp.int32, (n, n), 1)

    one_row = lax.broadcasted_iota(jnp.int32, (1, n), 1)

    def eliminate(j, carry):
        x = x_ref[...]
        row = x_ref[pl.ds(j, 1), :]
        column = jnp.take_along_axis(x, jnp.full((n, n), j, jnp.int32), axis=1)
        pivot = jnp.take_along_axis(jnp.broadcast_to(row, (8, n)),
                                    jnp.full((8, n), j, jnp.int32), axis=1)[:1]
        scaled = jnp.where(one_row == j, 1.0, row) / pivot
        below = rows > j
        x = jnp.where((columns == j) & below, 0.0, x)
        x_ref[...] = x - jnp.where(below, column, 0.0) * scaled
        return carry

    lax.fori_loop(0, n, eliminate, jnp.int32(0))
    x = x_ref[...]
    pivots = jnp.sum(jnp.where(rows == columns, x, 0.0), axis=1, keepdims=True)
    lower = jnp.where(rows > columns, x, jnp.where(rows == columns, 1.0, 0.0))
    inverse_ref[...] = lower * lax.rsqrt(pivots)


def basis_kernel(inverse_ref, *rest):
    pieces, q_ref = rest[:-1], rest[-1]
    at = 0
    for piece in pieces:
        for b in range(piece.shape[0]):
            q_ref[at] = lax.dot_general(piece[b], inverse_ref[...], (((1,), (1,)), ((), ())),
                                        precision=HIGHEST, preferred_element_type=F32)
            at += 1


def project_kernel(last, chips, owned, away, group_ref, slot_ref, col_ref, live_ref, place_ref,
                   tiles_ref, *rest):
    n_src = len(away)
    sources, rest = rest[:n_src], rest[n_src:]
    if last:
        before_ref, rest = rest[0], rest[1:]
    n_out = len(rest) - 5
    outs = rest[:n_out]
    doc_ref, weights_ref, list_ref, buf_ref, sems = rest[n_out:]
    tpi, edge = buf_ref.shape[1], buf_ref.shape[3]
    chip, core = place_ref[0] // 2, place_ref[0] % 2
    blocks = sources[0].shape[0]

    count = collect(lambda g: (abs(g // 2 - chip) == chips - 1) == last, group_ref, live_ref,
                    list_ref, tiles_ref, buf_ref, sems)
    if last:
        doc_ref[...] = before_ref[...]
    else:
        doc_ref[...] = jnp.zeros_like(doc_ref)
    for source, (hops, other, piece) in zip(sources, away):
        there = chip + hops

        @pl.when((there >= 0) & (there < chips))
        def _():
            owner = there * 2 + (core if other == 0 else 1 - core)
            weights_ref[pl.ds(owner * owned + piece * blocks, blocks)] = source[...]

    def work(strip, at, valid):
        left = weights_ref[group_ref[strip] * owned + slot_ref[strip]]
        right = jnp.concatenate([buf_ref[at, j] for j in range(tpi)], axis=1)
        out = jnp.dot(left, right, preferred_element_type=F32) * valid
        for j in range(tpi):
            doc_ref[col_ref[strip, j]] += out[:, j * edge:(j + 1) * edge]

    in_batches(count, list_ref, tiles_ref, buf_ref, sems, work)
    if not last:
        outs[0][...] = doc_ref[...]
    else:
        n_dev = len(outs)
        held = outs[0].shape[0]
        for s in range(n_dev):
            at = partner_of(n_dev, place_ref[1], s) * held
            outs[s][...] = doc_ref[pl.ds(at, held)].astype(outs[s].dtype)


def project(last, scalars, tiles, sources, away, before, chips, owned, n_dev, held):
    strips, tpi, edge, _ = tiles.shape
    cols = sources[0].shape[1]
    if last:
        out_shape = [pltpu.VMEM((held, cols, edge), BF16 if s else F32) for s in range(n_dev)]
    else:
        out_shape = [pltpu.VMEM((n_dev * held, cols, edge), F32)]
    more = [near(before)] if last else []
    return pl.pallas_call(
        functools.partial(project_kernel, last, chips, owned, away),
        out_shape=out_shape,
        in_specs=[SM] * 5 + [HB] + [VM] * (len(sources) + len(more)),
        out_specs=[VM] * len(out_shape),
        scratch_shapes=[
            pltpu.VMEM((n_dev * held, cols, edge), F32),
            pltpu.VMEM((2 * chips * owned, cols, edge), BF16),
            pltpu.SMEM((strips,), jnp.int32),
            pltpu.VMEM((strips, tpi, edge, edge), BF16),
            pltpu.SemaphoreType.DMA((strips,)),
        ],
        compiler_params=params(28),
        cost_estimate=cost(strips // 4 if last else strips),
        name="project_last" if last else "project",
    )(*scalars, far_off(tiles), *[near(s) for s in sources], *more)


def finish_kernel(inverse_ref, own_ref, *rest):
    arrived, out_ref = rest[:-1], rest[-1]
    blocks, _, edge = own_ref.shape
    for b in range(blocks):
        total = own_ref[b]
        for r in arrived:
            total += r[b].astype(F32)
        out_ref[:, b * edge:(b + 1) * edge] = jnp.dot(
            inverse_ref[...], total, precision=HIGHEST, preferred_element_type=F32).astype(BF16)


def on_chip(kernel, out_shape, *args, in_specs=None, scratch=(), mib=8):
    specs = in_specs or [VM] * len(args)
    return pl.pallas_call(
        kernel, out_shape=out_shape, in_specs=specs,
        out_specs=jax.tree.map(lambda _: VM, out_shape,
                               is_leaf=lambda x: not isinstance(x, (tuple, list))),
        scratch_shapes=list(scratch), compiler_params=params(mib),
    )(*[near(a) if s is VM else a for a, s in zip(args, specs)])


def partner_of(n, me, s, back=False):
    if n & (n - 1) == 0:
        return me ^ s
    return (me + (n - s if back else s)) % n


def partners(n, s):
    return [(i, partner_of(n, i, s)) for i in range(n)]


def sum_over(x, axis, n, least=1):
    s = least
    while s < n:
        width = min(4, n // s)
        others = []
        for k in range(1, width):
            others.append(lax.ppermute(
                x, axis, [(i, i // (s * width) * (s * width)
                           + (i + k * s) % (s * width)) for i in range(n)]))
        for other in others:
            x = x + other
        s *= width
    return x


def on_device(tiles, tile_col, strip_group, strip_slot, live_count, omega, idf):
    n_group = lax.axis_size("group")
    n_dev = lax.axis_size("dev")
    chips = n_group // 2
    edge = tiles.shape[2]
    cols = omega.shape[1]
    owned = idf.shape[0] // edge
    pieces = 2 if owned % 2 == 0 else 1
    blocks = owned // pieces
    me, band = lax.axis_index("group"), lax.axis_index("dev")
    place = jnp.stack([me, band]).astype(jnp.int32)
    scalars = (strip_group, strip_slot, tile_col, live_count, place)
    swap = lambda x: lax.ppermute(x, "group", [(i, i ^ 1) for i in range(n_group)])

    def along(x, links):
        return lax.ppermute(
            x, "group", [(2 * a + k, 2 * b + k) for a, b in links for k in (0, 1)])

    col_own = omega.shape[0] // edge
    own_omega = omega.reshape(col_own, edge, cols)
    omegas = [own_omega] + [lax.ppermute(own_omega, "dev", partners(n_dev, s))
                            for s in range(1, n_dev)]

    far_mine, far_theirs = partial_sketch(True, scalars, tiles, omegas, chips, owned)
    far_pair = swap(far_theirs)
    piece_shape = pltpu.VMEM((blocks, edge, cols), BF16)
    first = [on_chip(functools.partial(first_kernel, blocks, p), piece_shape,
                     far_mine, far_pair) for p in range(pieces)]
    ends = [(0, 1), (chips - 1, chips - 2)]
    ups = [along(x, ends) for x in first]
    downs = list(ups) if chips > 2 else [jnp.zeros_like(x) for x in ups]
    rest_mine, rest_theirs = partial_sketch(False, scalars, tiles, omegas, chips, owned, first)
    rest_pair = swap(rest_theirs)
    for t in range(2, chips):
        up_links = [(c, c + 1) for c in range(t)]
        down_links = [(chips - 1 - a, chips - 1 - b) for a, b in up_links]
        for p in range(pieces):
            to_up, to_down = on_chip(
                functools.partial(relay_kernel, t, chips, owned, blocks, p),
                (piece_shape, piece_shape), place, far_mine, far_pair, rest_mine,
                rest_pair, ups[p], downs[p], in_specs=[SM] + [VM] * 6)
            ups[p] = along(to_up, up_links)
            downs[p] = along(to_down, down_links)

    gram = jnp.zeros((cols, cols), F32)
    sketches, weights = [], []
    for p in range(pieces):
        sk, w, gram = on_chip(
            functools.partial(combine_kernel, chips, owned, p),
            (pltpu.VMEM((blocks, edge, cols), F32), pltpu.VMEM((blocks, cols, edge), BF16),
             pltpu.VMEM((cols, cols), F32)),
            place, rest_mine, rest_pair, ups[p], downs[p], idf.reshape(owned, edge),
            gram, in_specs=[SM] + [VM] * 6)
        sketches.append(sk)
        weights.append(w)

    up_links = [(c, c + 1) for c in range(chips - 1)]
    down_links = [(c + 1, c) for c in range(chips - 1)]
    sources, away = [], []
    for p in range(pieces):
        sources += [weights[p], swap(weights[p])]
        away += [(0, 0, p), (0, 1, p)]
    below, above = list(weights), list(weights)
    for t in range(1, chips):
        if t == chips - 1:
            near_sources, near_away, sources, away = sources, away, [], []
        for p in range(pieces):
            below[p] = along(below[p], up_links)
            above[p] = along(above[p], down_links)
        for p in range(pieces):
            sources += [below[p], swap(below[p]), above[p], swap(above[p])]
            away += [(-t, 0, p), (-t, 1, p), (t, 0, p), (t, 1, p)]

    gram = sum_over(gram, "dev", n_dev)
    gram = gram + swap(gram)
    gram = sum_over(gram, "group", n_group, 2)
    inverse = on_chip(functools.partial(factor_kernel, idf.shape[0] * n_group * n_dev),
                      pltpu.VMEM((cols, cols), F32), gram,
                      scratch=[pltpu.VMEM((cols, cols), F32)])
    q_basis = on_chip(basis_kernel, jax.ShapeDtypeStruct((owned, edge, cols), F32),
                      inverse, *sketches).reshape(owned * edge, cols)

    docs = project(False, scalars, tiles, near_sources, near_away, None, chips, owned, n_dev,
                   col_own)[0]
    parts = project(True, scalars, tiles, sources, away, docs, chips, owned, n_dev, col_own)
    arrived = [lax.ppermute(parts[s], "dev", partners(n_dev, s)) for s in range(1, n_dev)]
    doc_factor = on_chip(finish_kernel, jax.ShapeDtypeStruct((cols, col_own * edge), BF16),
                         inverse, parts[0], *arrived)
    return (q_basis, doc_factor)


def solution(mesh):
    placed = (
        P(("group", "dev"), None, None, None),
        P(("group", "dev"), None),
        P(("group", "dev")),
        P(("group", "dev")),
        P(("group", "dev")),
        P(("group", "dev"), None),
        P(("group", "dev")),
    )

    return jax.shard_map(
        on_device,
        mesh=mesh,
        in_specs=placed,
        out_specs=(P(("group", "dev"), None), P(None, ("group", "dev"))),
        check_vma=False,
    )
```

time: 529 us -> 163 us (0.31)
  waiting for transfers between devices: 330 us -> 35.4 us
  other arithmetic: 76.6 us -> 0.13 us
  starting transfers between devices: 12 us -> 77.3 us
  Pallas kernels: 0 us -> 45.2 us
  local copies, waits for them, and re-layouts: 42.8 us -> 2.11 us
  matrix products: 40.1 us -> 0 us
  between operations: 14.6 us -> 1.79 us
  blocking collectives: 11.5 us -> 0 us
    all_to_all x2 -> x0, waiting for transfers between devices: 138 us -> none  [the longest x1 138 us: on_device(): lax.all_to_all(outgoing.reshape(n_group, capacity, tile_edge, sketch_cols...]
    psum x1 -> x0, waiting for transfers between devices: 117 us -> none  [on_device(): gram_matrix = lax.psum(local_gram, ('group', 'dev')) / total_terms]
    ppermute x0 -> x51, starting transfers between devices: none -> 77.3 us  [the longest x22 57.9 us: along(): lax.ppermute(x, 'group', [(2 * a + k, 2 * b + k) for a, b in links for k...]
    scatter-add x1 -> x0, other arithmetic: 47.9 us -> none  [on_device(): jax.ops.segment_sum(contrib.reshape(-1, sketch_cols, tile_edge), tile_col...]
    all_gather x1 -> x0, waiting for transfers between devices: 47.7 us -> none  [on_device(): band_rows = lax.all_gather(weighted, 'group', axis=0, tiled=True)]
    pallas_call x0 -> x15, Pallas kernels: none -> 45.2 us  [the longest x11 22.1 us: on_chip(): pl.pallas_call(kernel, out_shape=out_shape, in_specs=specs, out_specs=jax...]
    dot_general x4 -> x0, matrix products: 38 us -> none  [the longest x1 15.5 us: on_device(): jnp.einsum('sik,stij->stkj', strip_q, tiles, preferred_element_type=jnp.f...]
    ppermute x0 -> x51, waiting for transfers between devices: none -> 35.4 us  [the longest x22 28.5 us: along(): lax.ppermute(x, 'group', [(2 * a + k, 2 * b + k) for a, b in links for k...]
  transfers between devices with their start and end apart: 5 -> 51, of which waited for: 4 -> 15; matrix products, arithmetic and copies ran while one was open for 9% -> 1% of each run, Pallas kernels for 0% -> 19%
where the time goes in v2:
time: 163 us; the launch traced here: 162 us
  starting transfers between devices  77.3 us (47%)
  Pallas kernels  45.2 us (28%)
  waiting for transfers between devices  35.4 us (22%)
  local copies, waits for them, and re-layouts  2.11 us (1%)
  between operations  1.79 us (1%)
    ppermute x22, starting transfers between devices, along(): lax.ppermute(x, 'group', [(2 * a + k, 2 * b + k) for a, b in links for k...  57.9 us
    ppermute x22, waiting for transfers between devices, along(): lax.ppermute(x, 'group', [(2 * a + k, 2 * b + k) for a, b in links for k...  28.5 us
    pallas_call x11, Pallas kernels, on_chip(): pl.pallas_call(kernel, out_shape=out_shape, in_specs=specs, out_specs=jax...  22.1 us
    pallas_call x2, Pallas kernels, project(): pl.pallas_call(functools.partial(project_kernel, last, chips, owned, away...  11.6 us
    pallas_call x2, Pallas kernels, partial_sketch(): pl.pallas_call(functools.partial(sketch_kernel, far_only, chips, owned, l...  11.5 us
    ppermute x6, starting transfers between devices, sum_over(): lax.ppermute(x, axis, [(i, i // (s * width) * (s * width) + (i + k * s) %...  6.94 us
    ppermute x3, waiting for transfers between devices, on_device(): lax.ppermute(own_omega, 'dev', partners(n_dev, s))  4.94 us
    ppermute x3, starting transfers between devices, on_device(): lax.ppermute(own_omega, 'dev', partners(n_dev, s))  4.57 us
  transfers between devices with their start and end apart: 51, of which 15 were waited for; matrix products, arithmetic and copies ran while one was open for 1% of the time, Pallas kernels for 19%

profile of v2, /device:TPU:0, one launch (start us, length us, event | category | flops | bytes accessed | tf_op | source)
XLA Modules:
  0.0 162.0 jit_solution(6939057304038628519)
XLA Ops:
  0.6 3.0 %collective-permute-start = (bf16[4,128,128]{2,1,0:T(8,128)(2,1)}, bf16[4,128,128]{2,1,0:T(8,128)(2,1)S(1)}, u32[]{:S(2)}, u32[]{:S(2)}) collective-permute-start(bf16[4,128,128]{2,1,0:T(8,128)(2,1)} %bitcast.8), channel_id=1, source_target_pairs={{0,1},{1,0},{2,3},{3,2},{4,5},{5,4},{6,7},{7,6},{8,9},{9,8},{10,11... | collective-permute-start | bytes 393224 | tf_op jit(solution)/shard_map/ppermute | solution.py:347
  3.7 1.5 collective-permute-start.1
  6.7 1.1 collective-permute-done.rest_1_
  7.9 3.8 %collective-permute-done.1.rest_2_ = bf16[4,128,128]{2,1,0:T(8,128)(2,1)S(1)} collective-permute-done((bf16[4,128,128]{2,1,0:T(8,128)(2,1)}, bf16[4,128,128]{2,1,0:T(8,128)(2,1)S(1)}, u32[]{:S(2)}, u32[]{:S(2)}) %collective-permute-start.1) | collective-permute-done | bytes 131104 | tf_op jit(solution)/shard_map/ppermute | solution.py:347
  13.0 4.5 %sketch_far.1 = (f32[32,128,128]{2,1,0:T(8,128)S(1)}, bf16[16,128,128]{2,1,0:T(8,128)(2,1)S(1)}) custom-call(s32[72]{0:T(128)S(1)} %copy-done.1, s32[72]{0:T(128)S(1)} %copy-done.3, s32[72,5]{1,0:T(8,128)S(1)} %copy.10.col_ref, s32[1]{0:T(128)S(6)} %copy.13.live_ref, s32[2]{0:T(128)S(1)} %pad_add_fusion.place_ref, bf16[72,5,128,128]{3,2,1,0:T(8,128)(2,1)} %tiles_ref.7, ...), custom_call_target="tpu_custom_call" | custom-call | flops 4831838208 | bytes 9437184 | tf_op jit(solution)/shard_map/sketch_far/pallas_call | solution.py:108
  17.6 1.9 %collective-permute-done.3.pair_ref.far_pair = bf16[16,128,128]{2,1,0:T(8,128)(2,1)S(1)} collective-permute-done((bf16[16,128,128]{2,1,0:T(8,128)(2,1)S(1)}, bf16[16,128,128]{2,1,0:T(8,128)(2,1)S(1)}, u32[]{:S(2)}, u32[]{:S(2)}) %collective-permute-start.3) | collective-permute-done | bytes 524320 | tf_op jit(solution)/shard_map/ppermute | solution.py:339
  19.6 7.0 %sketch_rest.1 = (f32[96,128,128]{2,1,0:T(8,128)S(1)}, bf16[48,128,128]{2,1,0:T(8,128)(2,1)S(1)}) custom-call(s32[72]{0:T(128)S(1)} %copy-done.1, s32[72]{0:T(128)S(1)} %copy-done.3, s32[72,5]{1,0:T(8,128)S(1)} %copy.10.col_ref, s32[1]{0:T(128)S(6)} %copy.13.live_ref, s32[2]{0:T(128)S(1)} %pad_add_fusion.place_ref, bf16[72,5,128,128]{3,2,1,0:T(8,128)(2,1)} %tiles_ref.7, ...), custom_call_target="tpu_custom_call" | custom-call | flops 19327352832 | bytes 37748736 | tf_op jit(solution)/shard_map/sketch_rest/pallas_call | solution.py:108
  26.6 1.5 collective-permute-start.4
  28.1 2.5 %collective-permute-start.10 = (bf16[8,128,128]{2,1,0:T(8,128)(2,1)S(1)}, bf16[8,128,128]{2,1,0:T(8,128)(2,1)S(1)}, u32[]{:S(2)}, u32[]{:S(2)}) collective-permute-start(bf16[8,128,128]{2,1,0:T(8,128)(2,1)S(1)} %shard_map.86.rest_4_), channel_id=1, source_target_pairs={{0,8},{4,12},{24,16},{28,20},{1,9},{5,13},{25,17},{29,21},{2,10},{... | collective-permute-start | bytes 786440 | tf_op jit(solution)/shard_map/ppermute | solution.py:342
  30.6 1.3 collective-permute-start.5
  31.9 5.4 %collective-permute-done.10.up_ref.down_ref = bf16[8,128,128]{2,1,0:T(8,128)(2,1)S(1)} collective-permute-done((bf16[8,128,128]{2,1,0:T(8,128)(2,1)S(1)}, bf16[8,128,128]{2,1,0:T(8,128)(2,1)S(1)}, u32[]{:S(2)}, u32[]{:S(2)}) %collective-permute-start.10) | collective-permute-done | bytes 262176 | tf_op jit(solution)/shard_map/ppermute | solution.py:342
  38.0 4.4 %collective-permute-start.11 = (bf16[8,128,128]{2,1,0:T(8,128)(2,1)S(1)}, bf16[8,128,128]{2,1,0:T(8,128)(2,1)S(1)}, u32[]{:S(2)}, u32[]{:S(2)}) collective-permute-start(bf16[8,128,128]{2,1,0:T(8,128)(2,1)S(1)} %get-tuple-element.32), channel_id=1, source_target_pairs={{0,8},{4,12},{8,16},{12,20},{1,9},{5,13},{9,17},{13,21},{2,10},{6,... | collective-permute-start | bytes 786440 | tf_op jit(solution)/shard_map/ppermute | solution.py:342
  43.9 4.2 %collective-permute-start.6 = (bf16[8,128,128]{2,1,0:T(8,128)(2,1)S(1)}, bf16[8,128,128]{2,1,0:T(8,128)(2,1)S(1)}, u32[]{:S(2)}, u32[]{:S(2)}) collective-permute-start(bf16[8,128,128]{2,1,0:T(8,128)(2,1)S(1)} %get-tuple-element.28), channel_id=1, source_target_pairs={{0,8},{4,12},{8,16},{12,20},{1,9},{5,13},{9,17},{13,21},{2,10},{6,... | collective-permute-start | bytes 786440 | tf_op jit(solution)/shard_map/ppermute | solution.py:342
  49.5 6.6 %collective-permute-start.13 = (bf16[8,128,128]{2,1,0:T(8,128)(2,1)S(1)}, bf16[8,128,128]{2,1,0:T(8,128)(2,1)S(1)}, u32[]{:S(2)}, u32[]{:S(2)}) collective-permute-start(bf16[8,128,128]{2,1,0:T(8,128)(2,1)S(1)} %get-tuple-element.34), channel_id=1, source_target_pairs={{0,8},{4,12},{8,16},{12,20},{16,24},{20,28},{1,9},{5,13},{9,17},{1... | collective-permute-start | bytes 786440 | tf_op jit(solution)/shard_map/ppermute | solution.py:342
  56.1 1.3 collective-permute-start.14
  58.2 4.6 %collective-permute-start.8 = (bf16[8,128,128]{2,1,0:T(8,128)(2,1)S(1)}, bf16[8,128,128]{2,1,0:T(8,128)(2,1)S(1)}, u32[]{:S(2)}, u32[]{:S(2)}) collective-permute-start(bf16[8,128,128]{2,1,0:T(8,128)(2,1)S(1)} %get-tuple-element.30), channel_id=1, source_target_pairs={{0,8},{4,12},{8,16},{12,20},{16,24},{20,28},{1,9},{5,13},{9,17},{1... | collective-permute-start | bytes 786440 | tf_op jit(solution)/shard_map/ppermute | solution.py:342
  62.8 1.3 collective-permute-start.9
  64.5 1.3 shard_map.92
  66.6 4.4 %collective-permute-done.9.down_ref = bf16[8,128,128]{2,1,0:T(8,128)(2,1)S(1)} collective-permute-done((bf16[8,128,128]{2,1,0:T(8,128)(2,1)S(1)}, bf16[8,128,128]{2,1,0:T(8,128)(2,1)S(1)}, u32[]{:S(2)}, u32[]{:S(2)}) %collective-permute-start.9) | collective-permute-done | bytes 262176 | tf_op jit(solution)/shard_map/ppermute | solution.py:342
  71.0 1.3 shard_map.93
  72.4 1.8 %collective-permute-start.17 = (f32[128,128]{1,0:T(8,128)S(1)}, f32[128,128]{1,0:T(8,128)S(1)}, u32[]{:S(2)}, u32[]{:S(2)}) collective-permute-start(f32[128,128]{1,0:T(8,128)S(1)} %get-tuple-element.37), channel_id=1, source_target_pairs={{0,3},{1,0},{2,1},{3,2},{4,7},{5,4},{6,5},{7,6},{8,11},{9,8},{10,9... | collective-permute-start | bytes 196616 | tf_op jit(solution)/shard_map/ppermute | solution.py:318
  74.4 1.9 %collective-permute-start.15 = (f32[128,128]{1,0:T(8,128)S(1)}, f32[128,128]{1,0:T(8,128)S(1)}, u32[]{:S(2)}, u32[]{:S(2)}) collective-permute-start(f32[128,128]{1,0:T(8,128)S(1)} %get-tuple-element.37), channel_id=1, source_target_pairs={{0,1},{1,2},{2,3},{3,0},{4,5},{5,6},{6,7},{7,4},{8,9},{9,10},{10,1... | collective-permute-start | bytes 196616 | tf_op jit(solution)/shard_map/ppermute | solution.py:318
  76.3 3.5 %collective-permute-start.22 = (bf16[8,128,128]{2,1,0:T(8,128)(2,1)S(1)}, bf16[8,128,128]{2,1,0:T(8,128)(2,1)S(1)}, u32[]{:S(2)}, u32[]{:S(2)}) collective-permute-start(bf16[8,128,128]{2,1,0:T(8,128)(2,1)S(1)} %get-tuple-element.40.rest_0_), channel_id=1, source_target_pairs={{0,8},{4,12},{8,16},{12,20},{16,24},{20,28},{1,9},{5,13},{9,17},{1... | collective-permute-start | bytes 786440 | tf_op jit(solution)/shard_map/ppermute | solution.py:342
  79.9 1.3 collective-permute-start.26
  81.3 4.6 %collective-permute-start.30 = (bf16[8,128,128]{2,1,0:T(8,128)(2,1)S(1)}, bf16[8,128,128]{2,1,0:T(8,128)(2,1)S(1)}, u32[]{:S(2)}, u32[]{:S(2)}) collective-permute-start(bf16[8,128,128]{2,1,0:T(8,128)(2,1)S(1)} %get-tuple-element.41.rest_2_), channel_id=1, source_target_pairs={{0,8},{4,12},{8,16},{12,20},{16,24},{20,28},{1,9},{5,13},{9,17},{1... | collective-permute-start | bytes 786440 | tf_op jit(solution)/shard_map/ppermute | solution.py:342
  85.9 1.3 collective-permute-start.34
  88.1 4.2 %collective-permute-start.23 = (bf16[8,128,128]{2,1,0:T(8,128)(2,1)S(1)}, bf16[8,128,128]{2,1,0:T(8,128)(2,1)S(1)}, u32[]{:S(2)}, u32[]{:S(2)}) collective-permute-start(bf16[8,128,128]{2,1,0:T(8,128)(2,1)S(1)} %collective-permute-done.22.rest_4_), channel_id=1, source_target_pairs={{0,8},{4,12},{8,16},{12,20},{16,24},{20,28},{1,9},{5,13},{9,17},{1... | collective-permute-start | bytes 786440 | tf_op jit(solution)/shard_map/ppermute | solution.py:342
  92.3 1.3 collective-permute-start.27
  93.6 2.5 %collective-permute-done.34.rest_10_ = bf16[8,128,128]{2,1,0:T(8,128)(2,1)S(1)} collective-permute-done((bf16[8,128,128]{2,1,0:T(8,128)(2,1)S(1)}, bf16[8,128,128]{2,1,0:T(8,128)(2,1)S(1)}, u32[]{:S(2)}, u32[]{:S(2)}) %collective-permute-start.34) | collective-permute-done | bytes 262176 | tf_op jit(solution)/shard_map/ppermute | solution.py:342
  96.2 2.2 %collective-permute-start.31 = (bf16[8,128,128]{2,1,0:T(8,128)(2,1)S(1)}, bf16[8,128,128]{2,1,0:T(8,128)(2,1)S(1)}, u32[]{:S(2)}, u32[]{:S(2)}) collective-permute-start(bf16[8,128,128]{2,1,0:T(8,128)(2,1)S(1)} %collective-permute-done.30.rest_8_), channel_id=1, source_target_pairs={{0,8},{4,12},{8,16},{12,20},{16,24},{20,28},{1,9},{5,13},{9,17},{1... | collective-permute-start | bytes 786440 | tf_op jit(solution)/shard_map/ppermute | solution.py:342
  98.4 1.3 collective-permute-start.35
  100.3 2.5 %collective-permute-done.27.rest_14_ = bf16[8,128,128]{2,1,0:T(8,128)(2,1)S(1)} collective-permute-done((bf16[8,128,128]{2,1,0:T(8,128)(2,1)S(1)}, bf16[8,128,128]{2,1,0:T(8,128)(2,1)S(1)}, u32[]{:S(2)}, u32[]{:S(2)}) %collective-permute-start.27) | collective-permute-done | bytes 262176 | tf_op jit(solution)/shard_map/ppermute | solution.py:342
  103.7 4.4 %collective-permute-done.35.rest_18_ = bf16[8,128,128]{2,1,0:T(8,128)(2,1)S(1)} collective-permute-done((bf16[8,128,128]{2,1,0:T(8,128)(2,1)S(1)}, bf16[8,128,128]{2,1,0:T(8,128)(2,1)S(1)}, u32[]{:S(2)}, u32[]{:S(2)}) %collective-permute-start.35) | collective-permute-done | bytes 262176 | tf_op jit(solution)/shard_map/ppermute | solution.py:342
  108.1 3.6 %collective-permute-start.24 = (bf16[8,128,128]{2,1,0:T(8,128)(2,1)S(1)}, bf16[8,128,128]{2,1,0:T(8,128)(2,1)S(1)}, u32[]{:S(2)}, u32[]{:S(2)}) collective-permute-start(bf16[8,128,128]{2,1,0:T(8,128)(2,1)S(1)} %collective-permute-done.23.rest_12_), channel_id=1, source_target_pairs={{0,8},{4,12},{8,16},{12,20},{16,24},{20,28},{1,9},{5,13},{9,17},{1... | collective-permute-start | bytes 786440 | tf_op jit(solution)/shard_map/ppermute | solution.py:342
  111.8 1.3 collective-permute-start.28
  113.1 4.6 %collective-permute-start.32 = (bf16[8,128,128]{2,1,0:T(8,128)(2,1)S(1)}, bf16[8,128,128]{2,1,0:T(8,128)(2,1)S(1)}, u32[]{:S(2)}, u32[]{:S(2)}) collective-permute-start(bf16[8,128,128]{2,1,0:T(8,128)(2,1)S(1)} %collective-permute-done.31.rest_16_), channel_id=1, source_target_pairs={{0,8},{4,12},{8,16},{12,20},{16,24},{20,28},{1,9},{5,13},{9,17},{1... | collective-permute-start | bytes 786440 | tf_op jit(solution)/shard_map/ppermute | solution.py:342
  117.7 1.3 collective-permute-start.36
  120.4 1.2 collective-permute-done.32.rest_4_
  121.6 4.8 %collective-permute-done.36.rest_6_ = bf16[8,128,128]{2,1,0:T(8,128)(2,1)S(1)} collective-permute-done((bf16[8,128,128]{2,1,0:T(8,128)(2,1)S(1)}, bf16[8,128,128]{2,1,0:T(8,128)(2,1)S(1)}, u32[]{:S(2)}, u32[]{:S(2)}) %collective-permute-start.36) | collective-permute-done | bytes 262176 | tf_op jit(solution)/shard_map/ppermute | solution.py:342
  127.4 7.0 %project.1.rest_8_ = f32[16,128,128]{2,1,0:T(8,128)S(1)} custom-call(s32[72]{0:T(128)S(1)} %copy-done.2, s32[72]{0:T(128)S(1)} %copy-done.4, s32[72,5]{1,0:T(8,128)S(1)} %copy.10.col_ref, s32[1]{0:T(128)S(6)} %copy.13.live_ref, s32[2]{0:T(128)S(1)} %pad_add_fusion.place_ref, bf16[72,5,128,128]{3,2,1,0:T(8,128)(2,1)} %tiles_ref.7, ...), custom_call_target="tpu_custom_call" | custom-call | flops 19327352832 | bytes 37748736 | tf_op jit(solution)/shard_map/project/pallas_call | solution.py:263
  134.5 2.0 %collective-permute-start.20 = (f32[128,128]{1,0:T(8,128)S(1)}, f32[128,128]{1,0:T(8,128)S(1)}, u32[]{:S(2)}, u32[]{:S(2)}) collective-permute-start(f32[128,128]{1,0:T(8,128)S(1)} %add.24), channel_id=1, source_target_pairs={{0,16},{4,20},{8,24},{12,28},{16,0},{20,4},{24,8},{28,12},{1,17},{... | collective-permute-start | bytes 196616 | tf_op jit(solution)/shard_map/ppermute | solution.py:318
  136.5 1.0 collective-permute-start.19
  137.5 4.6 %project_last.1 = (f32[4,128,128]{2,1,0:T(8,128)S(1)}, bf16[4,128,128]{2,1,0:T(8,128)(2,1)S(1)}, bf16[4,128,128]{2,1,0:T(8,128)(2,1)S(1)}, bf16[4,128,128]{2,1,0:T(8,128)(2,1)S(1)}) custom-call(s32[72]{0:T(128)S(1)} %copy-done.2, s32[72]{0:T(128)S(1)} %copy-done.4, s32[72,5]{1,0:T(8,128)S(1)} %copy.10.col_ref, s32[1]{0:T(128)S(6)} %copy.13.live_ref, ...), custom_call_target="tpu_custom_call" | custom-call | flops 4831838208 | bytes 9437184 | tf_op jit(solution)/shard_map/project_last/pallas_call | solution.py:263
  142.0 1.6 collective-permute-start.48
  144.1 1.5 collective-permute-start.50
  145.6 12.1 %shard_map.94.inverse_ref = f32[128,128]{1,0:T(8,128)S(1)} custom-call(f32[128,128]{1,0:T(8,128)S(1)} %add_add_fusion.gram_ref), custom_call_target="tpu_custom_call" | custom-call | tf_op jit(solution)/shard_map/pallas_call | solution.py:294
  157.7 3.2 %shard_map.95 = f32[16,128,128]{2,1,0:T(8,128)} custom-call(f32[128,128]{1,0:T(8,128)S(1)} %shard_map.94.inverse_ref, f32[8,128,128]{2,1,0:T(8,128)S(1)} %get-tuple-element.38.rest_0_, f32[8,128,128]{2,1,0:T(8,128)S(1)} %get-tuple-element.39.rest_1_), custom_call_target="tpu_custom_call" | custom-call | tf_op jit(solution)/shard_map/pallas_call | solution.py:294
  160.9 1.0 shard_map.96
  (85 shorter events, 13.7 us)
Async XLA Ops:
  0.6 7.2 %collective-permute-start = (bf16[4,128,128]{2,1,0:T(8,128)(2,1)}, bf16[4,128,128]{2,1,0:T(8,128)(2,1)S(1)}, u32[]{:S(2)}, u32[]{:S(2)}) collective-permute-start(bf16[4,128,128]{2,1,0:T(8,128)(2,1)} %bitcast.8), channel_id=1, source_target_pairs={{0,1},{1,0},{2,3},{3,2},{4,5},{5,4},{6,7},{7,6},{8,9},{9,8},{10,11... | collective-permute-start | bytes 393224 | tf_op jit(solution)/shard_map/ppermute | solution.py:347
  3.7 8.0 %collective-permute-start.1 = (bf16[4,128,128]{2,1,0:T(8,128)(2,1)}, bf16[4,128,128]{2,1,0:T(8,128)(2,1)S(1)}, u32[]{:S(2)}, u32[]{:S(2)}) collective-permute-start(bf16[4,128,128]{2,1,0:T(8,128)(2,1)} %bitcast.9), channel_id=1, source_target_pairs={{0,2},{1,3},{2,0},{3,1},{4,6},{5,7},{6,4},{7,5},{8,10},{9,11},{10,... | collective-permute-start | bytes 393224 | tf_op jit(solution)/shard_map/ppermute | solution.py:347
  5.2 6.5 %collective-permute-start.2 = (bf16[4,128,128]{2,1,0:T(8,128)(2,1)}, bf16[4,128,128]{2,1,0:T(8,128)(2,1)S(1)}, u32[]{:S(2)}, u32[]{:S(2)}) collective-permute-start(bf16[4,128,128]{2,1,0:T(8,128)(2,1)} %bitcast.10), channel_id=1, source_target_pairs={{0,3},{1,2},{2,1},{3,0},{4,7},{5,6},{6,5},{7,4},{8,11},{9,10},{10,... | collective-permute-start | bytes 393224 | tf_op jit(solution)/shard_map/ppermute | solution.py:347
  26.6 10.6 %collective-permute-start.4 = (bf16[48,128,128]{2,1,0:T(8,128)(2,1)S(1)}, bf16[48,128,128]{2,1,0:T(8,128)(2,1)S(1)}, u32[]{:S(2)}, u32[]{:S(2)}) collective-permute-start(bf16[48,128,128]{2,1,0:T(8,128)(2,1)S(1)} %get-tuple-element.27), channel_id=1, source_target_pairs={{0,4},{4,0},{8,12},{12,8},{16,20},{20,16},{24,28},{28,24},{1,5},{5... | collective-permute-start | bytes 4718600 | tf_op jit(solution)/shard_map/ppermute | solution.py:339
  28.1 9.2 %collective-permute-start.10 = (bf16[8,128,128]{2,1,0:T(8,128)(2,1)S(1)}, bf16[8,128,128]{2,1,0:T(8,128)(2,1)S(1)}, u32[]{:S(2)}, u32[]{:S(2)}) collective-permute-start(bf16[8,128,128]{2,1,0:T(8,128)(2,1)S(1)} %shard_map.86.rest_4_), channel_id=1, source_target_pairs={{0,8},{4,12},{24,16},{28,20},{1,9},{5,13},{25,17},{29,21},{2,10},{... | collective-permute-start | bytes 786440 | tf_op jit(solution)/shard_map/ppermute | solution.py:342
  30.6 12.5 %collective-permute-start.5 = (bf16[8,128,128]{2,1,0:T(8,128)(2,1)S(1)}, bf16[8,128,128]{2,1,0:T(8,128)(2,1)S(1)}, u32[]{:S(2)}, u32[]{:S(2)}) collective-permute-start(bf16[8,128,128]{2,1,0:T(8,128)(2,1)S(1)} %shard_map.87.rest_5_), channel_id=1, source_target_pairs={{0,8},{4,12},{24,16},{28,20},{1,9},{5,13},{25,17},{29,21},{2,10},{... | collective-permute-start | bytes 786440 | tf_op jit(solution)/shard_map/ppermute | solution.py:342
  38.0 10.7 %collective-permute-start.11 = (bf16[8,128,128]{2,1,0:T(8,128)(2,1)S(1)}, bf16[8,128,128]{2,1,0:T(8,128)(2,1)S(1)}, u32[]{:S(2)}, u32[]{:S(2)}) collective-permute-start(bf16[8,128,128]{2,1,0:T(8,128)(2,1)S(1)} %get-tuple-element.32), channel_id=1, source_target_pairs={{0,8},{4,12},{8,16},{12,20},{1,9},{5,13},{9,17},{13,21},{2,10},{6,... | collective-permute-start | bytes 786440 | tf_op jit(solution)/shard_map/ppermute | solution.py:342
  42.4 6.3 %collective-permute-start.12 = (bf16[8,128,128]{2,1,0:T(8,128)(2,1)S(1)}, bf16[8,128,128]{2,1,0:T(8,128)(2,1)S(1)}, u32[]{:S(2)}, u32[]{:S(2)}) collective-permute-start(bf16[8,128,128]{2,1,0:T(8,128)(2,1)S(1)} %get-tuple-element.33), channel_id=1, source_target_pairs={{24,16},{28,20},{16,8},{20,12},{25,17},{29,21},{17,9},{21,13},{26,... | collective-permute-start | bytes 786440 | tf_op jit(solution)/shard_map/ppermute | solution.py:342
  43.9 13.6 %collective-permute-start.6 = (bf16[8,128,128]{2,1,0:T(8,128)(2,1)S(1)}, bf16[8,128,128]{2,1,0:T(8,128)(2,1)S(1)}, u32[]{:S(2)}, u32[]{:S(2)}) collective-permute-start(bf16[8,128,128]{2,1,0:T(8,128)(2,1)S(1)} %get-tuple-element.28), channel_id=1, source_target_pairs={{0,8},{4,12},{8,16},{12,20},{1,9},{5,13},{9,17},{13,21},{2,10},{6,... | collective-permute-start | bytes 786440 | tf_op jit(solution)/shard_map/ppermute | solution.py:342
  48.0 9.4 %collective-permute-start.7 = (bf16[8,128,128]{2,1,0:T(8,128)(2,1)S(1)}, bf16[8,128,128]{2,1,0:T(8,128)(2,1)S(1)}, u32[]{:S(2)}, u32[]{:S(2)}) collective-permute-start(bf16[8,128,128]{2,1,0:T(8,128)(2,1)S(1)} %get-tuple-element.29), channel_id=1, source_target_pairs={{24,16},{28,20},{16,8},{20,12},{25,17},{29,21},{17,9},{21,13},{26,... | collective-permute-start | bytes 786440 | tf_op jit(solution)/shard_map/ppermute | solution.py:342
  49.5 14.6 %collective-permute-start.13 = (bf16[8,128,128]{2,1,0:T(8,128)(2,1)S(1)}, bf16[8,128,128]{2,1,0:T(8,128)(2,1)S(1)}, u32[]{:S(2)}, u32[]{:S(2)}) collective-permute-start(bf16[8,128,128]{2,1,0:T(8,128)(2,1)S(1)} %get-tuple-element.34), channel_id=1, source_target_pairs={{0,8},{4,12},{8,16},{12,20},{16,24},{20,28},{1,9},{5,13},{9,17},{1... | collective-permute-start | bytes 786440 | tf_op jit(solution)/shard_map/ppermute | solution.py:342
  56.1 8.3 %collective-permute-start.14 = (bf16[8,128,128]{2,1,0:T(8,128)(2,1)S(1)}, bf16[8,128,128]{2,1,0:T(8,128)(2,1)S(1)}, u32[]{:S(2)}, u32[]{:S(2)}) collective-permute-start(bf16[8,128,128]{2,1,0:T(8,128)(2,1)S(1)} %get-tuple-element.35), channel_id=1, source_target_pairs={{24,16},{28,20},{16,8},{20,12},{8,0},{12,4},{25,17},{29,21},{17,9}... | collective-permute-start | bytes 786440 | tf_op jit(solution)/shard_map/ppermute | solution.py:342
  58.2 8.4 %collective-permute-start.8 = (bf16[8,128,128]{2,1,0:T(8,128)(2,1)S(1)}, bf16[8,128,128]{2,1,0:T(8,128)(2,1)S(1)}, u32[]{:S(2)}, u32[]{:S(2)}) collective-permute-start(bf16[8,128,128]{2,1,0:T(8,128)(2,1)S(1)} %get-tuple-element.30), channel_id=1, source_target_pairs={{0,8},{4,12},{8,16},{12,20},{16,24},{20,28},{1,9},{5,13},{9,17},{1... | collective-permute-start | bytes 786440 | tf_op jit(solution)/shard_map/ppermute | solution.py:342
  62.8 8.3 %collective-permute-start.9 = (bf16[8,128,128]{2,1,0:T(8,128)(2,1)S(1)}, bf16[8,128,128]{2,1,0:T(8,128)(2,1)S(1)}, u32[]{:S(2)}, u32[]{:S(2)}) collective-permute-start(bf16[8,128,128]{2,1,0:T(8,128)(2,1)S(1)} %get-tuple-element.31), channel_id=1, source_target_pairs={{24,16},{28,20},{16,8},{20,12},{8,0},{12,4},{25,17},{29,21},{17,9}... | collective-permute-start | bytes 786440 | tf_op jit(solution)/shard_map/ppermute | solution.py:342
  72.4 8.8 %collective-permute-start.17 = (f32[128,128]{1,0:T(8,128)S(1)}, f32[128,128]{1,0:T(8,128)S(1)}, u32[]{:S(2)}, u32[]{:S(2)}) collective-permute-start(f32[128,128]{1,0:T(8,128)S(1)} %get-tuple-element.37), channel_id=1, source_target_pairs={{0,3},{1,0},{2,1},{3,2},{4,7},{5,4},{6,5},{7,6},{8,11},{9,8},{10,9... | collective-permute-start | bytes 196616 | tf_op jit(solution)/shard_map/ppermute | solution.py:318
  74.2 7.0 %collective-permute-start.16 = (f32[128,128]{1,0:T(8,128)S(1)}, f32[128,128]{1,0:T(8,128)S(1)}, u32[]{:S(2)}, u32[]{:S(2)}) collective-permute-start(f32[128,128]{1,0:T(8,128)S(1)} %get-tuple-element.37), channel_id=1, source_target_pairs={{0,2},{1,3},{2,0},{3,1},{4,6},{5,7},{6,4},{7,5},{8,10},{9,11},{10,... | collective-permute-start | bytes 196616 | tf_op jit(solution)/shard_map/ppermute | solution.py:318
  74.4 6.8 %collective-permute-start.15 = (f32[128,128]{1,0:T(8,128)S(1)}, f32[128,128]{1,0:T(8,128)S(1)}, u32[]{:S(2)}, u32[]{:S(2)}) collective-permute-start(f32[128,128]{1,0:T(8,128)S(1)} %get-tuple-element.37), channel_id=1, source_target_pairs={{0,1},{1,2},{2,3},{3,0},{4,5},{5,6},{6,7},{7,4},{8,9},{9,10},{10,1... | collective-permute-start | bytes 196616 | tf_op jit(solution)/shard_map/ppermute | solution.py:318
  76.3 11.1 %collective-permute-start.22 = (bf16[8,128,128]{2,1,0:T(8,128)(2,1)S(1)}, bf16[8,128,128]{2,1,0:T(8,128)(2,1)S(1)}, u32[]{:S(2)}, u32[]{:S(2)}) collective-permute-start(bf16[8,128,128]{2,1,0:T(8,128)(2,1)S(1)} %get-tuple-element.40.rest_0_), channel_id=1, source_target_pairs={{0,8},{4,12},{8,16},{12,20},{16,24},{20,28},{1,9},{5,13},{9,17},{1... | collective-permute-start | bytes 786440 | tf_op jit(solution)/shard_map/ppermute | solution.py:342
  79.9 8.3 %collective-permute-start.26 = (bf16[8,128,128]{2,1,0:T(8,128)(2,1)S(1)}, bf16[8,128,128]{2,1,0:T(8,128)(2,1)S(1)}, u32[]{:S(2)}, u32[]{:S(2)}) collective-permute-start(bf16[8,128,128]{2,1,0:T(8,128)(2,1)S(1)} %get-tuple-element.40.rest_0_), channel_id=1, source_target_pairs={{8,0},{12,4},{16,8},{20,12},{24,16},{28,20},{9,1},{13,5},{17,9},{2... | collective-permute-start | bytes 786440 | tf_op jit(solution)/shard_map/ppermute | solution.py:342
  81.3 11.0 %collective-permute-start.30 = (bf16[8,128,128]{2,1,0:T(8,128)(2,1)S(1)}, bf16[8,128,128]{2,1,0:T(8,128)(2,1)S(1)}, u32[]{:S(2)}, u32[]{:S(2)}) collective-permute-start(bf16[8,128,128]{2,1,0:T(8,128)(2,1)S(1)} %get-tuple-element.41.rest_2_), channel_id=1, source_target_pairs={{0,8},{4,12},{8,16},{12,20},{16,24},{20,28},{1,9},{5,13},{9,17},{1... | collective-permute-start | bytes 786440 | tf_op jit(solution)/shard_map/ppermute | solution.py:342
  85.9 10.3 %collective-permute-start.34 = (bf16[8,128,128]{2,1,0:T(8,128)(2,1)S(1)}, bf16[8,128,128]{2,1,0:T(8,128)(2,1)S(1)}, u32[]{:S(2)}, u32[]{:S(2)}) collective-permute-start(bf16[8,128,128]{2,1,0:T(8,128)(2,1)S(1)} %get-tuple-element.41.rest_2_), channel_id=1, source_target_pairs={{8,0},{12,4},{16,8},{20,12},{24,16},{28,20},{9,1},{13,5},{17,9},{2... | collective-permute-start | bytes 786440 | tf_op jit(solution)/shard_map/ppermute | solution.py:342
  87.2 11.2 %collective-permute-start.38 = (bf16[8,128,128]{2,1,0:T(8,128)(2,1)S(1)}, bf16[8,128,128]{2,1,0:T(8,128)(2,1)S(1)}, u32[]{:S(2)}, u32[]{:S(2)}) collective-permute-start(bf16[8,128,128]{2,1,0:T(8,128)(2,1)S(1)} %get-tuple-element.40.rest_0_), channel_id=1, source_target_pairs={{0,4},{4,0},{8,12},{12,8},{16,20},{20,16},{24,28},{28,24},{1,5},{5... | collective-permute-start | bytes 786440 | tf_op jit(solution)/shard_map/ppermute | solution.py:339
  87.5 12.2 %collective-permute-start.39 = (bf16[8,128,128]{2,1,0:T(8,128)(2,1)S(1)}, bf16[8,128,128]{2,1,0:T(8,128)(2,1)S(1)}, u32[]{:S(2)}, u32[]{:S(2)}) collective-permute-start(bf16[8,128,128]{2,1,0:T(8,128)(2,1)S(1)} %get-tuple-element.41.rest_2_), channel_id=1, source_target_pairs={{0,4},{4,0},{8,12},{12,8},{16,20},{20,16},{24,28},{28,24},{1,5},{5... | collective-permute-start | bytes 786440 | tf_op jit(solution)/shard_map/ppermute | solution.py:339
  88.1 11.7 %collective-permute-start.23 = (bf16[8,128,128]{2,1,0:T(8,128)(2,1)S(1)}, bf16[8,128,128]{2,1,0:T(8,128)(2,1)S(1)}, u32[]{:S(2)}, u32[]{:S(2)}) collective-permute-start(bf16[8,128,128]{2,1,0:T(8,128)(2,1)S(1)} %collective-permute-done.22.rest_4_), channel_id=1, source_target_pairs={{0,8},{4,12},{8,16},{12,20},{16,24},{20,28},{1,9},{5,13},{9,17},{1... | collective-permute-start | bytes 786440 | tf_op jit(solution)/shard_map/ppermute | solution.py:342
  92.3 10.5 %collective-permute-start.27 = (bf16[8,128,128]{2,1,0:T(8,128)(2,1)S(1)}, bf16[8,128,128]{2,1,0:T(8,128)(2,1)S(1)}, u32[]{:S(2)}, u32[]{:S(2)}) collective-permute-start(bf16[8,128,128]{2,1,0:T(8,128)(2,1)S(1)} %collective-permute-done.26.rest_6_), channel_id=1, source_target_pairs={{8,0},{12,4},{16,8},{20,12},{24,16},{28,20},{9,1},{13,5},{17,9},{2... | collective-permute-start | bytes 786440 | tf_op jit(solution)/shard_map/ppermute | solution.py:342
  96.2 7.5 %collective-permute-start.31 = (bf16[8,128,128]{2,1,0:T(8,128)(2,1)S(1)}, bf16[8,128,128]{2,1,0:T(8,128)(2,1)S(1)}, u32[]{:S(2)}, u32[]{:S(2)}) collective-permute-start(bf16[8,128,128]{2,1,0:T(8,128)(2,1)S(1)} %collective-permute-done.30.rest_8_), channel_id=1, source_target_pairs={{0,8},{4,12},{8,16},{12,20},{16,24},{20,28},{1,9},{5,13},{9,17},{1... | collective-permute-start | bytes 786440 | tf_op jit(solution)/shard_map/ppermute | solution.py:342
  98.4 9.7 %collective-permute-start.35 = (bf16[8,128,128]{2,1,0:T(8,128)(2,1)S(1)}, bf16[8,128,128]{2,1,0:T(8,128)(2,1)S(1)}, u32[]{:S(2)}, u32[]{:S(2)}) collective-permute-start(bf16[8,128,128]{2,1,0:T(8,128)(2,1)S(1)} %collective-permute-done.34.rest_10_), channel_id=1, source_target_pairs={{8,0},{12,4},{16,8},{20,12},{24,16},{28,20},{9,1},{13,5},{17,9},{2... | collective-permute-start | bytes 786440 | tf_op jit(solution)/shard_map/ppermute | solution.py:342
  99.7 12.1 %collective-permute-start.40 = (bf16[8,128,128]{2,1,0:T(8,128)(2,1)S(1)}, bf16[8,128,128]{2,1,0:T(8,128)(2,1)S(1)}, u32[]{:S(2)}, u32[]{:S(2)}) collective-permute-start(bf16[8,128,128]{2,1,0:T(8,128)(2,1)S(1)} %collective-permute-done.22.rest_4_), channel_id=1, source_target_pairs={{0,4},{4,0},{8,12},{12,8},{16,20},{20,16},{24,28},{28,24},{1,5},{5... | collective-permute-start | bytes 786440 | tf_op jit(solution)/shard_map/ppermute | solution.py:339
  99.8 13.3 %collective-permute-start.41 = (bf16[8,128,128]{2,1,0:T(8,128)(2,1)S(1)}, bf16[8,128,128]{2,1,0:T(8,128)(2,1)S(1)}, u32[]{:S(2)}, u32[]{:S(2)}) collective-permute-start(bf16[8,128,128]{2,1,0:T(8,128)(2,1)S(1)} %collective-permute-done.26.rest_6_), channel_id=1, source_target_pairs={{0,4},{4,0},{8,12},{12,8},{16,20},{20,16},{24,28},{28,24},{1,5},{5... | collective-permute-start | bytes 786440 | tf_op jit(solution)/shard_map/ppermute | solution.py:339
  102.8 14.9 %collective-permute-start.42 = (bf16[8,128,128]{2,1,0:T(8,128)(2,1)S(1)}, bf16[8,128,128]{2,1,0:T(8,128)(2,1)S(1)}, u32[]{:S(2)}, u32[]{:S(2)}) collective-permute-start(bf16[8,128,128]{2,1,0:T(8,128)(2,1)S(1)} %collective-permute-done.30.rest_8_), channel_id=1, source_target_pairs={{0,4},{4,0},{8,12},{12,8},{16,20},{20,16},{24,28},{28,24},{1,5},{5... | collective-permute-start | bytes 786440 | tf_op jit(solution)/shard_map/ppermute | solution.py:339
  103.7 15.3 %collective-permute-start.43 = (bf16[8,128,128]{2,1,0:T(8,128)(2,1)S(1)}, bf16[8,128,128]{2,1,0:T(8,128)(2,1)S(1)}, u32[]{:S(2)}, u32[]{:S(2)}) collective-permute-start(bf16[8,128,128]{2,1,0:T(8,128)(2,1)S(1)} %collective-permute-done.34.rest_10_), channel_id=1, source_target_pairs={{0,4},{4,0},{8,12},{12,8},{16,20},{20,16},{24,28},{28,24},{1,5},{5... | collective-permute-start | bytes 786440 | tf_op jit(solution)/shard_map/ppermute | solution.py:339
  108.1 10.9 %collective-permute-start.24 = (bf16[8,128,128]{2,1,0:T(8,128)(2,1)S(1)}, bf16[8,128,128]{2,1,0:T(8,128)(2,1)S(1)}, u32[]{:S(2)}, u32[]{:S(2)}) collective-permute-start(bf16[8,128,128]{2,1,0:T(8,128)(2,1)S(1)} %collective-permute-done.23.rest_12_), channel_id=1, source_target_pairs={{0,8},{4,12},{8,16},{12,20},{16,24},{20,28},{1,9},{5,13},{9,17},{1... | collective-permute-start | bytes 786440 | tf_op jit(solution)/shard_map/ppermute | solution.py:342
  111.8 8.6 %collective-permute-start.28 = (bf16[8,128,128]{2,1,0:T(8,128)(2,1)S(1)}, bf16[8,128,128]{2,1,0:T(8,128)(2,1)S(1)}, u32[]{:S(2)}, u32[]{:S(2)}) collective-permute-start(bf16[8,128,128]{2,1,0:T(8,128)(2,1)S(1)} %collective-permute-done.27.rest_14_), channel_id=1, source_target_pairs={{8,0},{12,4},{16,8},{20,12},{24,16},{28,20},{9,1},{13,5},{17,9},{2... | collective-permute-start | bytes 786440 | tf_op jit(solution)/shard_map/ppermute | solution.py:342
  113.1 8.5 %collective-permute-start.32 = (bf16[8,128,128]{2,1,0:T(8,128)(2,1)S(1)}, bf16[8,128,128]{2,1,0:T(8,128)(2,1)S(1)}, u32[]{:S(2)}, u32[]{:S(2)}) collective-permute-start(bf16[8,128,128]{2,1,0:T(8,128)(2,1)S(1)} %collective-permute-done.31.rest_16_), channel_id=1, source_target_pairs={{0,8},{4,12},{8,16},{12,20},{16,24},{20,28},{1,9},{5,13},{9,17},{1... | collective-permute-start | bytes 786440 | tf_op jit(solution)/shard_map/ppermute | solution.py:342
  117.7 8.7 %collective-permute-start.36 = (bf16[8,128,128]{2,1,0:T(8,128)(2,1)S(1)}, bf16[8,128,128]{2,1,0:T(8,128)(2,1)S(1)}, u32[]{:S(2)}, u32[]{:S(2)}) collective-permute-start(bf16[8,128,128]{2,1,0:T(8,128)(2,1)S(1)} %collective-permute-done.35.rest_18_), channel_id=1, source_target_pairs={{8,0},{12,4},{16,8},{20,12},{24,16},{28,20},{9,1},{13,5},{17,9},{2... | collective-permute-start | bytes 786440 | tf_op jit(solution)/shard_map/ppermute | solution.py:342
  119.0 7.4 %collective-permute-start.44 = (bf16[8,128,128]{2,1,0:T(8,128)(2,1)S(1)}, bf16[8,128,128]{2,1,0:T(8,128)(2,1)S(1)}, u32[]{:S(2)}, u32[]{:S(2)}) collective-permute-start(bf16[8,128,128]{2,1,0:T(8,128)(2,1)S(1)} %collective-permute-done.23.rest_12_), channel_id=1, source_target_pairs={{0,4},{4,0},{8,12},{12,8},{16,20},{20,16},{24,28},{28,24},{1,5},{5... | collective-permute-start | bytes 786440 | tf_op jit(solution)/shard_map/ppermute | solution.py:339
  119.1 7.3 %collective-permute-start.45 = (bf16[8,128,128]{2,1,0:T(8,128)(2,1)S(1)}, bf16[8,128,128]{2,1,0:T(8,128)(2,1)S(1)}, u32[]{:S(2)}, u32[]{:S(2)}) collective-permute-start(bf16[8,128,128]{2,1,0:T(8,128)(2,1)S(1)} %collective-permute-done.27.rest_14_), channel_id=1, source_target_pairs={{0,4},{4,0},{8,12},{12,8},{16,20},{20,16},{24,28},{28,24},{1,5},{5... | collective-permute-start | bytes 786440 | tf_op jit(solution)/shard_map/ppermute | solution.py:339
  120.4 6.5 %collective-permute-start.46 = (bf16[8,128,128]{2,1,0:T(8,128)(2,1)S(1)}, bf16[8,128,128]{2,1,0:T(8,128)(2,1)S(1)}, u32[]{:S(2)}, u32[]{:S(2)}) collective-permute-start(bf16[8,128,128]{2,1,0:T(8,128)(2,1)S(1)} %collective-permute-done.31.rest_16_), channel_id=1, source_target_pairs={{0,4},{4,0},{8,12},{12,8},{16,20},{20,16},{24,28},{28,24},{1,5},{5... | collective-permute-start | bytes 786440 | tf_op jit(solution)/shard_map/ppermute | solution.py:339
  126.4 17.7 %collective-permute-start.21 = (f32[128,128]{1,0:T(8,128)S(1)}, f32[128,128]{1,0:T(8,128)S(1)}, u32[]{:S(2)}, u32[]{:S(2)}) collective-permute-start(f32[128,128]{1,0:T(8,128)S(1)} %add.24), channel_id=1, source_target_pairs={{0,24},{4,28},{8,0},{12,4},{16,8},{20,12},{24,16},{28,20},{1,25},{... | collective-permute-start | bytes 196616 | tf_op jit(solution)/shard_map/ppermute | solution.py:318
  126.4 8.1 %collective-permute-start.25 = (bf16[8,128,128]{2,1,0:T(8,128)(2,1)S(1)}, bf16[8,128,128]{2,1,0:T(8,128)(2,1)S(1)}, u32[]{:S(2)}, u32[]{:S(2)}) collective-permute-start(bf16[8,128,128]{2,1,0:T(8,128)(2,1)S(1)} %collective-permute-done.24.rest_0_), channel_id=1, source_target_pairs={{0,4},{4,0},{8,12},{12,8},{16,20},{20,16},{24,28},{28,24},{1,5},{5... | collective-permute-start | bytes 786440 | tf_op jit(solution)/shard_map/ppermute | solution.py:339
  126.4 10.1 %collective-permute-start.29 = (bf16[8,128,128]{2,1,0:T(8,128)(2,1)S(1)}, bf16[8,128,128]{2,1,0:T(8,128)(2,1)S(1)}, u32[]{:S(2)}, u32[]{:S(2)}) collective-permute-start(bf16[8,128,128]{2,1,0:T(8,128)(2,1)S(1)} %collective-permute-done.28.rest_2_), channel_id=1, source_target_pairs={{0,4},{4,0},{8,12},{12,8},{16,20},{20,16},{24,28},{28,24},{1,5},{5... | collective-permute-start | bytes 786440 | tf_op jit(solution)/shard_map/ppermute | solution.py:339
  126.9 10.5 %collective-permute-start.33 = (bf16[8,128,128]{2,1,0:T(8,128)(2,1)S(1)}, bf16[8,128,128]{2,1,0:T(8,128)(2,1)S(1)}, u32[]{:S(2)}, u32[]{:S(2)}) collective-permute-start(bf16[8,128,128]{2,1,0:T(8,128)(2,1)S(1)} %collective-permute-done.32.rest_4_), channel_id=1, source_target_pairs={{0,4},{4,0},{8,12},{12,8},{16,20},{20,16},{24,28},{28,24},{1,5},{5... | collective-permute-start | bytes 786440 | tf_op jit(solution)/shard_map/ppermute | solution.py:339
  127.0 10.5 %collective-permute-start.37 = (bf16[8,128,128]{2,1,0:T(8,128)(2,1)S(1)}, bf16[8,128,128]{2,1,0:T(8,128)(2,1)S(1)}, u32[]{:S(2)}, u32[]{:S(2)}) collective-permute-start(bf16[8,128,128]{2,1,0:T(8,128)(2,1)S(1)} %collective-permute-done.36.rest_6_), channel_id=1, source_target_pairs={{0,4},{4,0},{8,12},{12,8},{16,20},{20,16},{24,28},{28,24},{1,5},{5... | collective-permute-start | bytes 786440 | tf_op jit(solution)/shard_map/ppermute | solution.py:339
  134.5 11.1 %collective-permute-start.20 = (f32[128,128]{1,0:T(8,128)S(1)}, f32[128,128]{1,0:T(8,128)S(1)}, u32[]{:S(2)}, u32[]{:S(2)}) collective-permute-start(f32[128,128]{1,0:T(8,128)S(1)} %add.24), channel_id=1, source_target_pairs={{0,16},{4,20},{8,24},{12,28},{16,0},{20,4},{24,8},{28,12},{1,17},{... | collective-permute-start | bytes 196616 | tf_op jit(solution)/shard_map/ppermute | solution.py:318
  136.5 9.1 %collective-permute-start.19 = (f32[128,128]{1,0:T(8,128)S(1)}, f32[128,128]{1,0:T(8,128)S(1)}, u32[]{:S(2)}, u32[]{:S(2)}) collective-permute-start(f32[128,128]{1,0:T(8,128)S(1)} %add.24), channel_id=1, source_target_pairs={{0,8},{4,12},{8,16},{12,20},{16,24},{20,28},{24,0},{28,4},{1,9},{5... | collective-permute-start | bytes 196616 | tf_op jit(solution)/shard_map/ppermute | solution.py:318
  142.0 18.9 %collective-permute-start.48 = (bf16[4,128,128]{2,1,0:T(8,128)(2,1)S(1)}, bf16[4,128,128]{2,1,0:T(8,128)(2,1)S(1)}, u32[]{:S(2)}, u32[]{:S(2)}) collective-permute-start(bf16[4,128,128]{2,1,0:T(8,128)(2,1)S(1)} %get-tuple-element.43), channel_id=1, source_target_pairs={{0,1},{1,0},{2,3},{3,2},{4,5},{5,4},{6,7},{7,6},{8,9},{9,8},{10,11... | collective-permute-start | bytes 393224 | tf_op jit(solution)/shard_map/ppermute | solution.py:412
  143.6 17.3 %collective-permute-start.49 = (bf16[4,128,128]{2,1,0:T(8,128)(2,1)S(1)}, bf16[4,128,128]{2,1,0:T(8,128)(2,1)S(1)}, u32[]{:S(2)}, u32[]{:S(2)}) collective-permute-start(bf16[4,128,128]{2,1,0:T(8,128)(2,1)S(1)} %get-tuple-element.44), channel_id=1, source_target_pairs={{0,2},{1,3},{2,0},{3,1},{4,6},{5,7},{6,4},{7,5},{8,10},{9,11},{10,... | collective-permute-start | bytes 393224 | tf_op jit(solution)/shard_map/ppermute | solution.py:412
  144.1 16.8 %collective-permute-start.50 = (bf16[4,128,128]{2,1,0:T(8,128)(2,1)S(1)}, bf16[4,128,128]{2,1,0:T(8,128)(2,1)S(1)}, u32[]{:S(2)}, u32[]{:S(2)}) collective-permute-start(bf16[4,128,128]{2,1,0:T(8,128)(2,1)S(1)} %get-tuple-element.45), channel_id=1, source_target_pairs={{0,3},{1,2},{2,1},{3,0},{4,7},{5,6},{6,5},{7,4},{8,11},{9,10},{10,... | collective-permute-start | bytes 393224 | tf_op jit(solution)/shard_map/ppermute | solution.py:412
  (8 other events, 135.8 us)

commit v3 on v2

v3 whole, which is shorter than its diff:
```python
import functools
import jax
import jax.numpy as jnp
from jax import lax
from jax.experimental import pallas as pl
from jax.experimental.pallas import tpu as pltpu
from jax.sharding import PartitionSpec as P

F32 = jnp.float32
BF16 = jnp.bfloat16
HIGHEST = lax.Precision.HIGHEST
BATCH = 4
WIDE = 4

VM = pl.BlockSpec(memory_space=pltpu.VMEM)
SM = pl.BlockSpec(memory_space=pltpu.SMEM)
HB = pl.BlockSpec(memory_space=pltpu.HBM)


def near(x):
    return pltpu.with_memory_space_constraint(x, pltpu.VMEM)


def far_off(x):
    return pltpu.with_memory_space_constraint(x, pltpu.HBM)


def cost(strips):
    return pl.CostEstimate(flops=strips << 28, bytes_accessed=strips << 19, transcendentals=0)


def params(mib):
    return pltpu.CompilerParams(vmem_limit_bytes=mib << 20)


ME, BAND, LIVE, LISTS = 0, 1, 2, 3


class Ints:
    def __init__(self, ref, strips, tpi):
        self.ref, self.strips, self.tpi = ref, strips, tpi

    def me(self):
        return self.ref[ME]

    def band(self):
        return self.ref[BAND]

    def live(self):
        return self.ref[LIVE]

    def group(self, strip):
        return self.ref[LISTS + strip]

    def slot(self, strip):
        return self.ref[LISTS + self.strips + strip]

    def column(self, strip, j):
        return self.ref[LISTS + (2 + j) * self.strips + strip]


def far_chip(chip, chips):
    return jnp.where(chip < chips // 2, chips - 1, 0)


def lists_kernel(strips, tpi, chips, ints_ref, lists_ref):
    ints = Ints(ints_ref, strips, tpi)
    far = far_chip(ints.me() // 2, chips)

    def scan(strip, count):
        hit = ints.group(strip) // 2 == far
        lists_ref[jnp.where(hit, count, strips - 1 - strip + count)] = strip
        return count + hit.astype(jnp.int32)

    count = lax.fori_loop(0, ints.live(), scan, jnp.int32(0))
    lists_ref[strips] = count
    lists_ref[strips + 1] = ints.live() - count


class Picked:
    def __init__(self, lists_ref, strips, far, rest):
        n_far, n_rest = lists_ref[strips], lists_ref[strips + 1]
        self.lists, self.strips = lists_ref, strips
        self.start = jnp.where(rest, strips - n_rest, 0)
        self.count = jnp.where(far, n_far, 0) + jnp.where(rest, n_rest, 0)

    def strip(self, at):
        where = self.start + at
        return self.lists[jnp.where(where >= self.strips, where - self.strips, where)]

    def fetch(self, tiles_ref, buf_ref, sems):
        def begin(at, carry):
            pltpu.make_async_copy(tiles_ref.at[self.strip(at)], buf_ref.at[at],
                                  sems.at[at]).start()
            return carry

        lax.fori_loop(0, self.count, begin, jnp.int32(0))

    def in_batches(self, tiles_ref, buf_ref, sems, work):
        def trip(b, carry):
            for i in range(BATCH):
                at = b * BATCH + i

                @pl.when(at < self.count)
                def _():
                    pltpu.make_async_copy(tiles_ref.at[0], buf_ref.at[at], sems.at[at]).wait()

            for i in range(BATCH):
                at = jnp.minimum(b * BATCH + i, self.count - 1)
                work(self.strip(at), at, (b * BATCH + i < self.count).astype(F32))
            return carry

        lax.fori_loop(0, (self.count + BATCH - 1) // BATCH, trip, jnp.int32(0))


def sketch_kernel(far_only, chips, owned, n_src, ints_ref, lists_ref, tiles_ref, *rest):
    sources = rest[:n_src]
    both_ref, theirs_ref, omega_ref, buf_ref, sems = rest[-5:]
    half = theirs_ref.shape[0]
    strips, tpi = buf_ref.shape[:2]
    ints = Ints(ints_ref, strips, tpi)
    chip, core, band = ints.me() // 2, ints.me() % 2, ints.band()
    far = far_chip(chip, chips)
    held = sources[0].shape[0]
    own = pltpu.make_async_copy(sources[0], omega_ref.at[pl.ds(band * held, held)],
                                sems.at[strips])
    own.start()
    picked = Picked(lists_ref, strips, far_only, not far_only)
    picked.fetch(tiles_ref, buf_ref, sems)
    both_ref[...] = jnp.zeros_like(both_ref)
    for s in range(1, n_src):
        omega_ref[pl.ds(partner_of(n_src, band, s, back=True) * held, held)] = sources[s][...]
    own.wait()

    def work(strip, at, valid):
        owner = ints.group(strip)
        unit = jnp.int32(0) if far_only else owner // 2 - (far == 0).astype(jnp.int32)
        side = jnp.where(owner % 2 == core, 0, half)
        block = side + unit * owned + ints.slot(strip)
        left = jnp.concatenate([buf_ref[at, j] for j in range(tpi)], axis=1)
        right = jnp.concatenate([omega_ref[ints.column(strip, j)] for j in range(tpi)], axis=0)
        both_ref[block] += jnp.dot(left, right, preferred_element_type=F32) * valid

    picked.in_batches(tiles_ref, buf_ref, sems, work)
    theirs_ref[...] = both_ref[pl.ds(half, half)].astype(BF16)


def partial_sketch(far_only, scalars, tiles, sources, chips, owned, after=()):
    strips, tpi, edge, _ = tiles.shape
    col_own, _, cols = sources[0].shape
    blocks = owned * (1 if far_only else chips - 1)
    return pl.pallas_call(
        functools.partial(sketch_kernel, far_only, chips, owned, len(sources)),
        out_shape=(pltpu.VMEM((2 * blocks, edge, cols), F32),
                   pltpu.VMEM((blocks, edge, cols), BF16)),
        in_specs=[SM] * 2 + [HB] * 2 + [VM] * (len(sources) - 1 + len(after)),
        out_specs=(VM, VM),
        scratch_shapes=[
            pltpu.VMEM((col_own * len(sources), edge, cols), BF16),
            pltpu.VMEM((strips, tpi, edge, edge), BF16),
            pltpu.SemaphoreType.DMA((strips + 1,)),
        ],
        compiler_params=params(16),
        cost_estimate=cost(strips // 4 if far_only else strips),
        name="sketch_far" if far_only else "sketch_rest",
    )(*scalars, far_off(tiles), far_off(sources[0]),
      *[near(s) for s in (*sources[1:], *after)])


def first_kernel(blocks, piece, mine_ref, pair_ref, out_ref):
    rows = pl.ds(piece * blocks, blocks)
    out_ref[...] = (mine_ref[rows] + pair_ref[rows].astype(F32)).astype(BF16)


def relay_kernel(t, chips, owned, blocks, piece, ints_ref, far_mine, far_pair, rest_mine,
                 rest_pair, even_in, odd_in, even_out, odd_out):
    chip = ints_ref[ME] // 2
    far = far_chip(chip, chips)
    for parity in (0, 1):
        one_way = (chips - t + chip, chip > 0, (odd_in, even_in)[parity],
                   (even_out, odd_out)[parity])
        other_way = (t - chips + chip, chip < chips - 1, (even_in, odd_in)[parity],
                     (odd_out, even_out)[parity])
        for unit, fed, carried, out in (one_way, other_way):
            unit = jnp.clip(unit, 0, chips - 1)

            @pl.when((chip % 2 == parity) & (unit == far))
            def _():
                rows = pl.ds(piece * blocks, blocks)
                more = jnp.where(fed, carried[...].astype(F32), 0.0)
                out[...] = (far_mine[rows] + far_pair[rows].astype(F32) + more).astype(BF16)

            @pl.when((chip % 2 == parity) & (unit != far))
            def _():
                unit_at = unit - (far == 0).astype(jnp.int32)
                rows = pl.ds(unit_at * owned + piece * blocks, blocks)
                more = jnp.where(fed, carried[...].astype(F32), 0.0)
                out[...] = (rest_mine[rows] + rest_pair[rows].astype(F32) + more).astype(BF16)


def combine_kernel(chips, owned, piece, ints_ref, rest_mine, rest_pair, even_ref,
                   odd_ref, idf_ref, gram_in, sketch_ref, weight_ref, gram_ref):
    blocks = sketch_ref.shape[0]
    chip = ints_ref[ME] // 2
    unit_at = chip - (far_chip(chip, chips) == 0).astype(jnp.int32)
    inner = (chip > 0) & (chip < chips - 1)
    gram = gram_in[...]
    for b in range(blocks):
        at = unit_at * owned + piece * blocks + b
        total = (rest_mine[at] + rest_pair[at].astype(F32) + even_ref[b].astype(F32)
                 + jnp.where(inner, odd_ref[b].astype(F32), 0.0))
        row = idf_ref[pl.ds(piece * blocks + b, 1), :]
        scale = jnp.transpose(jnp.broadcast_to(row, total.shape[::-1]))
        sk = total * scale
        sketch_ref[b] = sk
        weight_ref[b] = jnp.transpose(sk * scale).astype(BF16)
        gram += lax.dot_general(sk, sk, (((0,), (0,)), ((), ())), precision=HIGHEST,
                                preferred_element_type=F32)
    gram_ref[...] = gram


def factor_kernel(total_terms, begin, end, *refs):
    x_ref = refs[-1]
    n = x_ref.shape[0]
    if begin == 0:
        x_ref[...] = refs[0][...] * (1.0 / total_terms)
    else:
        x_ref[...] = refs[0][...]
    rows = lax.broadcasted_iota(jnp.int32, (n, n), 0)
    columns = lax.broadcasted_iota(jnp.int32, (n, n), 1)

    lane = lax.broadcasted_iota(jnp.int32, (8, n), 1)

    def pick(values, at):
        return jnp.take_along_axis(values, jnp.full(values.shape, at, jnp.int32), axis=1)

    def eliminate(trip, carry):
        j = trip * WIDE
        x = x_ref[...]
        row = [jnp.broadcast_to(x_ref[pl.ds(j + k, 1), :], (8, n)) for k in range(WIDE)]
        column = [pick(x, j + k) for k in range(WIDE)]
        scaled = []
        for k in range(WIDE):
            here = lane == j + k
            scaled.append(jnp.where(here, 1.0, row[k]) / pick(row[k], j + k))
            for m in range(k + 1, WIDE):
                entry = pick(row[m], j + k)
                row[m] = jnp.where(here, 0.0, row[m]) - entry * scaled[k]
                column[m] = column[m] - column[k] * pick(scaled[k], j + m)[:1]
        below = rows >= j + WIDE
        x = jnp.where((columns >= j) & (columns < j + WIDE) & below, 0.0, x)
        for k in range(WIDE):
            passed = (lane > j + k) & (lane < j + WIDE)
            step = jnp.where(passed, 0.0, scaled[k])[:1]
            x = x - jnp.where(below, column[k], 0.0) * step
        x_ref[...] = x
        for k in range(WIDE):
            x_ref[pl.ds(j + k, 1), :] = row[k][:1]
        return carry

    lax.fori_loop(begin // WIDE, end // WIDE, eliminate, jnp.int32(0))
    if end == n:
        x = x_ref[...]
        pivots = jnp.sum(jnp.where(rows == columns, x, 0.0), axis=1, keepdims=True)
        lower = jnp.where(rows > columns, x, jnp.where(rows == columns, 1.0, 0.0))
        x_ref[...] = lower * lax.rsqrt(pivots)


def basis_kernel(inverse_ref, *rest):
    pieces, q_ref = rest[:-1], rest[-1]
    at = 0
    for piece in pieces:
        for b in range(piece.shape[0]):
            q_ref[at] = lax.dot_general(piece[b], inverse_ref[...], (((1,), (1,)), ((), ())),
                                        precision=HIGHEST, preferred_element_type=F32)
            at += 1


def project_kernel(last, chips, owned, away, ints_ref, lists_ref, tiles_ref, *rest):
    sources, rest = rest[:len(away)], rest[len(away):]
    before, outs = (rest[:1], rest[1:-4]) if last else ((), rest[:-4])
    doc_ref, weights_ref, buf_ref, sems = rest[-4:]
    strips, tpi, edge = buf_ref.shape[:3]
    ints = Ints(ints_ref, strips, tpi)
    chip, core = ints.me() // 2, ints.me() % 2
    at_end = abs(far_chip(chip, chips) - chip) == chips - 1
    picked = Picked(lists_ref, strips, at_end if last else jnp.logical_not(at_end), not last)
    picked.fetch(tiles_ref, buf_ref, sems)
    doc_ref[...] = before[0][...] if last else jnp.zeros_like(doc_ref)
    for source, (hops, other, piece) in zip(sources, away):
        there = chip + jnp.where(chip % 2 == 0, hops, -hops)
        size = source.shape[0]

        @pl.when((there >= 0) & (there < chips))
        def _():
            owner = there * 2 + (core if other == 0 else 1 - core)
            weights_ref[pl.ds(owner * owned + piece * size, size)] = source[...]

    def work(strip, at, valid):
        left = weights_ref[ints.group(strip) * owned + ints.slot(strip)]
        right = jnp.concatenate([buf_ref[at, j] for j in range(tpi)], axis=1)
        out = jnp.dot(left, right, preferred_element_type=F32) * valid
        for j in range(tpi):
            doc_ref[ints.column(strip, j)] += out[:, j * edge:(j + 1) * edge]

    picked.in_batches(tiles_ref, buf_ref, sems, work)
    if not last:
        outs[0][...] = doc_ref[...]
    else:
        n_dev, held = len(outs), outs[0].shape[0]
        for s in range(n_dev):
            at = partner_of(n_dev, ints.band(), s) * held
            outs[s][...] = doc_ref[pl.ds(at, held)].astype(outs[s].dtype)


def project(last, scalars, tiles, sources, away, before, chips, owned, n_dev, held):
    strips, tpi, edge, _ = tiles.shape
    cols = sources[0].shape[1]
    if last:
        out_shape = [pltpu.VMEM((held, cols, edge), BF16 if s else F32) for s in range(n_dev)]
    else:
        out_shape = [pltpu.VMEM((n_dev * held, cols, edge), F32)]
    more = [near(before)] if last else []
    return pl.pallas_call(
        functools.partial(project_kernel, last, chips, owned, away),
        out_shape=out_shape,
        in_specs=[SM] * 2 + [HB] + [VM] * (len(sources) + len(more)),
        out_specs=[VM] * len(out_shape),
        scratch_shapes=[
            pltpu.VMEM((n_dev * held, cols, edge), F32),
            pltpu.VMEM((2 * chips * owned, cols, edge), BF16),
            pltpu.VMEM((strips, tpi, edge, edge), BF16),
            pltpu.SemaphoreType.DMA((strips,)),
        ],
        compiler_params=params(28),
        cost_estimate=cost(strips // 4 if last else strips),
        name="project_last" if last else "project",
    )(*scalars, far_off(tiles), *[near(s) for s in sources], *more)


def finish_kernel(inverse_ref, own_ref, *rest):
    arrived, out_ref = rest[:-1], rest[-1]
    blocks, _, edge = own_ref.shape
    for b in range(blocks):
        total = own_ref[b]
        for r in arrived:
            total += r[b].astype(F32)
        out_ref[:, b * edge:(b + 1) * edge] = jnp.dot(
            inverse_ref[...], total, precision=HIGHEST, preferred_element_type=F32).astype(BF16)


def on_chip(kernel, out_shape, *args, in_specs=None, scratch=(), mib=8):
    specs = in_specs or [VM] * len(args)
    return pl.pallas_call(
        kernel, out_shape=out_shape, in_specs=specs,
        out_specs=jax.tree.map(lambda _: VM, out_shape,
                               is_leaf=lambda x: not isinstance(x, (tuple, list))),
        scratch_shapes=list(scratch), compiler_params=params(mib),
    )(*[near(a) if s is VM else a for a, s in zip(args, specs)])


def partner_of(n, me, s, back=False):
    if n & (n - 1) == 0:
        return me ^ s
    return (me + (n - s if back else s)) % n


def partners(n, s):
    return [(i, partner_of(n, i, s)) for i in range(n)]


def exchanges(x, axis, n, least=1):
    s, terms = least, [x]
    while s < n:
        x = functools.reduce(jnp.add, terms)
        width = min(4, n // s)
        span = s * width
        terms = [x] + [lax.ppermute(x, axis, [(i, i // span * span + (i + k * s) % span)
                                              for i in range(n)]) for k in range(1, width)]
        s = span
    return terms


def on_device(tiles, tile_col, strip_group, strip_slot, live_count, omega, idf):
    n_group = lax.axis_size("group")
    n_dev = lax.axis_size("dev")
    chips = n_group // 2
    edge = tiles.shape[2]
    cols = omega.shape[1]
    owned = idf.shape[0] // edge
    pieces = 2 if owned % 2 == 0 else 1
    blocks = owned // pieces
    me, band = lax.axis_index("group"), lax.axis_index("dev")
    strips, tpi = tile_col.shape
    ints = jnp.concatenate([me[None], band[None], live_count, strip_group, strip_slot]
                           + [tile_col[:, j] for j in range(tpi)]).astype(jnp.int32)
    lists = pl.pallas_call(
        functools.partial(lists_kernel, strips, tpi, chips),
        out_shape=jax.ShapeDtypeStruct((strips + 2,), jnp.int32), in_specs=[SM], out_specs=SM,
        name="lists")(ints)
    ints, lists = far_off(ints), far_off(lists)
    scalars = (ints, lists)
    swap_links = [(i, i ^ 1) for i in range(n_group)]

    def swap(x):
        return lax.ppermute(x, "group", swap_links)

    even_links = [(2 * c + k, 2 * (c ^ 1) + k) for c in range(chips) for k in (0, 1)]
    odd_links = []
    for c in range(chips):
        to = c + 1 if c % 2 else c - 1
        for k in (0, 1):
            odd_links.append((2 * c + k, 2 * to + k if 0 <= to < chips else 2 * c + 1 - k))

    def over(x, links):
        return lax.ppermute(x, "group", links)

    col_own = omega.shape[0] // edge
    own_omega = omega.reshape(col_own, edge, cols)
    omegas = [own_omega] + [lax.ppermute(own_omega, "dev", partners(n_dev, s))
                            for s in range(1, n_dev)]

    far_mine, far_theirs = partial_sketch(True, scalars, tiles, omegas, chips, owned)
    far_pair = swap(far_theirs)
    piece_shape = pltpu.VMEM((blocks, edge, cols), BF16)
    first = [on_chip(functools.partial(first_kernel, blocks, p), piece_shape,
                     far_mine, far_pair) for p in range(pieces)]
    evens = [over(x, even_links) for x in first]
    odds = list(evens)
    rest_mine, rest_theirs = partial_sketch(False, scalars, tiles, omegas, chips, owned, first)
    rest_pair = swap(rest_theirs)
    for t in range(2, chips):
        for p in range(pieces):
            to_even, to_odd = on_chip(
                functools.partial(relay_kernel, t, chips, owned, blocks, p),
                (piece_shape, piece_shape), ints, far_mine, far_pair, rest_mine,
                rest_pair, evens[p], odds[p], in_specs=[SM] + [VM] * 6)
            evens[p] = over(to_even, even_links)
            odds[p] = over(to_odd, odd_links)

    gram = jnp.zeros((cols, cols), F32)
    sketches, weights = [], []
    for p in range(pieces):
        sk, w, gram = on_chip(
            functools.partial(combine_kernel, chips, owned, p),
            (pltpu.VMEM((blocks, edge, cols), F32), pltpu.VMEM((blocks, cols, edge), BF16),
             pltpu.VMEM((cols, cols), F32)),
            ints, rest_mine, rest_pair, evens[p], odds[p],
            idf.reshape(owned, edge), gram, in_specs=[SM] + [VM] * 6)
        sketches.append(sk)
        weights.append(w)

    evens, odds = list(weights), list(weights)
    sources, away = [], []
    for p in range(pieces):
        sources += [weights[p], swap(weights[p])]
        away += [(0, 0, p), (0, 1, p)]
    for t in range(1, chips):
        if t == chips - 1:
            near_sources, near_away, sources, away = sources, away, [], []
        for p in range(pieces):
            to_even, to_odd = odds[p], evens[p]
            evens[p] = over(to_even, even_links)
            sources += [evens[p], swap(evens[p])]
            away += [(t, 0, p), (t, 1, p)]
            if t < chips - 1:
                odds[p] = over(to_odd, odd_links)
                sources += [odds[p], swap(odds[p])]
                away += [(-t, 0, p), (-t, 1, p)]

    near_chip = 2
    while near_chip < n_group:
        gram = gram + lax.ppermute(gram, "group", partners(n_group, near_chip))
        near_chip *= 2
    gram = functools.reduce(jnp.add, exchanges(gram, "dev", n_dev))
    gram = gram + swap(gram)
    square = pltpu.VMEM((cols, cols), F32)
    total = idf.shape[0] * n_group * n_dev
    inverse = on_chip(functools.partial(factor_kernel, total, 0, cols // 2), square,
                      gram)
    inverse = on_chip(functools.partial(factor_kernel, total, cols // 2, cols), square,
                      inverse)
    q_basis = on_chip(basis_kernel, jax.ShapeDtypeStruct((owned, edge, cols), F32),
                      inverse, *sketches).reshape(owned * edge, cols)

    docs = project(False, scalars, tiles, near_sources, near_away, None, chips, owned, n_dev,
                   col_own)[0]
    parts = project(True, scalars, tiles, sources, away, docs, chips, owned, n_dev, col_own)
    arrived = [lax.ppermute(parts[s], "dev", partners(n_dev, s)) for s in range(1, n_dev)]
    doc_factor = on_chip(finish_kernel, jax.ShapeDtypeStruct((cols, col_own * edge), BF16),
                         inverse, parts[0], *arrived)
    return (q_basis, doc_factor)


def solution(mesh):
    placed = (
        P(("group", "dev"), None, None, None),
        P(("group", "dev"), None),
        P(("group", "dev")),
        P(("group", "dev")),
        P(("group", "dev")),
        P(("group", "dev"), None),
        P(("group", "dev")),
    )

    return jax.shard_map(
        on_device,
        mesh=mesh,
        in_specs=placed,
        out_specs=(P(("group", "dev"), None), P(None, ("group", "dev"))),
        check_vma=False,
    )
```

time: 163 us -> 153 us (0.939)
  starting transfers between devices: 77.3 us -> 42.7 us
  waiting for transfers between devices: 35.4 us -> 61.3 us
    ppermute x45 -> x40, starting transfers between devices: 69.2 us -> 33.6 us  [the longest x20 23.9 us: over(): return lax.ppermute(x, 'group', links)]
    ppermute x45 -> x40, waiting for transfers between devices: 30.5 us -> 60 us  [the longest x20 53.1 us: over(): return lax.ppermute(x, 'group', links)]
    ppermute x3, waiting for transfers between devices: 4.94 us -> 1.32 us  [on_device(): lax.ppermute(own_omega, 'dev', partners(n_dev, s))]
    pallas_call x0 -> x1, Pallas kernels: none -> 2.25 us  [on_device(): pl.pallas_call(functools.partial(lists_kernel, strips, tpi, chips), out_s...]
    unnamed x11 -> x2, local copies, waits for them, and re-layouts: 2.1 us -> 0.01 us
    pallas_call x11 -> x12, Pallas kernels: 22.1 us -> 21.6 us  [on_chip(): pl.pallas_call(kernel, out_shape=out_shape, in_specs=specs, out_specs=jax...]
  transfers between devices with their start and end apart: 51 -> 46, of which waited for: 15 -> 16; matrix products, arithmetic and copies ran while one was open for 1% -> 1% of each run, Pallas kernels for 19% -> 21%
where the time goes in v3:
time: 153 us
  waiting for transfers between devices  61.3 us (40%)
  Pallas kernels  44.9 us (29%)
  starting transfers between devices  42.7 us (28%)
  local copies, waits for them, and re-layouts  2.22 us (1%)
    ppermute x20, waiting for transfers between devices, over(): return lax.ppermute(x, 'group', links)  53.1 us
    ppermute x20, starting transfers between devices, over(): return lax.ppermute(x, 'group', links)  23.9 us
    pallas_call x12, Pallas kernels, on_chip(): pl.pallas_call(kernel, out_shape=out_shape, in_specs=specs, out_specs=jax...  21.6 us
    pallas_call x2, Pallas kernels, project(): pl.pallas_call(functools.partial(project_kernel, last, chips, owned, away...  10.6 us
    pallas_call x2, Pallas kernels, partial_sketch(): pl.pallas_call(functools.partial(sketch_kernel, far_only, chips, owned, l...  10.5 us
    ppermute x3, starting transfers between devices, on_device(): lax.ppermute(own_omega, 'dev', partners(n_dev, s))  4.57 us
    ppermute x3, starting transfers between devices, on_device(): lax.ppermute(parts[s], 'dev', partners(n_dev, s))  4.54 us
    ppermute x2, waiting for transfers between devices, on_device(): gram = gram + lax.ppermute(gram, 'group', partners(n_group, near_chip))  3.68 us
  transfers between devices with their start and end apart: 46, of which 16 were waited for; matrix products, arithmetic and copies ran while one was open for 1% of the time, Pallas kernels for 21%

profile of v3, /device:TPU:0, one launch (start us, length us, event | category | flops | bytes accessed | tf_op | source)
XLA Modules:
  0.0 152.7 jit_solution(8924149164457244691)
XLA Ops:
  0.6 3.0 %collective-permute-start = (bf16[4,128,128]{2,1,0:T(8,128)(2,1)}, bf16[4,128,128]{2,1,0:T(8,128)(2,1)S(1)}, u32[]{:S(2)}, u32[]{:S(2)}) collective-permute-start(bf16[4,128,128]{2,1,0:T(8,128)(2,1)} %bitcast.18), channel_id=1, source_target_pairs={{0,1},{1,0},{2,3},{3,2},{4,5},{5,4},{6,7},{7,6},{8,9},{9,8},{10,11... | collective-permute-start | bytes 393224 | tf_op jit(solution)/shard_map/ppermute | solution.py:420
  3.7 1.5 collective-permute-start.1
  5.9 0.9 slice_bitcast_fusion
  6.7 1.3 concatenate.3.ints_ref
  8.1 2.2 %lists.1.lists_ref = s32[74]{0:T(128)} custom-call(s32[507]{0:T(512)} %concatenate.3.ints_ref), custom_call_target="tpu_custom_call" | custom-call | tf_op jit(solution)/shard_map/lists/pallas_call | solution.py:397
  10.3 1.3 collective-permute-done.1.rest_2_
  11.7 4.0 %sketch_far.1 = (f32[32,128,128]{2,1,0:T(8,128)S(1)}, bf16[16,128,128]{2,1,0:T(8,128)(2,1)S(1)}) custom-call(s32[507]{0:T(512)} %concatenate.3.ints_ref, s32[74]{0:T(128)} %lists.1.lists_ref, bf16[72,5,128,128]{3,2,1,0:T(8,128)(2,1)} %tiles_ref.7, bf16[4,128,128]{2,1,0:T(8,128)(2,1)} %bitcast.21, bf16[4,128,128]{2,1,0:T(8,128)(2,1)S(1)} %collective-permute-done.rest_1_, ...), custom_call_target="tpu_custom_call" | custom-call | flops 4831838208 | bytes 9437184 | tf_op jit(solution)/shard_map/sketch_far/pallas_call | solution.py:152
  15.7 1.9 %collective-permute-done.3.pair_ref.far_pair = bf16[16,128,128]{2,1,0:T(8,128)(2,1)S(1)} collective-permute-done((bf16[16,128,128]{2,1,0:T(8,128)(2,1)S(1)}, bf16[16,128,128]{2,1,0:T(8,128)(2,1)S(1)}, u32[]{:S(2)}, u32[]{:S(2)}) %collective-permute-start.3) | collective-permute-done | bytes 524320 | tf_op jit(solution)/shard_map/ppermute | solution.py:406
  17.7 6.5 %sketch_rest.1 = (f32[96,128,128]{2,1,0:T(8,128)S(1)}, bf16[48,128,128]{2,1,0:T(8,128)(2,1)S(1)}) custom-call(s32[507]{0:T(512)} %concatenate.3.ints_ref, s32[74]{0:T(128)} %lists.1.lists_ref, bf16[72,5,128,128]{3,2,1,0:T(8,128)(2,1)} %tiles_ref.7, bf16[4,128,128]{2,1,0:T(8,128)(2,1)} %bitcast.22, bf16[4,128,128]{2,1,0:T(8,128)(2,1)S(1)} %collective-permute-done.rest_1_, ...), custom_call_target="tpu_custom_call" | custom-call | flops 19327352832 | bytes 37748736 | tf_op jit(solution)/shard_map/sketch_rest/pallas_call | solution.py:152
  24.2 1.2 collective-permute-start.4
  26.0 1.5 collective-permute-start.5
  27.5 7.2 %collective-permute-done.10.even_in.odd_in = bf16[8,128,128]{2,1,0:T(8,128)(2,1)S(1)} collective-permute-done((bf16[8,128,128]{2,1,0:T(8,128)(2,1)S(1)}, bf16[8,128,128]{2,1,0:T(8,128)(2,1)S(1)}, u32[]{:S(2)}, u32[]{:S(2)}) %collective-permute-start.10) | collective-permute-done | bytes 262176 | tf_op jit(solution)/shard_map/ppermute | solution.py:416
  34.6 0.9 shard_map.90
  35.6 0.6 collective-permute-start.11
  36.2 4.1 %collective-permute-done.5.even_in.odd_in = bf16[8,128,128]{2,1,0:T(8,128)(2,1)S(1)} collective-permute-done((bf16[8,128,128]{2,1,0:T(8,128)(2,1)S(1)}, bf16[8,128,128]{2,1,0:T(8,128)(2,1)S(1)}, u32[]{:S(2)}, u32[]{:S(2)}) %collective-permute-start.5) | collective-permute-done | bytes 262176 | tf_op jit(solution)/shard_map/ppermute | solution.py:416
  40.2 0.9 shard_map.88
  41.8 4.1 %collective-permute-done.11.even_in = bf16[8,128,128]{2,1,0:T(8,128)(2,1)S(1)} collective-permute-done((bf16[8,128,128]{2,1,0:T(8,128)(2,1)S(1)}, bf16[8,128,128]{2,1,0:T(8,128)(2,1)S(1)}, u32[]{:S(2)}, u32[]{:S(2)}) %collective-permute-start.11) | collective-permute-done | bytes 262176 | tf_op jit(solution)/shard_map/ppermute | solution.py:416
  45.9 0.9 shard_map.91
  46.8 0.6 collective-permute-start.13
  47.4 4.1 %collective-permute-done.6.even_in = bf16[8,128,128]{2,1,0:T(8,128)(2,1)S(1)} collective-permute-done((bf16[8,128,128]{2,1,0:T(8,128)(2,1)S(1)}, bf16[8,128,128]{2,1,0:T(8,128)(2,1)S(1)}, u32[]{:S(2)}, u32[]{:S(2)}) %collective-permute-start.6) | collective-permute-done | bytes 262176 | tf_op jit(solution)/shard_map/ppermute | solution.py:416
  51.5 1.0 shard_map.89
  52.4 0.6 collective-permute-start.8
  53.0 4.0 %collective-permute-done.13.even_ref = bf16[8,128,128]{2,1,0:T(8,128)(2,1)S(1)} collective-permute-done((bf16[8,128,128]{2,1,0:T(8,128)(2,1)S(1)}, bf16[8,128,128]{2,1,0:T(8,128)(2,1)S(1)}, u32[]{:S(2)}, u32[]{:S(2)}) %collective-permute-start.13) | collective-permute-done | bytes 262176 | tf_op jit(solution)/shard_map/ppermute | solution.py:416
  57.1 1.5 shard_map.92
  58.6 3.2 %collective-permute-done.8.even_ref = bf16[8,128,128]{2,1,0:T(8,128)(2,1)S(1)} collective-permute-done((bf16[8,128,128]{2,1,0:T(8,128)(2,1)S(1)}, bf16[8,128,128]{2,1,0:T(8,128)(2,1)S(1)}, u32[]{:S(2)}, u32[]{:S(2)}) %collective-permute-start.8) | collective-permute-done | bytes 262176 | tf_op jit(solution)/shard_map/ppermute | solution.py:416
  61.8 1.5 shard_map.93
  63.3 0.7 collective-permute-start.15
  63.9 3.7 %collective-permute-done.15 = f32[128,128]{1,0:T(8,128)S(1)} collective-permute-done((f32[128,128]{1,0:T(8,128)S(1)}, f32[128,128]{1,0:T(8,128)S(1)}, u32[]{:S(2)}, u32[]{:S(2)}) %collective-permute-start.15) | collective-permute-done | bytes 65568 | tf_op jit(solution)/shard_map/ppermute | solution.py:473
  67.6 2.8 %collective-permute-start.16 = (f32[128,128]{1,0:T(8,128)S(1)}, f32[128,128]{1,0:T(8,128)S(1)}, u32[]{:S(2)}, u32[]{:S(2)}) collective-permute-start(f32[128,128]{1,0:T(8,128)S(1)} %add.18), channel_id=1, source_target_pairs={{0,16},{4,20},{8,24},{12,28},{16,0},{20,4},{24,8},{28,12},{1,17},{... | collective-permute-start | bytes 196616 | tf_op jit(solution)/shard_map/ppermute | solution.py:473
  70.4 1.7 %collective-permute-start.21 = (bf16[8,128,128]{2,1,0:T(8,128)(2,1)S(1)}, bf16[8,128,128]{2,1,0:T(8,128)(2,1)S(1)}, u32[]{:S(2)}, u32[]{:S(2)}) collective-permute-start(bf16[8,128,128]{2,1,0:T(8,128)(2,1)S(1)} %get-tuple-element.40.rest_0_), channel_id=1, source_target_pairs={{0,8},{4,12},{8,0},{12,4},{16,24},{20,28},{24,16},{28,20},{1,9},{5... | collective-permute-start | bytes 786440 | tf_op jit(solution)/shard_map/ppermute | solution.py:416
  73.0 6.6 %collective-permute-done.21.rest_4_ = bf16[8,128,128]{2,1,0:T(8,128)(2,1)S(1)} collective-permute-done((bf16[8,128,128]{2,1,0:T(8,128)(2,1)S(1)}, bf16[8,128,128]{2,1,0:T(8,128)(2,1)S(1)}, u32[]{:S(2)}, u32[]{:S(2)}) %collective-permute-start.21) | collective-permute-done | bytes 262176 | tf_op jit(solution)/shard_map/ppermute | solution.py:416
  79.6 3.8 %collective-permute-done.25.rest_8_ = bf16[8,128,128]{2,1,0:T(8,128)(2,1)S(1)} collective-permute-done((bf16[8,128,128]{2,1,0:T(8,128)(2,1)S(1)}, bf16[8,128,128]{2,1,0:T(8,128)(2,1)S(1)}, u32[]{:S(2)}, u32[]{:S(2)}) %collective-permute-start.25) | collective-permute-done | bytes 262176 | tf_op jit(solution)/shard_map/ppermute | solution.py:416
  84.9 11.2 %collective-permute-start.37 = (bf16[8,128,128]{2,1,0:T(8,128)(2,1)S(1)}, bf16[8,128,128]{2,1,0:T(8,128)(2,1)S(1)}, u32[]{:S(2)}, u32[]{:S(2)}) collective-permute-start(bf16[8,128,128]{2,1,0:T(8,128)(2,1)S(1)} %collective-permute-done.32.rest_6_), channel_id=1, source_target_pairs={{0,8},{4,12},{8,0},{12,4},{16,24},{20,28},{24,16},{28,20},{1,9},{5... | collective-permute-start | bytes 786440 | tf_op jit(solution)/shard_map/ppermute | solution.py:416
  96.2 3.6 %collective-permute-start.40 = (bf16[8,128,128]{2,1,0:T(8,128)(2,1)S(1)}, bf16[8,128,128]{2,1,0:T(8,128)(2,1)S(1)}, u32[]{:S(2)}, u32[]{:S(2)}) collective-permute-start(bf16[8,128,128]{2,1,0:T(8,128)(2,1)S(1)} %collective-permute-done.35.rest_10_), channel_id=1, source_target_pairs={{0,8},{4,12},{8,0},{12,4},{16,24},{20,28},{24,16},{28,20},{1,9},{5... | collective-permute-start | bytes 786440 | tf_op jit(solution)/shard_map/ppermute | solution.py:416
  99.9 1.9 %collective-permute-start.27 = (bf16[8,128,128]{2,1,0:T(8,128)(2,1)S(1)}, bf16[8,128,128]{2,1,0:T(8,128)(2,1)S(1)}, u32[]{:S(2)}, u32[]{:S(2)}) collective-permute-start(bf16[8,128,128]{2,1,0:T(8,128)(2,1)S(1)} %collective-permute-done.26.rest_18_), channel_id=1, source_target_pairs={{0,8},{4,12},{8,0},{12,4},{16,24},{20,28},{24,16},{28,20},{1,9},{5... | collective-permute-start | bytes 786440 | tf_op jit(solution)/shard_map/ppermute | solution.py:416
  102.3 4.6 %collective-permute-done.40.rest_16_ = bf16[8,128,128]{2,1,0:T(8,128)(2,1)S(1)} collective-permute-done((bf16[8,128,128]{2,1,0:T(8,128)(2,1)S(1)}, bf16[8,128,128]{2,1,0:T(8,128)(2,1)S(1)}, u32[]{:S(2)}, u32[]{:S(2)}) %collective-permute-start.40) | collective-permute-done | bytes 262176 | tf_op jit(solution)/shard_map/ppermute | solution.py:416
  106.9 5.6 %collective-permute-done.23.rest_0_ = bf16[8,128,128]{2,1,0:T(8,128)(2,1)S(1)} collective-permute-done((bf16[8,128,128]{2,1,0:T(8,128)(2,1)S(1)}, bf16[8,128,128]{2,1,0:T(8,128)(2,1)S(1)}, u32[]{:S(2)}, u32[]{:S(2)}) %collective-permute-start.23) | collective-permute-done | bytes 262176 | tf_op jit(solution)/shard_map/ppermute | solution.py:416
  112.6 5.4 %collective-permute-done.27.rest_2_ = bf16[8,128,128]{2,1,0:T(8,128)(2,1)S(1)} collective-permute-done((bf16[8,128,128]{2,1,0:T(8,128)(2,1)S(1)}, bf16[8,128,128]{2,1,0:T(8,128)(2,1)S(1)}, u32[]{:S(2)}, u32[]{:S(2)}) %collective-permute-start.27) | collective-permute-done | bytes 262176 | tf_op jit(solution)/shard_map/ppermute | solution.py:416
  118.0 2.2 %collective-permute-start.19 = (f32[128,128]{1,0:T(8,128)S(1)}, f32[128,128]{1,0:T(8,128)S(1)}, u32[]{:S(2)}, u32[]{:S(2)}) collective-permute-start(f32[128,128]{1,0:T(8,128)S(1)} %add.19), channel_id=1, source_target_pairs={{0,3},{1,0},{2,1},{3,2},{4,7},{5,4},{6,5},{7,6},{8,11},{9,8},{10,9... | collective-permute-start | bytes 196616 | tf_op jit(solution)/shard_map/ppermute | solution.py:378
  121.3 6.4 %project.1.rest_4_ = f32[16,128,128]{2,1,0:T(8,128)S(1)} custom-call(s32[507]{0:T(512)} %concatenate.3.ints_ref, s32[74]{0:T(128)} %lists.1.lists_ref, bf16[72,5,128,128]{3,2,1,0:T(8,128)(2,1)} %tiles_ref.7, bf16[8,128,128]{2,1,0:T(8,128)(2,1)S(1)} %get-tuple-element.40.rest_0_, bf16[8,128,128]{2,1,0:T(8,128)(2,1)S(1)} %collective-permute-done.29.rest_1_, ...), custom_call_target="tpu_custom_call" | custom-call | flops 19327352832 | bytes 37748736 | tf_op jit(solution)/shard_map/project/pallas_call | solution.py:324
  127.8 4.2 %project_last.1 = (f32[4,128,128]{2,1,0:T(8,128)S(1)}, bf16[4,128,128]{2,1,0:T(8,128)(2,1)S(1)}, bf16[4,128,128]{2,1,0:T(8,128)(2,1)S(1)}, bf16[4,128,128]{2,1,0:T(8,128)(2,1)S(1)}) custom-call(s32[507]{0:T(512)} %concatenate.3.ints_ref, s32[74]{0:T(128)} %lists.1.lists_ref, bf16[72,5,128,128]{3,2,1,0:T(8,128)(2,1)} %tiles_ref.7, ...), custom_call_target="tpu_custom_call" | custom-call | flops 4831838208 | bytes 9437184 | tf_op jit(solution)/shard_map/project_last/pallas_call | solution.py:324
  131.9 3.0 %collective-permute-start.43 = (bf16[4,128,128]{2,1,0:T(8,128)(2,1)S(1)}, bf16[4,128,128]{2,1,0:T(8,128)(2,1)S(1)}, u32[]{:S(2)}, u32[]{:S(2)}) collective-permute-start(bf16[4,128,128]{2,1,0:T(8,128)(2,1)S(1)} %get-tuple-element.43), channel_id=1, source_target_pairs={{0,1},{1,0},{2,3},{3,2},{4,5},{5,4},{6,7},{7,6},{8,9},{9,8},{10,11... | collective-permute-start | bytes 393224 | tf_op jit(solution)/shard_map/ppermute | solution.py:489
  134.9 1.5 collective-permute-start.44
  136.6 1.2 collective-permute-done.20
  137.8 5.3 %shard_map.94.refs_0_ = f32[128,128]{1,0:T(8,128)S(1)} custom-call(f32[128,128]{1,0:T(8,128)S(1)} %add.23.refs_0_), custom_call_target="tpu_custom_call" | custom-call | tf_op jit(solution)/shard_map/pallas_call | solution.py:354
  143.1 5.3 %shard_map.95.inverse_ref = f32[128,128]{1,0:T(8,128)S(1)} custom-call(f32[128,128]{1,0:T(8,128)S(1)} %shard_map.94.refs_0_), custom_call_target="tpu_custom_call" | custom-call | tf_op jit(solution)/shard_map/pallas_call | solution.py:354
  148.4 3.2 %shard_map.96 = f32[16,128,128]{2,1,0:T(8,128)} custom-call(f32[128,128]{1,0:T(8,128)S(1)} %shard_map.95.inverse_ref, f32[8,128,128]{2,1,0:T(8,128)S(1)} %get-tuple-element.38.rest_0_, f32[8,128,128]{2,1,0:T(8,128)S(1)} %get-tuple-element.39.rest_1_), custom_call_target="tpu_custom_call" | custom-call | tf_op jit(solution)/shard_map/pallas_call | solution.py:354
  151.7 1.0 shard_map.97
  (70 shorter events, 5.6 us)
Async XLA Ops:
  0.6 9.7 %collective-permute-start = (bf16[4,128,128]{2,1,0:T(8,128)(2,1)}, bf16[4,128,128]{2,1,0:T(8,128)(2,1)S(1)}, u32[]{:S(2)}, u32[]{:S(2)}) collective-permute-start(bf16[4,128,128]{2,1,0:T(8,128)(2,1)} %bitcast.18), channel_id=1, source_target_pairs={{0,1},{1,0},{2,3},{3,2},{4,5},{5,4},{6,7},{7,6},{8,9},{9,8},{10,11... | collective-permute-start | bytes 393224 | tf_op jit(solution)/shard_map/ppermute | solution.py:420
  3.7 8.0 %collective-permute-start.1 = (bf16[4,128,128]{2,1,0:T(8,128)(2,1)}, bf16[4,128,128]{2,1,0:T(8,128)(2,1)S(1)}, u32[]{:S(2)}, u32[]{:S(2)}) collective-permute-start(bf16[4,128,128]{2,1,0:T(8,128)(2,1)} %bitcast.19), channel_id=1, source_target_pairs={{0,2},{1,3},{2,0},{3,1},{4,6},{5,7},{6,4},{7,5},{8,10},{9,11},{10,... | collective-permute-start | bytes 393224 | tf_op jit(solution)/shard_map/ppermute | solution.py:420
  5.2 6.5 %collective-permute-start.2 = (bf16[4,128,128]{2,1,0:T(8,128)(2,1)}, bf16[4,128,128]{2,1,0:T(8,128)(2,1)S(1)}, u32[]{:S(2)}, u32[]{:S(2)}) collective-permute-start(bf16[4,128,128]{2,1,0:T(8,128)(2,1)} %bitcast.20), channel_id=1, source_target_pairs={{0,3},{1,2},{2,1},{3,0},{4,7},{5,6},{6,5},{7,4},{8,11},{9,10},{10,... | collective-permute-start | bytes 393224 | tf_op jit(solution)/shard_map/ppermute | solution.py:420
  15.6 2.0 %collective-permute-start.3 = (bf16[16,128,128]{2,1,0:T(8,128)(2,1)S(1)}, bf16[16,128,128]{2,1,0:T(8,128)(2,1)S(1)}, u32[]{:S(2)}, u32[]{:S(2)}) collective-permute-start(bf16[16,128,128]{2,1,0:T(8,128)(2,1)S(1)} %get-tuple-element.25), channel_id=1, source_target_pairs={{0,4},{4,0},{8,12},{12,8},{16,20},{20,16},{24,28},{28,24},{1,5},{5... | collective-permute-start | bytes 1572872 | tf_op jit(solution)/shard_map/ppermute | solution.py:406
  24.2 10.4 %collective-permute-start.4 = (bf16[48,128,128]{2,1,0:T(8,128)(2,1)S(1)}, bf16[48,128,128]{2,1,0:T(8,128)(2,1)S(1)}, u32[]{:S(2)}, u32[]{:S(2)}) collective-permute-start(bf16[48,128,128]{2,1,0:T(8,128)(2,1)S(1)} %get-tuple-element.27), channel_id=1, source_target_pairs={{0,4},{4,0},{8,12},{12,8},{16,20},{20,16},{24,28},{28,24},{1,5},{5... | collective-permute-start | bytes 4718600 | tf_op jit(solution)/shard_map/ppermute | solution.py:406
  25.4 9.2 %collective-permute-start.10 = (bf16[8,128,128]{2,1,0:T(8,128)(2,1)S(1)}, bf16[8,128,128]{2,1,0:T(8,128)(2,1)S(1)}, u32[]{:S(2)}, u32[]{:S(2)}) collective-permute-start(bf16[8,128,128]{2,1,0:T(8,128)(2,1)S(1)} %shard_map.86.rest_4_), channel_id=1, source_target_pairs={{0,8},{4,12},{8,0},{12,4},{16,24},{20,28},{24,16},{28,20},{1,9},{5... | collective-permute-start | bytes 786440 | tf_op jit(solution)/shard_map/ppermute | solution.py:416
  26.0 14.3 %collective-permute-start.5 = (bf16[8,128,128]{2,1,0:T(8,128)(2,1)S(1)}, bf16[8,128,128]{2,1,0:T(8,128)(2,1)S(1)}, u32[]{:S(2)}, u32[]{:S(2)}) collective-permute-start(bf16[8,128,128]{2,1,0:T(8,128)(2,1)S(1)} %shard_map.87.rest_5_), channel_id=1, source_target_pairs={{0,8},{4,12},{8,0},{12,4},{16,24},{20,28},{24,16},{28,20},{1,9},{5... | collective-permute-start | bytes 786440 | tf_op jit(solution)/shard_map/ppermute | solution.py:416
  35.6 10.3 %collective-permute-start.11 = (bf16[8,128,128]{2,1,0:T(8,128)(2,1)S(1)}, bf16[8,128,128]{2,1,0:T(8,128)(2,1)S(1)}, u32[]{:S(2)}, u32[]{:S(2)}) collective-permute-start(bf16[8,128,128]{2,1,0:T(8,128)(2,1)S(1)} %get-tuple-element.32), channel_id=1, source_target_pairs={{0,8},{4,12},{8,0},{12,4},{16,24},{20,28},{24,16},{28,20},{1,9},{5... | collective-permute-start | bytes 786440 | tf_op jit(solution)/shard_map/ppermute | solution.py:416
  36.2 9.7 %collective-permute-start.12 = (bf16[8,128,128]{2,1,0:T(8,128)(2,1)S(1)}, bf16[8,128,128]{2,1,0:T(8,128)(2,1)S(1)}, u32[]{:S(2)}, u32[]{:S(2)}) collective-permute-start(bf16[8,128,128]{2,1,0:T(8,128)(2,1)S(1)} %get-tuple-element.33), channel_id=1, source_target_pairs={{0,4},{4,0},{8,16},{12,20},{16,8},{20,12},{24,28},{28,24},{1,5},{5... | collective-permute-start | bytes 786440 | tf_op jit(solution)/shard_map/ppermute | solution.py:416
  41.2 10.3 %collective-permute-start.6 = (bf16[8,128,128]{2,1,0:T(8,128)(2,1)S(1)}, bf16[8,128,128]{2,1,0:T(8,128)(2,1)S(1)}, u32[]{:S(2)}, u32[]{:S(2)}) collective-permute-start(bf16[8,128,128]{2,1,0:T(8,128)(2,1)S(1)} %get-tuple-element.28), channel_id=1, source_target_pairs={{0,8},{4,12},{8,0},{12,4},{16,24},{20,28},{24,16},{28,20},{1,9},{5... | collective-permute-start | bytes 786440 | tf_op jit(solution)/shard_map/ppermute | solution.py:416
  41.8 9.7 %collective-permute-start.7 = (bf16[8,128,128]{2,1,0:T(8,128)(2,1)S(1)}, bf16[8,128,128]{2,1,0:T(8,128)(2,1)S(1)}, u32[]{:S(2)}, u32[]{:S(2)}) collective-permute-start(bf16[8,128,128]{2,1,0:T(8,128)(2,1)S(1)} %get-tuple-element.29), channel_id=1, source_target_pairs={{0,4},{4,0},{8,16},{12,20},{16,8},{20,12},{24,28},{28,24},{1,5},{5... | collective-permute-start | bytes 786440 | tf_op jit(solution)/shard_map/ppermute | solution.py:416
  46.8 10.3 %collective-permute-start.13 = (bf16[8,128,128]{2,1,0:T(8,128)(2,1)S(1)}, bf16[8,128,128]{2,1,0:T(8,128)(2,1)S(1)}, u32[]{:S(2)}, u32[]{:S(2)}) collective-permute-start(bf16[8,128,128]{2,1,0:T(8,128)(2,1)S(1)} %get-tuple-element.34), channel_id=1, source_target_pairs={{0,8},{4,12},{8,0},{12,4},{16,24},{20,28},{24,16},{28,20},{1,9},{5... | collective-permute-start | bytes 786440 | tf_op jit(solution)/shard_map/ppermute | solution.py:416
  47.4 9.7 %copy-start = (f32[2048]{0:T(1024)S(1)}, f32[2048]{0:T(1024)}, u32[]{:S(2)}) copy-start(f32[2048]{0:T(1024)} %param.13) | copy-start | bytes 24580
  47.4 9.7 %collective-permute-start.14 = (bf16[8,128,128]{2,1,0:T(8,128)(2,1)S(1)}, bf16[8,128,128]{2,1,0:T(8,128)(2,1)S(1)}, u32[]{:S(2)}, u32[]{:S(2)}) collective-permute-start(bf16[8,128,128]{2,1,0:T(8,128)(2,1)S(1)} %get-tuple-element.35), channel_id=1, source_target_pairs={{0,4},{4,0},{8,16},{12,20},{16,8},{20,12},{24,28},{28,24},{1,5},{5... | collective-permute-start | bytes 786440 | tf_op jit(solution)/shard_map/ppermute | solution.py:416
  52.4 9.4 %collective-permute-start.8 = (bf16[8,128,128]{2,1,0:T(8,128)(2,1)S(1)}, bf16[8,128,128]{2,1,0:T(8,128)(2,1)S(1)}, u32[]{:S(2)}, u32[]{:S(2)}) collective-permute-start(bf16[8,128,128]{2,1,0:T(8,128)(2,1)S(1)} %get-tuple-element.30), channel_id=1, source_target_pairs={{0,8},{4,12},{8,0},{12,4},{16,24},{20,28},{24,16},{28,20},{1,9},{5... | collective-permute-start | bytes 786440 | tf_op jit(solution)/shard_map/ppermute | solution.py:416
  53.0 8.8 %collective-permute-start.9 = (bf16[8,128,128]{2,1,0:T(8,128)(2,1)S(1)}, bf16[8,128,128]{2,1,0:T(8,128)(2,1)S(1)}, u32[]{:S(2)}, u32[]{:S(2)}) collective-permute-start(bf16[8,128,128]{2,1,0:T(8,128)(2,1)S(1)} %get-tuple-element.31), channel_id=1, source_target_pairs={{0,4},{4,0},{8,16},{12,20},{16,8},{20,12},{24,28},{28,24},{1,5},{5... | collective-permute-start | bytes 786440 | tf_op jit(solution)/shard_map/ppermute | solution.py:416
  63.3 4.3 %collective-permute-start.15 = (f32[128,128]{1,0:T(8,128)S(1)}, f32[128,128]{1,0:T(8,128)S(1)}, u32[]{:S(2)}, u32[]{:S(2)}) collective-permute-start(f32[128,128]{1,0:T(8,128)S(1)} %get-tuple-element.37), channel_id=1, source_target_pairs={{0,8},{4,12},{8,0},{12,4},{16,24},{20,28},{24,16},{28,20},{1,9},{5... | collective-permute-start | bytes 196616 | tf_op jit(solution)/shard_map/ppermute | solution.py:473
  67.6 5.3 %collective-permute-start.16 = (f32[128,128]{1,0:T(8,128)S(1)}, f32[128,128]{1,0:T(8,128)S(1)}, u32[]{:S(2)}, u32[]{:S(2)}) collective-permute-start(f32[128,128]{1,0:T(8,128)S(1)} %add.18), channel_id=1, source_target_pairs={{0,16},{4,20},{8,24},{12,28},{16,0},{20,4},{24,8},{28,12},{1,17},{... | collective-permute-start | bytes 196616 | tf_op jit(solution)/shard_map/ppermute | solution.py:473
  70.4 9.2 %collective-permute-start.21 = (bf16[8,128,128]{2,1,0:T(8,128)(2,1)S(1)}, bf16[8,128,128]{2,1,0:T(8,128)(2,1)S(1)}, u32[]{:S(2)}, u32[]{:S(2)}) collective-permute-start(bf16[8,128,128]{2,1,0:T(8,128)(2,1)S(1)} %get-tuple-element.40.rest_0_), channel_id=1, source_target_pairs={{0,8},{4,12},{8,0},{12,4},{16,24},{20,28},{24,16},{28,20},{1,9},{5... | collective-permute-start | bytes 786440 | tf_op jit(solution)/shard_map/ppermute | solution.py:416
  72.2 11.2 %collective-permute-start.25 = (bf16[8,128,128]{2,1,0:T(8,128)(2,1)S(1)}, bf16[8,128,128]{2,1,0:T(8,128)(2,1)S(1)}, u32[]{:S(2)}, u32[]{:S(2)}) collective-permute-start(bf16[8,128,128]{2,1,0:T(8,128)(2,1)S(1)} %get-tuple-element.41.rest_2_), channel_id=1, source_target_pairs={{0,8},{4,12},{8,0},{12,4},{16,24},{20,28},{24,16},{28,20},{1,9},{5... | collective-permute-start | bytes 786440 | tf_op jit(solution)/shard_map/ppermute | solution.py:416
  72.4 10.9 %collective-permute-start.29 = (bf16[8,128,128]{2,1,0:T(8,128)(2,1)S(1)}, bf16[8,128,128]{2,1,0:T(8,128)(2,1)S(1)}, u32[]{:S(2)}, u32[]{:S(2)}) collective-permute-start(bf16[8,128,128]{2,1,0:T(8,128)(2,1)S(1)} %get-tuple-element.40.rest_0_), channel_id=1, source_target_pairs={{0,4},{4,0},{8,12},{12,8},{16,20},{20,16},{24,28},{28,24},{1,5},{5... | collective-permute-start | bytes 786440 | tf_op jit(solution)/shard_map/ppermute | solution.py:406
  72.5 11.4 %collective-permute-start.30 = (bf16[8,128,128]{2,1,0:T(8,128)(2,1)S(1)}, bf16[8,128,128]{2,1,0:T(8,128)(2,1)S(1)}, u32[]{:S(2)}, u32[]{:S(2)}) collective-permute-start(bf16[8,128,128]{2,1,0:T(8,128)(2,1)S(1)} %get-tuple-element.41.rest_2_), channel_id=1, source_target_pairs={{0,4},{4,0},{8,12},{12,8},{16,20},{20,16},{24,28},{28,24},{1,5},{5... | collective-permute-start | bytes 786440 | tf_op jit(solution)/shard_map/ppermute | solution.py:406
  73.0 11.0 %collective-permute-start.32 = (bf16[8,128,128]{2,1,0:T(8,128)(2,1)S(1)}, bf16[8,128,128]{2,1,0:T(8,128)(2,1)S(1)}, u32[]{:S(2)}, u32[]{:S(2)}) collective-permute-start(bf16[8,128,128]{2,1,0:T(8,128)(2,1)S(1)} %get-tuple-element.40.rest_0_), channel_id=1, source_target_pairs={{0,4},{4,0},{8,16},{12,20},{16,8},{20,12},{24,28},{28,24},{1,5},{5... | collective-permute-start | bytes 786440 | tf_op jit(solution)/shard_map/ppermute | solution.py:416
  79.6 4.8 %collective-permute-start.35 = (bf16[8,128,128]{2,1,0:T(8,128)(2,1)S(1)}, bf16[8,128,128]{2,1,0:T(8,128)(2,1)S(1)}, u32[]{:S(2)}, u32[]{:S(2)}) collective-permute-start(bf16[8,128,128]{2,1,0:T(8,128)(2,1)S(1)} %get-tuple-element.41.rest_2_), channel_id=1, source_target_pairs={{0,4},{4,0},{8,16},{12,20},{16,8},{20,12},{24,28},{28,24},{1,5},{5... | collective-permute-start | bytes 786440 | tf_op jit(solution)/shard_map/ppermute | solution.py:416
  83.4 1.5 %collective-permute-start.22 = (bf16[8,128,128]{2,1,0:T(8,128)(2,1)S(1)}, bf16[8,128,128]{2,1,0:T(8,128)(2,1)S(1)}, u32[]{:S(2)}, u32[]{:S(2)}) collective-permute-start(bf16[8,128,128]{2,1,0:T(8,128)(2,1)S(1)} %collective-permute-done.21.rest_4_), channel_id=1, source_target_pairs={{0,4},{4,0},{8,16},{12,20},{16,8},{20,12},{24,28},{28,24},{1,5},{5... | collective-permute-start | bytes 786440 | tf_op jit(solution)/shard_map/ppermute | solution.py:416
  83.4 12.8 %collective-permute-start.26 = (bf16[8,128,128]{2,1,0:T(8,128)(2,1)S(1)}, bf16[8,128,128]{2,1,0:T(8,128)(2,1)S(1)}, u32[]{:S(2)}, u32[]{:S(2)}) collective-permute-start(bf16[8,128,128]{2,1,0:T(8,128)(2,1)S(1)} %collective-permute-done.25.rest_8_), channel_id=1, source_target_pairs={{0,4},{4,0},{8,16},{12,20},{16,8},{20,12},{24,28},{28,24},{1,5},{5... | collective-permute-start | bytes 786440 | tf_op jit(solution)/shard_map/ppermute | solution.py:416
  83.9 12.3 %collective-permute-start.31 = (bf16[8,128,128]{2,1,0:T(8,128)(2,1)S(1)}, bf16[8,128,128]{2,1,0:T(8,128)(2,1)S(1)}, u32[]{:S(2)}, u32[]{:S(2)}) collective-permute-start(bf16[8,128,128]{2,1,0:T(8,128)(2,1)S(1)} %collective-permute-done.21.rest_4_), channel_id=1, source_target_pairs={{0,4},{4,0},{8,12},{12,8},{16,20},{20,16},{24,28},{28,24},{1,5},{5... | collective-permute-start | bytes 786440 | tf_op jit(solution)/shard_map/ppermute | solution.py:406
  84.0 15.8 %collective-permute-start.33 = (bf16[8,128,128]{2,1,0:T(8,128)(2,1)S(1)}, bf16[8,128,128]{2,1,0:T(8,128)(2,1)S(1)}, u32[]{:S(2)}, u32[]{:S(2)}) collective-permute-start(bf16[8,128,128]{2,1,0:T(8,128)(2,1)S(1)} %collective-permute-done.32.rest_6_), channel_id=1, source_target_pairs={{0,4},{4,0},{8,12},{12,8},{16,20},{20,16},{24,28},{28,24},{1,5},{5... | collective-permute-start | bytes 786440 | tf_op jit(solution)/shard_map/ppermute | solution.py:406
  84.4 15.5 %collective-permute-start.34 = (bf16[8,128,128]{2,1,0:T(8,128)(2,1)S(1)}, bf16[8,128,128]{2,1,0:T(8,128)(2,1)S(1)}, u32[]{:S(2)}, u32[]{:S(2)}) collective-permute-start(bf16[8,128,128]{2,1,0:T(8,128)(2,1)S(1)} %collective-permute-done.25.rest_8_), channel_id=1, source_target_pairs={{0,4},{4,0},{8,12},{12,8},{16,20},{20,16},{24,28},{28,24},{1,5},{5... | collective-permute-start | bytes 786440 | tf_op jit(solution)/shard_map/ppermute | solution.py:406
  84.9 16.9 %collective-permute-start.37 = (bf16[8,128,128]{2,1,0:T(8,128)(2,1)S(1)}, bf16[8,128,128]{2,1,0:T(8,128)(2,1)S(1)}, u32[]{:S(2)}, u32[]{:S(2)}) collective-permute-start(bf16[8,128,128]{2,1,0:T(8,128)(2,1)S(1)} %collective-permute-done.32.rest_6_), channel_id=1, source_target_pairs={{0,8},{4,12},{8,0},{12,4},{16,24},{20,28},{24,16},{28,20},{1,9},{5... | collective-permute-start | bytes 786440 | tf_op jit(solution)/shard_map/ppermute | solution.py:416
  96.1 5.7 %collective-permute-start.36 = (bf16[8,128,128]{2,1,0:T(8,128)(2,1)S(1)}, bf16[8,128,128]{2,1,0:T(8,128)(2,1)S(1)}, u32[]{:S(2)}, u32[]{:S(2)}) collective-permute-start(bf16[8,128,128]{2,1,0:T(8,128)(2,1)S(1)} %collective-permute-done.35.rest_10_), channel_id=1, source_target_pairs={{0,4},{4,0},{8,12},{12,8},{16,20},{20,16},{24,28},{28,24},{1,5},{5... | collective-permute-start | bytes 786440 | tf_op jit(solution)/shard_map/ppermute | solution.py:406
  96.2 10.8 %collective-permute-start.40 = (bf16[8,128,128]{2,1,0:T(8,128)(2,1)S(1)}, bf16[8,128,128]{2,1,0:T(8,128)(2,1)S(1)}, u32[]{:S(2)}, u32[]{:S(2)}) collective-permute-start(bf16[8,128,128]{2,1,0:T(8,128)(2,1)S(1)} %collective-permute-done.35.rest_10_), channel_id=1, source_target_pairs={{0,8},{4,12},{8,0},{12,4},{16,24},{20,28},{24,16},{28,20},{1,9},{5... | collective-permute-start | bytes 786440 | tf_op jit(solution)/shard_map/ppermute | solution.py:416
  99.8 12.8 %collective-permute-start.23 = (bf16[8,128,128]{2,1,0:T(8,128)(2,1)S(1)}, bf16[8,128,128]{2,1,0:T(8,128)(2,1)S(1)}, u32[]{:S(2)}, u32[]{:S(2)}) collective-permute-start(bf16[8,128,128]{2,1,0:T(8,128)(2,1)S(1)} %collective-permute-done.22.rest_14_), channel_id=1, source_target_pairs={{0,8},{4,12},{8,0},{12,4},{16,24},{20,28},{24,16},{28,20},{1,9},{5... | collective-permute-start | bytes 786440 | tf_op jit(solution)/shard_map/ppermute | solution.py:416
  99.9 18.1 %collective-permute-start.27 = (bf16[8,128,128]{2,1,0:T(8,128)(2,1)S(1)}, bf16[8,128,128]{2,1,0:T(8,128)(2,1)S(1)}, u32[]{:S(2)}, u32[]{:S(2)}) collective-permute-start(bf16[8,128,128]{2,1,0:T(8,128)(2,1)S(1)} %collective-permute-done.26.rest_18_), channel_id=1, source_target_pairs={{0,8},{4,12},{8,0},{12,4},{16,24},{20,28},{24,16},{28,20},{1,9},{5... | collective-permute-start | bytes 786440 | tf_op jit(solution)/shard_map/ppermute | solution.py:416
  101.8 18.4 %collective-permute-start.38 = (bf16[8,128,128]{2,1,0:T(8,128)(2,1)S(1)}, bf16[8,128,128]{2,1,0:T(8,128)(2,1)S(1)}, u32[]{:S(2)}, u32[]{:S(2)}) collective-permute-start(bf16[8,128,128]{2,1,0:T(8,128)(2,1)S(1)} %collective-permute-done.37.rest_12_), channel_id=1, source_target_pairs={{0,4},{4,0},{8,12},{12,8},{16,20},{20,16},{24,28},{28,24},{1,5},{5... | collective-permute-start | bytes 786440 | tf_op jit(solution)/shard_map/ppermute | solution.py:406
  101.8 18.4 %collective-permute-start.39 = (bf16[8,128,128]{2,1,0:T(8,128)(2,1)S(1)}, bf16[8,128,128]{2,1,0:T(8,128)(2,1)S(1)}, u32[]{:S(2)}, u32[]{:S(2)}) collective-permute-start(bf16[8,128,128]{2,1,0:T(8,128)(2,1)S(1)} %collective-permute-done.22.rest_14_), channel_id=1, source_target_pairs={{0,4},{4,0},{8,12},{12,8},{16,20},{20,16},{24,28},{28,24},{1,5},{5... | collective-permute-start | bytes 786440 | tf_op jit(solution)/shard_map/ppermute | solution.py:406
  106.9 13.8 %collective-permute-start.41 = (bf16[8,128,128]{2,1,0:T(8,128)(2,1)S(1)}, bf16[8,128,128]{2,1,0:T(8,128)(2,1)S(1)}, u32[]{:S(2)}, u32[]{:S(2)}) collective-permute-start(bf16[8,128,128]{2,1,0:T(8,128)(2,1)S(1)} %collective-permute-done.40.rest_16_), channel_id=1, source_target_pairs={{0,4},{4,0},{8,12},{12,8},{16,20},{20,16},{24,28},{28,24},{1,5},{5... | collective-permute-start | bytes 786440 | tf_op jit(solution)/shard_map/ppermute | solution.py:406
  112.6 8.2 %collective-permute-start.42 = (bf16[8,128,128]{2,1,0:T(8,128)(2,1)S(1)}, bf16[8,128,128]{2,1,0:T(8,128)(2,1)S(1)}, u32[]{:S(2)}, u32[]{:S(2)}) collective-permute-start(bf16[8,128,128]{2,1,0:T(8,128)(2,1)S(1)} %collective-permute-done.26.rest_18_), channel_id=1, source_target_pairs={{0,4},{4,0},{8,12},{12,8},{16,20},{20,16},{24,28},{28,24},{1,5},{5... | collective-permute-start | bytes 786440 | tf_op jit(solution)/shard_map/ppermute | solution.py:406
  118.0 18.4 %collective-permute-start.19 = (f32[128,128]{1,0:T(8,128)S(1)}, f32[128,128]{1,0:T(8,128)S(1)}, u32[]{:S(2)}, u32[]{:S(2)}) collective-permute-start(f32[128,128]{1,0:T(8,128)S(1)} %add.19), channel_id=1, source_target_pairs={{0,3},{1,0},{2,1},{3,2},{4,7},{5,4},{6,5},{7,6},{8,11},{9,8},{10,9... | collective-permute-start | bytes 196616 | tf_op jit(solution)/shard_map/ppermute | solution.py:378
  120.2 16.2 %collective-permute-start.18 = (f32[128,128]{1,0:T(8,128)S(1)}, f32[128,128]{1,0:T(8,128)S(1)}, u32[]{:S(2)}, u32[]{:S(2)}) collective-permute-start(f32[128,128]{1,0:T(8,128)S(1)} %add.19), channel_id=1, source_target_pairs={{0,2},{1,3},{2,0},{3,1},{4,6},{5,7},{6,4},{7,5},{8,10},{9,11},{10,... | collective-permute-start | bytes 196616 | tf_op jit(solution)/shard_map/ppermute | solution.py:378
  120.2 16.2 %collective-permute-start.17 = (f32[128,128]{1,0:T(8,128)S(1)}, f32[128,128]{1,0:T(8,128)S(1)}, u32[]{:S(2)}, u32[]{:S(2)}) collective-permute-start(f32[128,128]{1,0:T(8,128)S(1)} %add.19), channel_id=1, source_target_pairs={{0,1},{1,2},{2,3},{3,0},{4,5},{5,6},{6,7},{7,4},{8,9},{9,10},{10,1... | collective-permute-start | bytes 196616 | tf_op jit(solution)/shard_map/ppermute | solution.py:378
  120.8 6.9 %collective-permute-start.24 = (bf16[8,128,128]{2,1,0:T(8,128)(2,1)S(1)}, bf16[8,128,128]{2,1,0:T(8,128)(2,1)S(1)}, u32[]{:S(2)}, u32[]{:S(2)}) collective-permute-start(bf16[8,128,128]{2,1,0:T(8,128)(2,1)S(1)} %collective-permute-done.23.rest_0_), channel_id=1, source_target_pairs={{0,4},{4,0},{8,12},{12,8},{16,20},{20,16},{24,28},{28,24},{1,5},{5... | collective-permute-start | bytes 786440 | tf_op jit(solution)/shard_map/ppermute | solution.py:406
  120.8 6.9 %collective-permute-start.28 = (bf16[8,128,128]{2,1,0:T(8,128)(2,1)S(1)}, bf16[8,128,128]{2,1,0:T(8,128)(2,1)S(1)}, u32[]{:S(2)}, u32[]{:S(2)}) collective-permute-start(bf16[8,128,128]{2,1,0:T(8,128)(2,1)S(1)} %collective-permute-done.27.rest_2_), channel_id=1, source_target_pairs={{0,4},{4,0},{8,12},{12,8},{16,20},{20,16},{24,28},{28,24},{1,5},{5... | collective-permute-start | bytes 786440 | tf_op jit(solution)/shard_map/ppermute | solution.py:406
  131.9 19.7 %collective-permute-start.43 = (bf16[4,128,128]{2,1,0:T(8,128)(2,1)S(1)}, bf16[4,128,128]{2,1,0:T(8,128)(2,1)S(1)}, u32[]{:S(2)}, u32[]{:S(2)}) collective-permute-start(bf16[4,128,128]{2,1,0:T(8,128)(2,1)S(1)} %get-tuple-element.43), channel_id=1, source_target_pairs={{0,1},{1,0},{2,3},{3,2},{4,5},{5,4},{6,7},{7,6},{8,9},{9,8},{10,11... | collective-permute-start | bytes 393224 | tf_op jit(solution)/shard_map/ppermute | solution.py:489
  134.9 16.7 %collective-permute-start.44 = (bf16[4,128,128]{2,1,0:T(8,128)(2,1)S(1)}, bf16[4,128,128]{2,1,0:T(8,128)(2,1)S(1)}, u32[]{:S(2)}, u32[]{:S(2)}) collective-permute-start(bf16[4,128,128]{2,1,0:T(8,128)(2,1)S(1)} %get-tuple-element.44), channel_id=1, source_target_pairs={{0,2},{1,3},{2,0},{3,1},{4,6},{5,7},{6,4},{7,5},{8,10},{9,11},{10,... | collective-permute-start | bytes 393224 | tf_op jit(solution)/shard_map/ppermute | solution.py:489
  136.4 15.3 %collective-permute-start.45 = (bf16[4,128,128]{2,1,0:T(8,128)(2,1)S(1)}, bf16[4,128,128]{2,1,0:T(8,128)(2,1)S(1)}, u32[]{:S(2)}, u32[]{:S(2)}) collective-permute-start(bf16[4,128,128]{2,1,0:T(8,128)(2,1)S(1)} %get-tuple-element.45), channel_id=1, source_target_pairs={{0,3},{1,2},{2,1},{3,0},{4,7},{5,6},{6,5},{7,4},{8,11},{9,10},{10,... | collective-permute-start | bytes 393224 | tf_op jit(solution)/shard_map/ppermute | solution.py:489
  136.5 1.3 collective-permute-start.20

commit v4 on v3

--- a/solution.py
+++ b/solution.py
@@ -8,9 +8,11 @@
 
 F32 = jnp.float32
 BF16 = jnp.bfloat16
+HIGH = lax.Precision.HIGH
 HIGHEST = lax.Precision.HIGHEST
 BATCH = 4
 WIDE = 4
+PIECES = 2
 
 VM = pl.BlockSpec(memory_space=pltpu.VMEM)
 SM = pl.BlockSpec(memory_space=pltpu.SMEM)
@@ -63,30 +65,39 @@
     return jnp.where(chip < chips // 2, chips - 1, 0)
 
 
+CLASSES = 5
+
+
 def lists_kernel(strips, tpi, chips, ints_ref, lists_ref):
     ints = Ints(ints_ref, strips, tpi)
-    far = far_chip(ints.me() // 2, chips)
-
-    def scan(strip, count):
-        hit = ints.group(strip) // 2 == far
-        lists_ref[jnp.where(hit, count, strips - 1 - strip + count)] = strip
-        return count + hit.astype(jnp.int32)
-
-    count = lax.fori_loop(0, ints.live(), scan, jnp.int32(0))
-    lists_ref[strips] = count
-    lists_ref[strips + 1] = ints.live() - count
+    chip = ints.me() // 2
+    far = far_chip(chip, chips)
+
+    def scan(strip, counts):
+        owner = ints.group(strip) // 2
+        hops = abs(owner - chip)
+        is_far, is_last, is_near = owner == far, hops == chips - 1, hops <= 1
+        n_far, n_near, n_last = counts
+        n_mid = strip - n_near - n_last
+        lists_ref[jnp.where(is_far, n_far, strips + strip - n_far)] = strip
+        lists_ref[jnp.where(is_near, 2 * strips + n_near,
+                            jnp.where(is_last, 4 * strips + n_last, 3 * strips + n_mid))] = strip
+        return tuple(n + hit.astype(jnp.int32)
+                     for n, hit in zip(counts, (is_far, is_near, is_last)))
+
+    n_far, n_near, n_last = lax.fori_loop(0, ints.live(), scan, (jnp.int32(0),) * 3)
+    n_all = ints.live()
+    for c, count in enumerate((n_far, n_all - n_far, n_near, n_all - n_near - n_last, n_last)):
+        lists_ref[CLASSES * strips + c] = count
 
 
 class Picked:
-    def __init__(self, lists_ref, strips, far, rest):
-        n_far, n_rest = lists_ref[strips], lists_ref[strips + 1]
-        self.lists, self.strips = lists_ref, strips
-        self.start = jnp.where(rest, strips - n_rest, 0)
-        self.count = jnp.where(far, n_far, 0) + jnp.where(rest, n_rest, 0)
+    def __init__(self, lists_ref, strips, own):
+        self.lists, self.start = lists_ref, own * strips
+        self.count = lists_ref[CLASSES * strips + own]
 
     def strip(self, at):
-        where = self.start + at
-        return self.lists[jnp.where(where >= self.strips, where - self.strips, where)]
+        return self.lists[self.start + at]
 
     def fetch(self, tiles_ref, buf_ref, sems):
         def begin(at, carry):
@@ -113,10 +124,11 @@
         lax.fori_loop(0, (self.count + BATCH - 1) // BATCH, trip, jnp.int32(0))
 
 
-def sketch_kernel(far_only, chips, owned, n_src, ints_ref, lists_ref, tiles_ref, *rest):
+def sketch_kernel(far_only, chips, blocks, n_src, ints_ref, lists_ref, tiles_ref, *rest):
     sources = rest[:n_src]
-    both_ref, theirs_ref, omega_ref, buf_ref, sems = rest[-5:]
-    half = theirs_ref.shape[0]
+    both_ref, *theirs, omega_ref, buf_ref, sems = rest[-3 - 1 - (1 if far_only else PIECES):]
+    half = both_ref.shape[0] // 2
+    units = half // (PIECES * blocks)
     strips, tpi = buf_ref.shape[:2]
     ints = Ints(ints_ref, strips, tpi)
     chip, core, band = ints.me() // 2, ints.me() % 2, ints.band()
@@ -125,7 +137,7 @@
     own = pltpu.make_async_copy(sources[0], omega_ref.at[pl.ds(band * held, held)],
                                 sems.at[strips])
     own.start()
-    picked = Picked(lists_ref, strips, far_only, not far_only)
+    picked = Picked(lists_ref, strips, 0 if far_only else 1)
     picked.fetch(tiles_ref, buf_ref, sems)
     both_ref[...] = jnp.zeros_like(both_ref)
     for s in range(1, n_src):
@@ -136,25 +148,29 @@
         owner = ints.group(strip)
         unit = jnp.int32(0) if far_only else owner // 2 - (far == 0).astype(jnp.int32)
         side = jnp.where(owner % 2 == core, 0, half)
-        block = side + unit * owned + ints.slot(strip)
+        piece, slot = ints.slot(strip) // blocks, ints.slot(strip) % blocks
+        block = side + (piece * units + unit) * blocks + slot
         left = jnp.concatenate([buf_ref[at, j] for j in range(tpi)], axis=1)
         right = jnp.concatenate([omega_ref[ints.column(strip, j)] for j in range(tpi)], axis=0)
         both_ref[block] += jnp.dot(left, right, preferred_element_type=F32) * valid
 
     picked.in_batches(tiles_ref, buf_ref, sems, work)
-    theirs_ref[...] = both_ref[pl.ds(half, half)].astype(BF16)
-
-
-def partial_sketch(far_only, scalars, tiles, sources, chips, owned, after=()):
+    size = half // len(theirs)
+    for p, out in enumerate(theirs):
+        out[...] = both_ref[pl.ds(half + p * size, size)].astype(BF16)
+
+
+def partial_sketch(far_only, scalars, tiles, sources, chips, blocks, after=()):
     strips, tpi, edge, _ = tiles.shape
     col_own, _, cols = sources[0].shape
-    blocks = owned * (1 if far_only else chips - 1)
+    half = PIECES * blocks * (1 if far_only else chips - 1)
+    n_out = 1 if far_only else PIECES
     return pl.pallas_call(
-        functools.partial(sketch_kernel, far_only, chips, owned, len(sources)),
-        out_shape=(pltpu.VMEM((2 * blocks, edge, cols), F32),
-                   pltpu.VMEM((blocks, edge, cols), BF16)),
+        functools.partial(sketch_kernel, far_only, chips, blocks, len(sources)),
+        out_shape=(pltpu.VMEM((2 * half, edge, cols), F32),)
+        + (pltpu.VMEM((half // n_out, edge, cols), BF16),) * n_out,
         in_specs=[SM] * 2 + [HB] * 2 + [VM] * (len(sources) - 1 + len(after)),
-        out_specs=(VM, VM),
+        out_specs=(VM,) * (1 + n_out),
         scratch_shapes=[
             pltpu.VMEM((col_own * len(sources), edge, cols), BF16),
             pltpu.VMEM((strips, tpi, edge, edge), BF16),
@@ -172,7 +188,7 @@
     out_ref[...] = (mine_ref[rows] + pair_ref[rows].astype(F32)).astype(BF16)
 
 
-def relay_kernel(t, chips, owned, blocks, piece, ints_ref, far_mine, far_pair, rest_mine,
+def relay_kernel(t, chips, blocks, piece, ints_ref, far_mine, far_pair, rest_mine,
                  rest_pair, even_in, odd_in, even_out, odd_out):
     chip = ints_ref[ME] // 2
     far = far_chip(chip, chips)
@@ -193,12 +209,13 @@
             @pl.when((chip % 2 == parity) & (unit != far))
             def _():
                 unit_at = unit - (far == 0).astype(jnp.int32)
-                rows = pl.ds(unit_at * owned + piece * blocks, blocks)
+                rows = pl.ds((piece * (chips - 1) + unit_at) * blocks, blocks)
+                there = pl.ds(unit_at * blocks, blocks)
                 more = jnp.where(fed, carried[...].astype(F32), 0.0)
-                out[...] = (rest_mine[rows] + rest_pair[rows].astype(F32) + more).astype(BF16)
-
-
-def combine_kernel(chips, owned, piece, ints_ref, rest_mine, rest_pair, even_ref,
+                out[...] = (rest_mine[rows] + rest_pair[there].astype(F32) + more).astype(BF16)
+
+
+def combine_kernel(chips, piece, ints_ref, rest_mine, rest_pair, even_ref,
                    odd_ref, idf_ref, gram_in, sketch_ref, weight_ref, gram_ref):
     blocks = sketch_ref.shape[0]
     chip = ints_ref[ME] // 2
@@ -206,8 +223,8 @@
     inner = (chip > 0) & (chip < chips - 1)
     gram = gram_in[...]
     for b in range(blocks):
-        at = unit_at * owned + piece * blocks + b
-        total = (rest_mine[at] + rest_pair[at].astype(F32) + even_ref[b].astype(F32)
+        at = unit_at * blocks + b
+        total = (rest_mine[piece * (chips - 1) * blocks + at] + rest_pair[at].astype(F32) + even_ref[b].astype(F32)
                  + jnp.where(inner, odd_ref[b].astype(F32), 0.0))
         row = idf_ref[pl.ds(piece * blocks + b, 1), :]
         scale = jnp.transpose(jnp.broadcast_to(row, total.shape[::-1]))
@@ -239,14 +256,18 @@
         x = x_ref[...]
         row = [jnp.broadcast_to(x_ref[pl.ds(j + k, 1), :], (8, n)) for k in range(WIDE)]
         column = [pick(x, j + k) for k in range(WIDE)]
+        block = [[pick(row[k], j + m) for m in range(WIDE)] for k in range(WIDE)]
         scaled = []
         for k in range(WIDE):
             here = lane == j + k
-            scaled.append(jnp.where(here, 1.0, row[k]) / pick(row[k], j + k))
+            inverse = 1.0 / block[k][k]
+            scaled.append(jnp.where(here, 1.0, row[k]) * inverse)
             for m in range(k + 1, WIDE):
-                entry = pick(row[m], j + k)
+                entry, across = block[m][k], block[k][m] * inverse
+                for i in range(k + 1, WIDE):
+                    block[m][i] = block[m][i] - entry * (block[k][i] * inverse)
                 row[m] = jnp.where(here, 0.0, row[m]) - entry * scaled[k]
-                column[m] = column[m] - column[k] * pick(scaled[k], j + m)[:1]
+                column[m] = column[m] - column[k] * across[:1]
         below = rows >= j + WIDE
         x = jnp.where((columns >= j) & (columns < j + WIDE) & below, 0.0, x)
         for k in range(WIDE):
@@ -272,21 +293,22 @@
     for piece in pieces:
         for b in range(piece.shape[0]):
             q_ref[at] = lax.dot_general(piece[b], inverse_ref[...], (((1,), (1,)), ((), ())),
-                                        precision=HIGHEST, preferred_element_type=F32)
+                                        precision=HIGH, preferred_element_type=F32)
             at += 1
 
 
-def project_kernel(last, chips, owned, away, ints_ref, lists_ref, tiles_ref, *rest):
+def project_kernel(own_class, chips, owned, away, ints_ref, lists_ref, tiles_ref, *rest):
     sources, rest = rest[:len(away)], rest[len(away):]
-    before, outs = (rest[:1], rest[1:-4]) if last else ((), rest[:-4])
+    last = own_class == 2
+    n_more = 1 if own_class else 0
+    before, outs = rest[:n_more], rest[n_more:-4]
     doc_ref, weights_ref, buf_ref, sems = rest[-4:]
     strips, tpi, edge = buf_ref.shape[:3]
     ints = Ints(ints_ref, strips, tpi)
     chip, core = ints.me() // 2, ints.me() % 2
-    at_end = abs(far_chip(chip, chips) - chip) == chips - 1
-    picked = Picked(lists_ref, strips, at_end if last else jnp.logical_not(at_end), not last)
+    picked = Picked(lists_ref, strips, 2 + own_class)
     picked.fetch(tiles_ref, buf_ref, sems)
-    doc_ref[...] = before[0][...] if last else jnp.zeros_like(doc_ref)
+    doc_ref[...] = before[0][...] if n_more else jnp.zeros_like(doc_ref)
     for source, (hops, other, piece) in zip(sources, away):
         there = chip + jnp.where(chip % 2 == 0, hops, -hops)
         size = source.shape[0]
@@ -313,16 +335,17 @@
             outs[s][...] = doc_ref[pl.ds(at, held)].astype(outs[s].dtype)
 
 
-def project(last, scalars, tiles, sources, away, before, chips, owned, n_dev, held):
+def project(own_class, scalars, tiles, sources, away, before, chips, owned, n_dev, held):
     strips, tpi, edge, _ = tiles.shape
     cols = sources[0].shape[1]
+    last = own_class == 2
     if last:
         out_shape = [pltpu.VMEM((held, cols, edge), BF16 if s else F32) for s in range(n_dev)]
     else:
         out_shape = [pltpu.VMEM((n_dev * held, cols, edge), F32)]
-    more = [near(before)] if last else []
+    more = [near(before)] if own_class else []
     return pl.pallas_call(
-        functools.partial(project_kernel, last, chips, owned, away),
+        functools.partial(project_kernel, own_class, chips, owned, away),
         out_shape=out_shape,
         in_specs=[SM] * 2 + [HB] + [VM] * (len(sources) + len(more)),
         out_specs=[VM] * len(out_shape),
@@ -333,8 +356,7 @@
             pltpu.SemaphoreType.DMA((strips,)),
         ],
         compiler_params=params(28),
-        cost_estimate=cost(strips // 4 if last else strips),
-        name="project_last" if last else "project",
+        cost_estimate=cost(strips // 3),
     )(*scalars, far_off(tiles), *[near(s) for s in sources], *more)
 
 
@@ -388,17 +410,18 @@
     edge = tiles.shape[2]
     cols = omega.shape[1]
     owned = idf.shape[0] // edge
-    pieces = 2 if owned % 2 == 0 else 1
+    pieces = PIECES
     blocks = owned // pieces
     me, band = lax.axis_index("group"), lax.axis_index("dev")
     strips, tpi = tile_col.shape
     ints = jnp.concatenate([me[None], band[None], live_count, strip_group, strip_slot]
                            + [tile_col[:, j] for j in range(tpi)]).astype(jnp.int32)
-    lists = pl.pallas_call(
+    ints = far_off(ints)
+
+    lists = far_off(pl.pallas_call(
         functools.partial(lists_kernel, strips, tpi, chips),
-        out_shape=jax.ShapeDtypeStruct((strips + 2,), jnp.int32), in_specs=[SM], out_specs=SM,
-        name="lists")(ints)
-    ints, lists = far_off(ints), far_off(lists)
+        out_shape=jax.ShapeDtypeStruct((CLASSES * (strips + 1),), jnp.int32), in_specs=[SM],
+        out_specs=SM, compiler_params=params(1), name="lists")(ints))
     scalars = (ints, lists)
     swap_links = [(i, i ^ 1) for i in range(n_group)]
 
@@ -420,21 +443,22 @@
     omegas = [own_omega] + [lax.ppermute(own_omega, "dev", partners(n_dev, s))
                             for s in range(1, n_dev)]
 
-    far_mine, far_theirs = partial_sketch(True, scalars, tiles, omegas, chips, owned)
+    far_mine, far_theirs = partial_sketch(True, scalars, tiles, omegas, chips, blocks)
     far_pair = swap(far_theirs)
     piece_shape = pltpu.VMEM((blocks, edge, cols), BF16)
     first = [on_chip(functools.partial(first_kernel, blocks, p), piece_shape,
                      far_mine, far_pair) for p in range(pieces)]
     evens = [over(x, even_links) for x in first]
     odds = list(evens)
-    rest_mine, rest_theirs = partial_sketch(False, scalars, tiles, omegas, chips, owned, first)
-    rest_pair = swap(rest_theirs)
+    rest_mine, *rest_theirs = partial_sketch(False, scalars, tiles, omegas, chips, blocks,
+                                             first)
+    rest_pairs = [swap(x) for x in rest_theirs]
     for t in range(2, chips):
         for p in range(pieces):
             to_even, to_odd = on_chip(
-                functools.partial(relay_kernel, t, chips, owned, blocks, p),
+                functools.partial(relay_kernel, t, chips, blocks, p),
                 (piece_shape, piece_shape), ints, far_mine, far_pair, rest_mine,
-                rest_pair, evens[p], odds[p], in_specs=[SM] + [VM] * 6)
+                rest_pairs[p], evens[p], odds[p], in_specs=[SM] + [VM] * 6)
             evens[p] = over(to_even, even_links)
             odds[p] = over(to_odd, odd_links)
 
@@ -442,10 +466,10 @@
     sketches, weights = [], []
     for p in range(pieces):
         sk, w, gram = on_chip(
-            functools.partial(combine_kernel, chips, owned, p),
+            functools.partial(combine_kernel, chips, p),
             (pltpu.VMEM((blocks, edge, cols), F32), pltpu.VMEM((blocks, cols, edge), BF16),
              pltpu.VMEM((cols, cols), F32)),
-            ints, rest_mine, rest_pair, evens[p], odds[p],
+            ints, rest_mine, rest_pairs[p], evens[p], odds[p],
             idf.reshape(owned, edge), gram, in_specs=[SM] + [VM] * 6)
         sketches.append(sk)
         weights.append(w)
@@ -455,9 +479,11 @@
     for p in range(pieces):
         sources += [weights[p], swap(weights[p])]
         away += [(0, 0, p), (0, 1, p)]
+    stages = []
     for t in range(1, chips):
-        if t == chips - 1:
-            near_sources, near_away, sources, away = sources, away, [], []
+        if t in (2, chips - 1):
+            stages.append((sources, away))
+            sources, away = [], []
         for p in range(pieces):
             to_even, to_odd = odds[p], evens[p]
             evens[p] = over(to_even, even_links)
@@ -467,11 +493,12 @@
                 odds[p] = over(to_odd, odd_links)
                 sources += [odds[p], swap(odds[p])]
                 away += [(-t, 0, p), (-t, 1, p)]
-
-    near_chip = 2
-    while near_chip < n_group:
-        gram = gram + lax.ppermute(gram, "group", partners(n_group, near_chip))
-        near_chip *= 2
+    stages.append((sources, away))
+
+    step = 2
+    while step < n_group:
+        gram = gram + lax.ppermute(gram, "group", partners(n_group, step))
+        step *= 2
     gram = functools.reduce(jnp.add, exchanges(gram, "dev", n_dev))
     gram = gram + swap(gram)
     square = pltpu.VMEM((cols, cols), F32)
@@ -483,9 +510,12 @@
     q_basis = on_chip(basis_kernel, jax.ShapeDtypeStruct((owned, edge, cols), F32),
                       inverse, *sketches).reshape(owned * edge, cols)
 
-    docs = project(False, scalars, tiles, near_sources, near_away, None, chips, owned, n_dev,
-                   col_own)[0]
-    parts = project(True, scalars, tiles, sources, away, docs, chips, owned, n_dev, col_own)
+    docs = None
+    for own_class, (sources, away) in enumerate(stages):
+        docs = project(own_class, scalars, tiles, sources, away, docs, chips, owned, n_dev,
+                       col_own)
+        docs = docs if own_class == 2 else docs[0]
+    parts = docs
     arrived = [lax.ppermute(parts[s], "dev", partners(n_dev, s)) for s in range(1, n_dev)]
     doc_factor = on_chip(finish_kernel, jax.ShapeDtypeStruct((cols, col_own * edge), BF16),
                          inverse, parts[0], *arrived)

time: 153 us -> 142 us (0.928)
  starting transfers between devices: 42.7 us -> 33.9 us
    ppermute x20, starting transfers between devices: 23.9 us -> 13.5 us  [over(): return lax.ppermute(x, 'group', links)]
    pallas_call x12, Pallas kernels: 21.6 us -> 16.9 us  [on_chip(): pl.pallas_call(kernel, out_shape=out_shape, in_specs=specs, out_specs=jax...]
    pallas_call x4 -> x5, Pallas kernels: 21 us -> 24 us  [the longest x3 13.5 us: project(): pl.pallas_call(functools.partial(project_kernel, own_class, chips, owned,...]
    ppermute x3, starting transfers between devices: 2.78 us -> 4.59 us  [exchanges(): lax.ppermute(x, axis, [(i, i // span * span + (i + k * s) % span) for i i...]
    ppermute x15 -> x16, starting transfers between devices: 3.47 us -> 3.17 us  [swap(): return lax.ppermute(x, 'group', swap_links)]
    ppermute x15 -> x16, waiting for transfers between devices: 3.17 us -> 3.17 us  [swap(): return lax.ppermute(x, 'group', swap_links)]
  transfers between devices with their start and end apart: 46 -> 47, of which waited for: 16 -> 16; matrix products, arithmetic and copies ran while one was open for 1% -> 2% of each run, Pallas kernels for 21% -> 21%
where the time goes in v4:
time: 142 us
  waiting for transfers between devices  60.2 us (42%)
  Pallas kernels  43.4 us (31%)
  starting transfers between devices  33.9 us (24%)
  local copies, waits for them, and re-layouts  2.8 us (2%)
  between operations  1.58 us (1%)
    ppermute x20, waiting for transfers between devices, over(): return lax.ppermute(x, 'group', links)  52.7 us
    pallas_call x12, Pallas kernels, on_chip(): pl.pallas_call(kernel, out_shape=out_shape, in_specs=specs, out_specs=jax...  16.9 us
    pallas_call x3, Pallas kernels, project(): pl.pallas_call(functools.partial(project_kernel, own_class, chips, owned,...  13.5 us
    ppermute x20, starting transfers between devices, over(): return lax.ppermute(x, 'group', links)  13.5 us
    pallas_call x2, Pallas kernels, partial_sketch(): pl.pallas_call(functools.partial(sketch_kernel, far_only, chips, blocks,...  10.5 us
    ppermute x3, starting transfers between devices, on_device(): lax.ppermute(parts[s], 'dev', partners(n_dev, s))  4.79 us
    ppermute x3, starting transfers between devices, exchanges(): lax.ppermute(x, axis, [(i, i // span * span + (i + k * s) % span) for i i...  4.59 us
    ppermute x3, starting transfers between devices, on_device(): lax.ppermute(own_omega, 'dev', partners(n_dev, s))  4.57 us
  transfers between devices with their start and end apart: 47, of which 16 were waited for; matrix products, arithmetic and copies ran while one was open for 2% of the time, Pallas kernels for 21%

profile of v4, /device:TPU:0, one launch (start us, length us, event | category | flops | bytes accessed | tf_op | source)
XLA Modules:
  0.0 141.9 jit_solution(7135024661401578320)
XLA Ops:
  0.6 3.0 %collective-permute-start = (bf16[4,128,128]{2,1,0:T(8,128)(2,1)}, bf16[4,128,128]{2,1,0:T(8,128)(2,1)S(1)}, u32[]{:S(2)}, u32[]{:S(2)}) collective-permute-start(bf16[4,128,128]{2,1,0:T(8,128)(2,1)} %bitcast.18), channel_id=1, source_target_pairs={{0,1},{1,0},{2,3},{3,2},{4,5},{5,4},{6,7},{7,6},{8,9},{9,8},{10,11... | collective-permute-start | bytes 393224 | tf_op jit(solution)/shard_map/ppermute | solution.py:443
  3.7 1.5 %collective-permute-start.1 = (bf16[4,128,128]{2,1,0:T(8,128)(2,1)}, bf16[4,128,128]{2,1,0:T(8,128)(2,1)S(1)}, u32[]{:S(2)}, u32[]{:S(2)}) collective-permute-start(bf16[4,128,128]{2,1,0:T(8,128)(2,1)} %bitcast.19), channel_id=1, source_target_pairs={{0,2},{1,3},{2,0},{3,1},{4,6},{5,7},{6,4},{7,5},{8,10},{9,11},{10,... | collective-permute-start | bytes 393224 | tf_op jit(solution)/shard_map/ppermute | solution.py:443
  5.9 0.9 slice_bitcast_fusion
  6.7 1.3 concatenate.3.ints_ref
  8.1 2.5 %lists.1.lists_ref = s32[365]{0:T(512)S(1)} custom-call(s32[507]{0:T(512)} %concatenate.3.ints_ref), custom_call_target="tpu_custom_call" | custom-call | tf_op jit(solution)/shard_map/lists/pallas_call | solution.py:421
  11.7 4.0 %sketch_far.1 = (f32[32,128,128]{2,1,0:T(8,128)S(1)}, bf16[16,128,128]{2,1,0:T(8,128)(2,1)S(1)}) custom-call(s32[507]{0:T(512)} %concatenate.3.ints_ref, s32[365]{0:T(512)} %copy-done.1, bf16[72,5,128,128]{3,2,1,0:T(8,128)(2,1)} %tiles_ref.9, bf16[4,128,128]{2,1,0:T(8,128)(2,1)} %bitcast.21, bf16[4,128,128]{2,1,0:T(8,128)(2,1)S(1)} %collective-permute-done.rest_1_, ...), custom_call_target="tpu_custom_call" | custom-call | flops 4831838208 | bytes 9437184 | tf_op jit(solution)/shard_map/sketch_far/pallas_call | solution.py:168
  15.7 1.9 %collective-permute-done.3.pair_ref.far_pair = bf16[16,128,128]{2,1,0:T(8,128)(2,1)S(1)} collective-permute-done((bf16[16,128,128]{2,1,0:T(8,128)(2,1)S(1)}, bf16[16,128,128]{2,1,0:T(8,128)(2,1)S(1)}, u32[]{:S(2)}, u32[]{:S(2)}) %collective-permute-start.3) | collective-permute-done | bytes 524320 | tf_op jit(solution)/shard_map/ppermute | solution.py:429
  17.7 6.5 %sketch_rest.1 = (f32[96,128,128]{2,1,0:T(8,128)S(1)}, bf16[24,128,128]{2,1,0:T(8,128)(2,1)S(1)}, bf16[24,128,128]{2,1,0:T(8,128)(2,1)S(1)}) custom-call(s32[507]{0:T(512)} %concatenate.3.ints_ref, s32[365]{0:T(512)} %copy-done.1, bf16[72,5,128,128]{3,2,1,0:T(8,128)(2,1)} %tiles_ref.9, bf16[4,128,128]{2,1,0:T(8,128)(2,1)} %bitcast.22, ...), custom_call_target="tpu_custom_call" | custom-call | flops 19327352832 | bytes 37748736 | tf_op jit(solution)/shard_map/sketch_rest/pallas_call | solution.py:168
  24.2 1.2 collective-permute-start.10
  26.1 1.5 %collective-permute-start.5 = (bf16[8,128,128]{2,1,0:T(8,128)(2,1)S(1)}, bf16[8,128,128]{2,1,0:T(8,128)(2,1)S(1)}, u32[]{:S(2)}, u32[]{:S(2)}) collective-permute-start(bf16[8,128,128]{2,1,0:T(8,128)(2,1)S(1)} %shard_map.87.rest_5_), channel_id=1, source_target_pairs={{0,8},{4,12},{8,0},{12,4},{16,24},{20,28},{24,16},{28,20},{1,9},{5... | collective-permute-start | bytes 786440 | tf_op jit(solution)/shard_map/ppermute | solution.py:439
  27.5 7.2 %collective-permute-done.11.even_in.odd_in = bf16[8,128,128]{2,1,0:T(8,128)(2,1)S(1)} collective-permute-done((bf16[8,128,128]{2,1,0:T(8,128)(2,1)S(1)}, bf16[8,128,128]{2,1,0:T(8,128)(2,1)S(1)}, u32[]{:S(2)}, u32[]{:S(2)}) %collective-permute-start.11) | collective-permute-done | bytes 262176 | tf_op jit(solution)/shard_map/ppermute | solution.py:439
  34.7 0.9 shard_map.90
  36.3 4.0 %collective-permute-done.5.even_in.odd_in = bf16[8,128,128]{2,1,0:T(8,128)(2,1)S(1)} collective-permute-done((bf16[8,128,128]{2,1,0:T(8,128)(2,1)S(1)}, bf16[8,128,128]{2,1,0:T(8,128)(2,1)S(1)}, u32[]{:S(2)}, u32[]{:S(2)}) %collective-permute-start.5) | collective-permute-done | bytes 262176 | tf_op jit(solution)/shard_map/ppermute | solution.py:439
  40.3 0.9 shard_map.88
  41.3 0.8 collective-permute-start.6
  42.0 3.9 %collective-permute-done.12.even_in = bf16[8,128,128]{2,1,0:T(8,128)(2,1)S(1)} collective-permute-done((bf16[8,128,128]{2,1,0:T(8,128)(2,1)S(1)}, bf16[8,128,128]{2,1,0:T(8,128)(2,1)S(1)}, u32[]{:S(2)}, u32[]{:S(2)}) %collective-permute-start.12) | collective-permute-done | bytes 262176 | tf_op jit(solution)/shard_map/ppermute | solution.py:439
  45.9 0.9 shard_map.91
  46.9 0.8 collective-permute-start.14
  47.7 3.9 %collective-permute-done.6.even_in = bf16[8,128,128]{2,1,0:T(8,128)(2,1)S(1)} collective-permute-done((bf16[8,128,128]{2,1,0:T(8,128)(2,1)S(1)}, bf16[8,128,128]{2,1,0:T(8,128)(2,1)S(1)}, u32[]{:S(2)}, u32[]{:S(2)}) %collective-permute-start.6) | collective-permute-done | bytes 262176 | tf_op jit(solution)/shard_map/ppermute | solution.py:439
  51.6 0.9 shard_map.89
  52.5 0.8 collective-permute-start.8
  53.3 3.9 %collective-permute-done.14.even_ref = bf16[8,128,128]{2,1,0:T(8,128)(2,1)S(1)} collective-permute-done((bf16[8,128,128]{2,1,0:T(8,128)(2,1)S(1)}, bf16[8,128,128]{2,1,0:T(8,128)(2,1)S(1)}, u32[]{:S(2)}, u32[]{:S(2)}) %collective-permute-start.14) | collective-permute-done | bytes 262176 | tf_op jit(solution)/shard_map/ppermute | solution.py:439
  57.2 1.5 %shard_map.92 = (f32[8,128,128]{2,1,0:T(8,128)S(1)}, bf16[8,128,128]{2,1,0:T(8,128)(2,1)S(1)}, f32[128,128]{1,0:T(8,128)S(1)}) custom-call(s32[507]{0:T(512)} %concatenate.3.ints_ref, f32[96,128,128]{2,1,0:T(8,128)S(1)} %get-tuple-element.27.rest_mine, bf16[24,128,128]{2,1,0:T(8,128)(2,1)S(1)} %collective-permute-done.10.rest_pair, ...), custom_call_target="tpu_custom_call" | custom-call | tf_op jit(solution)/shard_map/pallas_call | solution.py:376
  58.7 3.6 %collective-permute-done.8.even_ref = bf16[8,128,128]{2,1,0:T(8,128)(2,1)S(1)} collective-permute-done((bf16[8,128,128]{2,1,0:T(8,128)(2,1)S(1)}, bf16[8,128,128]{2,1,0:T(8,128)(2,1)S(1)}, u32[]{:S(2)}, u32[]{:S(2)}) %collective-permute-start.8) | collective-permute-done | bytes 262176 | tf_op jit(solution)/shard_map/ppermute | solution.py:439
  62.3 1.5 %shard_map.93 = (f32[8,128,128]{2,1,0:T(8,128)S(1)}, bf16[8,128,128]{2,1,0:T(8,128)(2,1)S(1)}, f32[128,128]{1,0:T(8,128)S(1)}) custom-call(s32[507]{0:T(512)} %concatenate.3.ints_ref, f32[96,128,128]{2,1,0:T(8,128)S(1)} %get-tuple-element.27.rest_mine, bf16[24,128,128]{2,1,0:T(8,128)(2,1)S(1)} %collective-permute-done.4.rest_pair, ...), custom_call_target="tpu_custom_call" | custom-call | tf_op jit(solution)/shard_map/pallas_call | solution.py:376
  63.7 0.6 collective-permute-start.16
  64.4 3.7 %collective-permute-done.16 = f32[128,128]{1,0:T(8,128)S(1)} collective-permute-done((f32[128,128]{1,0:T(8,128)S(1)}, f32[128,128]{1,0:T(8,128)S(1)}, u32[]{:S(2)}, u32[]{:S(2)}) %collective-permute-start.16) | collective-permute-done | bytes 65568 | tf_op jit(solution)/shard_map/ppermute | solution.py:500
  68.1 2.7 %collective-permute-start.17 = (f32[128,128]{1,0:T(8,128)S(1)}, f32[128,128]{1,0:T(8,128)S(1)}, u32[]{:S(2)}, u32[]{:S(2)}) collective-permute-start(f32[128,128]{1,0:T(8,128)S(1)} %add.18), channel_id=1, source_target_pairs={{0,16},{4,20},{8,24},{12,28},{16,0},{20,4},{24,8},{28,12},{1,17},{... | collective-permute-start | bytes 196616 | tf_op jit(solution)/shard_map/ppermute | solution.py:500
  70.8 1.7 %collective-permute-start.22 = (bf16[8,128,128]{2,1,0:T(8,128)(2,1)S(1)}, bf16[8,128,128]{2,1,0:T(8,128)(2,1)S(1)}, u32[]{:S(2)}, u32[]{:S(2)}) collective-permute-start(bf16[8,128,128]{2,1,0:T(8,128)(2,1)S(1)} %get-tuple-element.42.rest_0_), channel_id=1, source_target_pairs={{0,8},{4,12},{8,0},{12,4},{16,24},{20,28},{24,16},{28,20},{1,9},{5... | collective-permute-start | bytes 786440 | tf_op jit(solution)/shard_map/ppermute | solution.py:439
  73.4 6.6 %collective-permute-done.22.rest_4_ = bf16[8,128,128]{2,1,0:T(8,128)(2,1)S(1)} collective-permute-done((bf16[8,128,128]{2,1,0:T(8,128)(2,1)S(1)}, bf16[8,128,128]{2,1,0:T(8,128)(2,1)S(1)}, u32[]{:S(2)}, u32[]{:S(2)}) %collective-permute-start.22) | collective-permute-done | bytes 262176 | tf_op jit(solution)/shard_map/ppermute | solution.py:439
  80.0 3.4 %collective-permute-done.26.rest_8_ = bf16[8,128,128]{2,1,0:T(8,128)(2,1)S(1)} collective-permute-done((bf16[8,128,128]{2,1,0:T(8,128)(2,1)S(1)}, bf16[8,128,128]{2,1,0:T(8,128)(2,1)S(1)}, u32[]{:S(2)}, u32[]{:S(2)}) %collective-permute-start.26) | collective-permute-done | bytes 262176 | tf_op jit(solution)/shard_map/ppermute | solution.py:439
  83.9 3.3 %collective-permute-start.31 = (bf16[8,128,128]{2,1,0:T(8,128)(2,1)S(1)}, bf16[8,128,128]{2,1,0:T(8,128)(2,1)S(1)}, u32[]{:S(2)}, u32[]{:S(2)}) collective-permute-start(bf16[8,128,128]{2,1,0:T(8,128)(2,1)S(1)} %collective-permute-done.30.rest_6_), channel_id=1, source_target_pairs={{0,8},{4,12},{8,0},{12,4},{16,24},{20,28},{24,16},{28,20},{1,9},{5... | collective-permute-start | bytes 786440 | tf_op jit(solution)/shard_map/ppermute | solution.py:439
  87.9 6.5 %collective-permute-done.31.rest_0_ = bf16[8,128,128]{2,1,0:T(8,128)(2,1)S(1)} collective-permute-done((bf16[8,128,128]{2,1,0:T(8,128)(2,1)S(1)}, bf16[8,128,128]{2,1,0:T(8,128)(2,1)S(1)}, u32[]{:S(2)}, u32[]{:S(2)}) %collective-permute-start.31) | collective-permute-done | bytes 262176 | tf_op jit(solution)/shard_map/ppermute | solution.py:439
  94.4 3.4 %collective-permute-done.35.rest_4_ = bf16[8,128,128]{2,1,0:T(8,128)(2,1)S(1)} collective-permute-done((bf16[8,128,128]{2,1,0:T(8,128)(2,1)S(1)}, bf16[8,128,128]{2,1,0:T(8,128)(2,1)S(1)}, u32[]{:S(2)}, u32[]{:S(2)}) %collective-permute-start.35) | collective-permute-done | bytes 262176 | tf_op jit(solution)/shard_map/ppermute | solution.py:439
  98.2 1.8 %collective-permute-start.28 = (bf16[8,128,128]{2,1,0:T(8,128)(2,1)S(1)}, bf16[8,128,128]{2,1,0:T(8,128)(2,1)S(1)}, u32[]{:S(2)}, u32[]{:S(2)}) collective-permute-start(bf16[8,128,128]{2,1,0:T(8,128)(2,1)S(1)} %collective-permute-done.27.rest_6_), channel_id=1, source_target_pairs={{0,8},{4,12},{8,0},{12,4},{16,24},{20,28},{24,16},{28,20},{1,9},{5... | collective-permute-start | bytes 786440 | tf_op jit(solution)/shard_map/ppermute | solution.py:439
  100.5 6.5 %collective-permute-done.24.rest_0_ = bf16[8,128,128]{2,1,0:T(8,128)(2,1)S(1)} collective-permute-done((bf16[8,128,128]{2,1,0:T(8,128)(2,1)S(1)}, bf16[8,128,128]{2,1,0:T(8,128)(2,1)S(1)}, u32[]{:S(2)}, u32[]{:S(2)}) %collective-permute-start.24) | collective-permute-done | bytes 262176 | tf_op jit(solution)/shard_map/ppermute | solution.py:439
  107.0 5.4 %shard_map.97.rest_8_ = f32[16,128,128]{2,1,0:T(8,128)S(1)} custom-call(s32[507]{0:T(512)} %concatenate.3.ints_ref, s32[365]{0:T(512)} %copy-done.1, bf16[72,5,128,128]{3,2,1,0:T(8,128)(2,1)} %tiles_ref.9, bf16[8,128,128]{2,1,0:T(8,128)(2,1)S(1)} %get-tuple-element.42.rest_0_, bf16[8,128,128]{2,1,0:T(8,128)(2,1)S(1)} %collective-permute-done.38.rest_1_, ...), custom_call_target="tpu_custom_call" | custom-call | flops 6442450944 | bytes 12582912 | tf_op jit(solution)/shard_map/pallas_call | solution.py:347
  112.4 3.9 %collective-permute-start.20 = (f32[128,128]{1,0:T(8,128)S(1)}, f32[128,128]{1,0:T(8,128)S(1)}, u32[]{:S(2)}, u32[]{:S(2)}) collective-permute-start(f32[128,128]{1,0:T(8,128)S(1)} %add.19), channel_id=1, source_target_pairs={{0,3},{1,0},{2,1},{3,2},{4,7},{5,4},{6,5},{7,6},{8,11},{9,8},{10,9... | collective-permute-start | bytes 196616 | tf_op jit(solution)/shard_map/ppermute | solution.py:400
  116.3 0.6 collective-permute-start.18
  117.5 4.2 %shard_map.98.rest_4_ = f32[16,128,128]{2,1,0:T(8,128)S(1)} custom-call(s32[507]{0:T(512)} %concatenate.3.ints_ref, s32[365]{0:T(512)} %copy-done.1, bf16[72,5,128,128]{3,2,1,0:T(8,128)(2,1)} %tiles_ref.9, bf16[8,128,128]{2,1,0:T(8,128)(2,1)S(1)} %collective-permute-done.31.rest_0_, bf16[8,128,128]{2,1,0:T(8,128)(2,1)S(1)} %collective-permute-done.32.rest_1_, ...), custom_call_target="tpu_custom_call" | custom-call | flops 6442450944 | bytes 12582912 | tf_op jit(solution)/shard_map/pallas_call | solution.py:347
  121.7 4.0 %shard_map.99 = (f32[4,128,128]{2,1,0:T(8,128)S(1)}, bf16[4,128,128]{2,1,0:T(8,128)(2,1)S(1)}, bf16[4,128,128]{2,1,0:T(8,128)(2,1)S(1)}, bf16[4,128,128]{2,1,0:T(8,128)(2,1)S(1)}) custom-call(s32[507]{0:T(512)} %concatenate.3.ints_ref, s32[365]{0:T(512)} %copy-done.1, bf16[72,5,128,128]{3,2,1,0:T(8,128)(2,1)} %tiles_ref.9, ...), custom_call_target="tpu_custom_call" | custom-call | flops 6442450944 | bytes 12582912 | tf_op jit(solution)/shard_map/pallas_call | solution.py:347
  125.7 3.3 %collective-permute-start.44 = (bf16[4,128,128]{2,1,0:T(8,128)(2,1)S(1)}, bf16[4,128,128]{2,1,0:T(8,128)(2,1)S(1)}, u32[]{:S(2)}, u32[]{:S(2)}) collective-permute-start(bf16[4,128,128]{2,1,0:T(8,128)(2,1)S(1)} %get-tuple-element.45), channel_id=1, source_target_pairs={{0,1},{1,0},{2,3},{3,2},{4,5},{5,4},{6,7},{7,6},{8,9},{9,8},{10,11... | collective-permute-start | bytes 393224 | tf_op jit(solution)/shard_map/ppermute | solution.py:519
  129.0 1.5 %collective-permute-start.46 = (bf16[4,128,128]{2,1,0:T(8,128)(2,1)S(1)}, bf16[4,128,128]{2,1,0:T(8,128)(2,1)S(1)}, u32[]{:S(2)}, u32[]{:S(2)}) collective-permute-start(bf16[4,128,128]{2,1,0:T(8,128)(2,1)S(1)} %get-tuple-element.47), channel_id=1, source_target_pairs={{0,3},{1,2},{2,1},{3,0},{4,7},{5,6},{6,5},{7,4},{8,11},{9,10},{10,... | collective-permute-start | bytes 393224 | tf_op jit(solution)/shard_map/ppermute | solution.py:519
  130.6 1.2 collective-permute-done.21
  131.8 3.4 %shard_map.94.refs_0_ = f32[128,128]{1,0:T(8,128)S(1)} custom-call(f32[128,128]{1,0:T(8,128)S(1)} %add.23.refs_0_), custom_call_target="tpu_custom_call" | custom-call | tf_op jit(solution)/shard_map/pallas_call | solution.py:376
  135.2 3.4 %shard_map.95.inverse_ref = f32[128,128]{1,0:T(8,128)S(1)} custom-call(f32[128,128]{1,0:T(8,128)S(1)} %shard_map.94.refs_0_), custom_call_target="tpu_custom_call" | custom-call | tf_op jit(solution)/shard_map/pallas_call | solution.py:376
  138.7 2.2 %shard_map.96 = f32[16,128,128]{2,1,0:T(8,128)} custom-call(f32[128,128]{1,0:T(8,128)S(1)} %shard_map.95.inverse_ref, f32[8,128,128]{2,1,0:T(8,128)S(1)} %get-tuple-element.40.rest_0_, f32[8,128,128]{2,1,0:T(8,128)S(1)} %get-tuple-element.41.rest_1_), custom_call_target="tpu_custom_call" | custom-call | tf_op jit(solution)/shard_map/pallas_call | solution.py:376
  140.9 1.0 shard_map.100
  (75 shorter events, 6.2 us)
Async XLA Ops:
  0.6 10.6 %collective-permute-start = (bf16[4,128,128]{2,1,0:T(8,128)(2,1)}, bf16[4,128,128]{2,1,0:T(8,128)(2,1)S(1)}, u32[]{:S(2)}, u32[]{:S(2)}) collective-permute-start(bf16[4,128,128]{2,1,0:T(8,128)(2,1)} %bitcast.18), channel_id=1, source_target_pairs={{0,1},{1,0},{2,3},{3,2},{4,5},{5,4},{6,7},{7,6},{8,9},{9,8},{10,11... | collective-permute-start | bytes 393224 | tf_op jit(solution)/shard_map/ppermute | solution.py:443
  3.7 8.0 %collective-permute-start.1 = (bf16[4,128,128]{2,1,0:T(8,128)(2,1)}, bf16[4,128,128]{2,1,0:T(8,128)(2,1)S(1)}, u32[]{:S(2)}, u32[]{:S(2)}) collective-permute-start(bf16[4,128,128]{2,1,0:T(8,128)(2,1)} %bitcast.19), channel_id=1, source_target_pairs={{0,2},{1,3},{2,0},{3,1},{4,6},{5,7},{6,4},{7,5},{8,10},{9,11},{10,... | collective-permute-start | bytes 393224 | tf_op jit(solution)/shard_map/ppermute | solution.py:443
  5.2 6.5 %collective-permute-start.2 = (bf16[4,128,128]{2,1,0:T(8,128)(2,1)}, bf16[4,128,128]{2,1,0:T(8,128)(2,1)S(1)}, u32[]{:S(2)}, u32[]{:S(2)}) collective-permute-start(bf16[4,128,128]{2,1,0:T(8,128)(2,1)} %bitcast.20), channel_id=1, source_target_pairs={{0,3},{1,2},{2,1},{3,0},{4,7},{5,6},{6,5},{7,4},{8,11},{9,10},{10,... | collective-permute-start | bytes 393224 | tf_op jit(solution)/shard_map/ppermute | solution.py:443
  15.7 2.0 %collective-permute-start.3 = (bf16[16,128,128]{2,1,0:T(8,128)(2,1)S(1)}, bf16[16,128,128]{2,1,0:T(8,128)(2,1)S(1)}, u32[]{:S(2)}, u32[]{:S(2)}) collective-permute-start(bf16[16,128,128]{2,1,0:T(8,128)(2,1)S(1)} %get-tuple-element.26), channel_id=1, source_target_pairs={{0,4},{4,0},{8,12},{12,8},{16,20},{20,16},{24,28},{28,24},{1,5},{5... | collective-permute-start | bytes 1572872 | tf_op jit(solution)/shard_map/ppermute | solution.py:429
  24.2 10.5 %collective-permute-start.10 = (bf16[24,128,128]{2,1,0:T(8,128)(2,1)S(1)}, bf16[24,128,128]{2,1,0:T(8,128)(2,1)S(1)}, u32[]{:S(2)}, u32[]{:S(2)}) collective-permute-start(bf16[24,128,128]{2,1,0:T(8,128)(2,1)S(1)} %get-tuple-element.33), channel_id=1, source_target_pairs={{0,4},{4,0},{8,12},{12,8},{16,20},{20,16},{24,28},{28,24},{1,5},{5... | collective-permute-start | bytes 2359304 | tf_op jit(solution)/shard_map/ppermute | solution.py:429
  25.4 14.9 %collective-permute-start.4 = (bf16[24,128,128]{2,1,0:T(8,128)(2,1)S(1)}, bf16[24,128,128]{2,1,0:T(8,128)(2,1)S(1)}, u32[]{:S(2)}, u32[]{:S(2)}) collective-permute-start(bf16[24,128,128]{2,1,0:T(8,128)(2,1)S(1)} %get-tuple-element.28), channel_id=1, source_target_pairs={{0,4},{4,0},{8,12},{12,8},{16,20},{20,16},{24,28},{28,24},{1,5},{5... | collective-permute-start | bytes 2359304 | tf_op jit(solution)/shard_map/ppermute | solution.py:429
  25.5 9.2 %collective-permute-start.11 = (bf16[8,128,128]{2,1,0:T(8,128)(2,1)S(1)}, bf16[8,128,128]{2,1,0:T(8,128)(2,1)S(1)}, u32[]{:S(2)}, u32[]{:S(2)}) collective-permute-start(bf16[8,128,128]{2,1,0:T(8,128)(2,1)S(1)} %shard_map.86.rest_4_), channel_id=1, source_target_pairs={{0,8},{4,12},{8,0},{12,4},{16,24},{20,28},{24,16},{28,20},{1,9},{5... | collective-permute-start | bytes 786440 | tf_op jit(solution)/shard_map/ppermute | solution.py:439
  26.1 14.2 %collective-permute-start.5 = (bf16[8,128,128]{2,1,0:T(8,128)(2,1)S(1)}, bf16[8,128,128]{2,1,0:T(8,128)(2,1)S(1)}, u32[]{:S(2)}, u32[]{:S(2)}) collective-permute-start(bf16[8,128,128]{2,1,0:T(8,128)(2,1)S(1)} %shard_map.87.rest_5_), channel_id=1, source_target_pairs={{0,8},{4,12},{8,0},{12,4},{16,24},{20,28},{24,16},{28,20},{1,9},{5... | collective-permute-start | bytes 786440 | tf_op jit(solution)/shard_map/ppermute | solution.py:439
  35.7 10.3 %collective-permute-start.12 = (bf16[8,128,128]{2,1,0:T(8,128)(2,1)S(1)}, bf16[8,128,128]{2,1,0:T(8,128)(2,1)S(1)}, u32[]{:S(2)}, u32[]{:S(2)}) collective-permute-start(bf16[8,128,128]{2,1,0:T(8,128)(2,1)S(1)} %get-tuple-element.34), channel_id=1, source_target_pairs={{0,8},{4,12},{8,0},{12,4},{16,24},{20,28},{24,16},{28,20},{1,9},{5... | collective-permute-start | bytes 786440 | tf_op jit(solution)/shard_map/ppermute | solution.py:439
  36.3 9.7 %collective-permute-start.13 = (bf16[8,128,128]{2,1,0:T(8,128)(2,1)S(1)}, bf16[8,128,128]{2,1,0:T(8,128)(2,1)S(1)}, u32[]{:S(2)}, u32[]{:S(2)}) collective-permute-start(bf16[8,128,128]{2,1,0:T(8,128)(2,1)S(1)} %get-tuple-element.35), channel_id=1, source_target_pairs={{0,4},{4,0},{8,16},{12,20},{16,8},{20,12},{24,28},{28,24},{1,5},{5... | collective-permute-start | bytes 786440 | tf_op jit(solution)/shard_map/ppermute | solution.py:439
  41.3 10.3 %collective-permute-start.6 = (bf16[8,128,128]{2,1,0:T(8,128)(2,1)S(1)}, bf16[8,128,128]{2,1,0:T(8,128)(2,1)S(1)}, u32[]{:S(2)}, u32[]{:S(2)}) collective-permute-start(bf16[8,128,128]{2,1,0:T(8,128)(2,1)S(1)} %get-tuple-element.29), channel_id=1, source_target_pairs={{0,8},{4,12},{8,0},{12,4},{16,24},{20,28},{24,16},{28,20},{1,9},{5... | collective-permute-start | bytes 786440 | tf_op jit(solution)/shard_map/ppermute | solution.py:439
  42.0 9.5 %collective-permute-start.7 = (bf16[8,128,128]{2,1,0:T(8,128)(2,1)S(1)}, bf16[8,128,128]{2,1,0:T(8,128)(2,1)S(1)}, u32[]{:S(2)}, u32[]{:S(2)}) collective-permute-start(bf16[8,128,128]{2,1,0:T(8,128)(2,1)S(1)} %get-tuple-element.30), channel_id=1, source_target_pairs={{0,4},{4,0},{8,16},{12,20},{16,8},{20,12},{24,28},{28,24},{1,5},{5... | collective-permute-start | bytes 786440 | tf_op jit(solution)/shard_map/ppermute | solution.py:439
  46.9 10.3 %copy-start = (f32[2048]{0:T(1024)S(1)}, f32[2048]{0:T(1024)}, u32[]{:S(2)}) copy-start(f32[2048]{0:T(1024)} %param.13) | copy-start | bytes 24580
  46.9 10.3 %collective-permute-start.14 = (bf16[8,128,128]{2,1,0:T(8,128)(2,1)S(1)}, bf16[8,128,128]{2,1,0:T(8,128)(2,1)S(1)}, u32[]{:S(2)}, u32[]{:S(2)}) collective-permute-start(bf16[8,128,128]{2,1,0:T(8,128)(2,1)S(1)} %get-tuple-element.36), channel_id=1, source_target_pairs={{0,8},{4,12},{8,0},{12,4},{16,24},{20,28},{24,16},{28,20},{1,9},{5... | collective-permute-start | bytes 786440 | tf_op jit(solution)/shard_map/ppermute | solution.py:439
  47.7 9.5 %collective-permute-start.15 = (bf16[8,128,128]{2,1,0:T(8,128)(2,1)S(1)}, bf16[8,128,128]{2,1,0:T(8,128)(2,1)S(1)}, u32[]{:S(2)}, u32[]{:S(2)}) collective-permute-start(bf16[8,128,128]{2,1,0:T(8,128)(2,1)S(1)} %get-tuple-element.37), channel_id=1, source_target_pairs={{0,4},{4,0},{8,16},{12,20},{16,8},{20,12},{24,28},{28,24},{1,5},{5... | collective-permute-start | bytes 786440 | tf_op jit(solution)/shard_map/ppermute | solution.py:439
  52.5 9.7 %collective-permute-start.8 = (bf16[8,128,128]{2,1,0:T(8,128)(2,1)S(1)}, bf16[8,128,128]{2,1,0:T(8,128)(2,1)S(1)}, u32[]{:S(2)}, u32[]{:S(2)}) collective-permute-start(bf16[8,128,128]{2,1,0:T(8,128)(2,1)S(1)} %get-tuple-element.31), channel_id=1, source_target_pairs={{0,8},{4,12},{8,0},{12,4},{16,24},{20,28},{24,16},{28,20},{1,9},{5... | collective-permute-start | bytes 786440 | tf_op jit(solution)/shard_map/ppermute | solution.py:439
  53.3 9.0 %collective-permute-start.9 = (bf16[8,128,128]{2,1,0:T(8,128)(2,1)S(1)}, bf16[8,128,128]{2,1,0:T(8,128)(2,1)S(1)}, u32[]{:S(2)}, u32[]{:S(2)}) collective-permute-start(bf16[8,128,128]{2,1,0:T(8,128)(2,1)S(1)} %get-tuple-element.32), channel_id=1, source_target_pairs={{0,4},{4,0},{8,16},{12,20},{16,8},{20,12},{24,28},{28,24},{1,5},{5... | collective-permute-start | bytes 786440 | tf_op jit(solution)/shard_map/ppermute | solution.py:439
  63.7 4.3 %collective-permute-start.16 = (f32[128,128]{1,0:T(8,128)S(1)}, f32[128,128]{1,0:T(8,128)S(1)}, u32[]{:S(2)}, u32[]{:S(2)}) collective-permute-start(f32[128,128]{1,0:T(8,128)S(1)} %get-tuple-element.39), channel_id=1, source_target_pairs={{0,8},{4,12},{8,0},{12,4},{16,24},{20,28},{24,16},{28,20},{1,9},{5... | collective-permute-start | bytes 196616 | tf_op jit(solution)/shard_map/ppermute | solution.py:500
  68.1 5.3 %collective-permute-start.17 = (f32[128,128]{1,0:T(8,128)S(1)}, f32[128,128]{1,0:T(8,128)S(1)}, u32[]{:S(2)}, u32[]{:S(2)}) collective-permute-start(f32[128,128]{1,0:T(8,128)S(1)} %add.18), channel_id=1, source_target_pairs={{0,16},{4,20},{8,24},{12,28},{16,0},{20,4},{24,8},{28,12},{1,17},{... | collective-permute-start | bytes 196616 | tf_op jit(solution)/shard_map/ppermute | solution.py:500
  70.8 9.2 %collective-permute-start.22 = (bf16[8,128,128]{2,1,0:T(8,128)(2,1)S(1)}, bf16[8,128,128]{2,1,0:T(8,128)(2,1)S(1)}, u32[]{:S(2)}, u32[]{:S(2)}) collective-permute-start(bf16[8,128,128]{2,1,0:T(8,128)(2,1)S(1)} %get-tuple-element.42.rest_0_), channel_id=1, source_target_pairs={{0,8},{4,12},{8,0},{12,4},{16,24},{20,28},{24,16},{28,20},{1,9},{5... | collective-permute-start | bytes 786440 | tf_op jit(solution)/shard_map/ppermute | solution.py:439
  72.5 10.9 %collective-permute-start.26 = (bf16[8,128,128]{2,1,0:T(8,128)(2,1)S(1)}, bf16[8,128,128]{2,1,0:T(8,128)(2,1)S(1)}, u32[]{:S(2)}, u32[]{:S(2)}) collective-permute-start(bf16[8,128,128]{2,1,0:T(8,128)(2,1)S(1)} %get-tuple-element.43.rest_2_), channel_id=1, source_target_pairs={{0,8},{4,12},{8,0},{12,4},{16,24},{20,28},{24,16},{28,20},{1,9},{5... | collective-permute-start | bytes 786440 | tf_op jit(solution)/shard_map/ppermute | solution.py:439
  72.8 10.6 %collective-permute-start.30 = (bf16[8,128,128]{2,1,0:T(8,128)(2,1)S(1)}, bf16[8,128,128]{2,1,0:T(8,128)(2,1)S(1)}, u32[]{:S(2)}, u32[]{:S(2)}) collective-permute-start(bf16[8,128,128]{2,1,0:T(8,128)(2,1)S(1)} %get-tuple-element.42.rest_0_), channel_id=1, source_target_pairs={{0,4},{4,0},{8,16},{12,20},{16,8},{20,12},{24,28},{28,24},{1,5},{5... | collective-permute-start | bytes 786440 | tf_op jit(solution)/shard_map/ppermute | solution.py:439
  72.8 11.1 %collective-permute-start.34 = (bf16[8,128,128]{2,1,0:T(8,128)(2,1)S(1)}, bf16[8,128,128]{2,1,0:T(8,128)(2,1)S(1)}, u32[]{:S(2)}, u32[]{:S(2)}) collective-permute-start(bf16[8,128,128]{2,1,0:T(8,128)(2,1)S(1)} %get-tuple-element.43.rest_2_), channel_id=1, source_target_pairs={{0,4},{4,0},{8,16},{12,20},{16,8},{20,12},{24,28},{28,24},{1,5},{5... | collective-permute-start | bytes 786440 | tf_op jit(solution)/shard_map/ppermute | solution.py:439
  73.4 13.8 %collective-permute-start.38 = (bf16[8,128,128]{2,1,0:T(8,128)(2,1)S(1)}, bf16[8,128,128]{2,1,0:T(8,128)(2,1)S(1)}, u32[]{:S(2)}, u32[]{:S(2)}) collective-permute-start(bf16[8,128,128]{2,1,0:T(8,128)(2,1)S(1)} %get-tuple-element.42.rest_0_), channel_id=1, source_target_pairs={{0,4},{4,0},{8,12},{12,8},{16,20},{20,16},{24,28},{28,24},{1,5},{5... | collective-permute-start | bytes 786440 | tf_op jit(solution)/shard_map/ppermute | solution.py:429
  80.0 7.3 %collective-permute-start.39 = (bf16[8,128,128]{2,1,0:T(8,128)(2,1)S(1)}, bf16[8,128,128]{2,1,0:T(8,128)(2,1)S(1)}, u32[]{:S(2)}, u32[]{:S(2)}) collective-permute-start(bf16[8,128,128]{2,1,0:T(8,128)(2,1)S(1)} %get-tuple-element.43.rest_2_), channel_id=1, source_target_pairs={{0,4},{4,0},{8,12},{12,8},{16,20},{20,16},{24,28},{28,24},{1,5},{5... | collective-permute-start | bytes 786440 | tf_op jit(solution)/shard_map/ppermute | solution.py:429
  83.4 4.0 %collective-permute-start.23 = (bf16[8,128,128]{2,1,0:T(8,128)(2,1)S(1)}, bf16[8,128,128]{2,1,0:T(8,128)(2,1)S(1)}, u32[]{:S(2)}, u32[]{:S(2)}) collective-permute-start(bf16[8,128,128]{2,1,0:T(8,128)(2,1)S(1)} %collective-permute-done.22.rest_4_), channel_id=1, source_target_pairs={{0,4},{4,0},{8,16},{12,20},{16,8},{20,12},{24,28},{28,24},{1,5},{5... | collective-permute-start | bytes 786440 | tf_op jit(solution)/shard_map/ppermute | solution.py:439
  83.4 4.4 %collective-permute-start.27 = (bf16[8,128,128]{2,1,0:T(8,128)(2,1)S(1)}, bf16[8,128,128]{2,1,0:T(8,128)(2,1)S(1)}, u32[]{:S(2)}, u32[]{:S(2)}) collective-permute-start(bf16[8,128,128]{2,1,0:T(8,128)(2,1)S(1)} %collective-permute-done.26.rest_8_), channel_id=1, source_target_pairs={{0,4},{4,0},{8,16},{12,20},{16,8},{20,12},{24,28},{28,24},{1,5},{5... | collective-permute-start | bytes 786440 | tf_op jit(solution)/shard_map/ppermute | solution.py:439
  83.9 10.5 %collective-permute-start.31 = (bf16[8,128,128]{2,1,0:T(8,128)(2,1)S(1)}, bf16[8,128,128]{2,1,0:T(8,128)(2,1)S(1)}, u32[]{:S(2)}, u32[]{:S(2)}) collective-permute-start(bf16[8,128,128]{2,1,0:T(8,128)(2,1)S(1)} %collective-permute-done.30.rest_6_), channel_id=1, source_target_pairs={{0,8},{4,12},{8,0},{12,4},{16,24},{20,28},{24,16},{28,20},{1,9},{5... | collective-permute-start | bytes 786440 | tf_op jit(solution)/shard_map/ppermute | solution.py:439
  87.2 10.6 %collective-permute-start.35 = (bf16[8,128,128]{2,1,0:T(8,128)(2,1)S(1)}, bf16[8,128,128]{2,1,0:T(8,128)(2,1)S(1)}, u32[]{:S(2)}, u32[]{:S(2)}) collective-permute-start(bf16[8,128,128]{2,1,0:T(8,128)(2,1)S(1)} %collective-permute-done.34.rest_10_), channel_id=1, source_target_pairs={{0,8},{4,12},{8,0},{12,4},{16,24},{20,28},{24,16},{28,20},{1,9},{5... | collective-permute-start | bytes 786440 | tf_op jit(solution)/shard_map/ppermute | solution.py:439
  87.3 10.8 %collective-permute-start.40 = (bf16[8,128,128]{2,1,0:T(8,128)(2,1)S(1)}, bf16[8,128,128]{2,1,0:T(8,128)(2,1)S(1)}, u32[]{:S(2)}, u32[]{:S(2)}) collective-permute-start(bf16[8,128,128]{2,1,0:T(8,128)(2,1)S(1)} %collective-permute-done.22.rest_4_), channel_id=1, source_target_pairs={{0,4},{4,0},{8,12},{12,8},{16,20},{20,16},{24,28},{28,24},{1,5},{5... | collective-permute-start | bytes 786440 | tf_op jit(solution)/shard_map/ppermute | solution.py:429
  87.3 10.8 %collective-permute-start.41 = (bf16[8,128,128]{2,1,0:T(8,128)(2,1)S(1)}, bf16[8,128,128]{2,1,0:T(8,128)(2,1)S(1)}, u32[]{:S(2)}, u32[]{:S(2)}) collective-permute-start(bf16[8,128,128]{2,1,0:T(8,128)(2,1)S(1)} %collective-permute-done.30.rest_6_), channel_id=1, source_target_pairs={{0,4},{4,0},{8,12},{12,8},{16,20},{20,16},{24,28},{28,24},{1,5},{5... | collective-permute-start | bytes 786440 | tf_op jit(solution)/shard_map/ppermute | solution.py:429
  87.8 12.2 %collective-permute-start.42 = (bf16[8,128,128]{2,1,0:T(8,128)(2,1)S(1)}, bf16[8,128,128]{2,1,0:T(8,128)(2,1)S(1)}, u32[]{:S(2)}, u32[]{:S(2)}) collective-permute-start(bf16[8,128,128]{2,1,0:T(8,128)(2,1)S(1)} %collective-permute-done.26.rest_8_), channel_id=1, source_target_pairs={{0,4},{4,0},{8,12},{12,8},{16,20},{20,16},{24,28},{28,24},{1,5},{5... | collective-permute-start | bytes 786440 | tf_op jit(solution)/shard_map/ppermute | solution.py:429
  94.4 5.8 %collective-permute-start.43 = (bf16[8,128,128]{2,1,0:T(8,128)(2,1)S(1)}, bf16[8,128,128]{2,1,0:T(8,128)(2,1)S(1)}, u32[]{:S(2)}, u32[]{:S(2)}) collective-permute-start(bf16[8,128,128]{2,1,0:T(8,128)(2,1)S(1)} %collective-permute-done.34.rest_10_), channel_id=1, source_target_pairs={{0,4},{4,0},{8,12},{12,8},{16,20},{20,16},{24,28},{28,24},{1,5},{5... | collective-permute-start | bytes 786440 | tf_op jit(solution)/shard_map/ppermute | solution.py:429
  97.8 9.2 %collective-permute-start.24 = (bf16[8,128,128]{2,1,0:T(8,128)(2,1)S(1)}, bf16[8,128,128]{2,1,0:T(8,128)(2,1)S(1)}, u32[]{:S(2)}, u32[]{:S(2)}) collective-permute-start(bf16[8,128,128]{2,1,0:T(8,128)(2,1)S(1)} %collective-permute-done.23.rest_2_), channel_id=1, source_target_pairs={{0,8},{4,12},{8,0},{12,4},{16,24},{20,28},{24,16},{28,20},{1,9},{5... | collective-permute-start | bytes 786440 | tf_op jit(solution)/shard_map/ppermute | solution.py:439
  98.1 18.2 %collective-permute-start.33 = (bf16[8,128,128]{2,1,0:T(8,128)(2,1)S(1)}, bf16[8,128,128]{2,1,0:T(8,128)(2,1)S(1)}, u32[]{:S(2)}, u32[]{:S(2)}) collective-permute-start(bf16[8,128,128]{2,1,0:T(8,128)(2,1)S(1)} %collective-permute-done.23.rest_2_), channel_id=1, source_target_pairs={{0,4},{4,0},{8,12},{12,8},{16,20},{20,16},{24,28},{28,24},{1,5},{5... | collective-permute-start | bytes 786440 | tf_op jit(solution)/shard_map/ppermute | solution.py:429
  98.2 14.2 %collective-permute-start.28 = (bf16[8,128,128]{2,1,0:T(8,128)(2,1)S(1)}, bf16[8,128,128]{2,1,0:T(8,128)(2,1)S(1)}, u32[]{:S(2)}, u32[]{:S(2)}) collective-permute-start(bf16[8,128,128]{2,1,0:T(8,128)(2,1)S(1)} %collective-permute-done.27.rest_6_), channel_id=1, source_target_pairs={{0,8},{4,12},{8,0},{12,4},{16,24},{20,28},{24,16},{28,20},{1,9},{5... | collective-permute-start | bytes 786440 | tf_op jit(solution)/shard_map/ppermute | solution.py:439
  100.0 17.0 %collective-permute-start.37 = (bf16[8,128,128]{2,1,0:T(8,128)(2,1)S(1)}, bf16[8,128,128]{2,1,0:T(8,128)(2,1)S(1)}, u32[]{:S(2)}, u32[]{:S(2)}) collective-permute-start(bf16[8,128,128]{2,1,0:T(8,128)(2,1)S(1)} %collective-permute-done.27.rest_6_), channel_id=1, source_target_pairs={{0,4},{4,0},{8,12},{12,8},{16,20},{20,16},{24,28},{28,24},{1,5},{5... | collective-permute-start | bytes 786440 | tf_op jit(solution)/shard_map/ppermute | solution.py:429
  100.2 16.2 %collective-permute-start.32 = (bf16[8,128,128]{2,1,0:T(8,128)(2,1)S(1)}, bf16[8,128,128]{2,1,0:T(8,128)(2,1)S(1)}, u32[]{:S(2)}, u32[]{:S(2)}) collective-permute-start(bf16[8,128,128]{2,1,0:T(8,128)(2,1)S(1)} %collective-permute-done.31.rest_0_), channel_id=1, source_target_pairs={{0,4},{4,0},{8,12},{12,8},{16,20},{20,16},{24,28},{28,24},{1,5},{5... | collective-permute-start | bytes 786440 | tf_op jit(solution)/shard_map/ppermute | solution.py:429
  107.0 10.0 %collective-permute-start.36 = (bf16[8,128,128]{2,1,0:T(8,128)(2,1)S(1)}, bf16[8,128,128]{2,1,0:T(8,128)(2,1)S(1)}, u32[]{:S(2)}, u32[]{:S(2)}) collective-permute-start(bf16[8,128,128]{2,1,0:T(8,128)(2,1)S(1)} %collective-permute-done.35.rest_4_), channel_id=1, source_target_pairs={{0,4},{4,0},{8,12},{12,8},{16,20},{20,16},{24,28},{28,24},{1,5},{5... | collective-permute-start | bytes 786440 | tf_op jit(solution)/shard_map/ppermute | solution.py:429
  112.4 16.6 %collective-permute-start.20 = (f32[128,128]{1,0:T(8,128)S(1)}, f32[128,128]{1,0:T(8,128)S(1)}, u32[]{:S(2)}, u32[]{:S(2)}) collective-permute-start(f32[128,128]{1,0:T(8,128)S(1)} %add.19), channel_id=1, source_target_pairs={{0,3},{1,0},{2,1},{3,2},{4,7},{5,4},{6,5},{7,6},{8,11},{9,8},{10,9... | collective-permute-start | bytes 196616 | tf_op jit(solution)/shard_map/ppermute | solution.py:400
  116.3 14.2 %collective-permute-start.19 = (f32[128,128]{1,0:T(8,128)S(1)}, f32[128,128]{1,0:T(8,128)S(1)}, u32[]{:S(2)}, u32[]{:S(2)}) collective-permute-start(f32[128,128]{1,0:T(8,128)S(1)} %add.19), channel_id=1, source_target_pairs={{0,2},{1,3},{2,0},{3,1},{4,6},{5,7},{6,4},{7,5},{8,10},{9,11},{10,... | collective-permute-start | bytes 196616 | tf_op jit(solution)/shard_map/ppermute | solution.py:400
  116.3 14.2 %collective-permute-start.18 = (f32[128,128]{1,0:T(8,128)S(1)}, f32[128,128]{1,0:T(8,128)S(1)}, u32[]{:S(2)}, u32[]{:S(2)}) collective-permute-start(f32[128,128]{1,0:T(8,128)S(1)} %add.19), channel_id=1, source_target_pairs={{0,1},{1,2},{2,3},{3,0},{4,5},{5,6},{6,7},{7,4},{8,9},{9,10},{10,1... | collective-permute-start | bytes 196616 | tf_op jit(solution)/shard_map/ppermute | solution.py:400
  117.0 4.7 %collective-permute-start.25 = (bf16[8,128,128]{2,1,0:T(8,128)(2,1)S(1)}, bf16[8,128,128]{2,1,0:T(8,128)(2,1)S(1)}, u32[]{:S(2)}, u32[]{:S(2)}) collective-permute-start(bf16[8,128,128]{2,1,0:T(8,128)(2,1)S(1)} %collective-permute-done.24.rest_0_), channel_id=1, source_target_pairs={{0,4},{4,0},{8,12},{12,8},{16,20},{20,16},{24,28},{28,24},{1,5},{5... | collective-permute-start | bytes 786440 | tf_op jit(solution)/shard_map/ppermute | solution.py:429
  117.0 4.7 %collective-permute-start.29 = (bf16[8,128,128]{2,1,0:T(8,128)(2,1)S(1)}, bf16[8,128,128]{2,1,0:T(8,128)(2,1)S(1)}, u32[]{:S(2)}, u32[]{:S(2)}) collective-permute-start(bf16[8,128,128]{2,1,0:T(8,128)(2,1)S(1)} %collective-permute-done.28.rest_2_), channel_id=1, source_target_pairs={{0,4},{4,0},{8,12},{12,8},{16,20},{20,16},{24,28},{28,24},{1,5},{5... | collective-permute-start | bytes 786440 | tf_op jit(solution)/shard_map/ppermute | solution.py:429
  125.7 15.2 %collective-permute-start.44 = (bf16[4,128,128]{2,1,0:T(8,128)(2,1)S(1)}, bf16[4,128,128]{2,1,0:T(8,128)(2,1)S(1)}, u32[]{:S(2)}, u32[]{:S(2)}) collective-permute-start(bf16[4,128,128]{2,1,0:T(8,128)(2,1)S(1)} %get-tuple-element.45), channel_id=1, source_target_pairs={{0,1},{1,0},{2,3},{3,2},{4,5},{5,4},{6,7},{7,6},{8,9},{9,8},{10,11... | collective-permute-start | bytes 393224 | tf_op jit(solution)/shard_map/ppermute | solution.py:519
  128.9 11.9 %collective-permute-start.45 = (bf16[4,128,128]{2,1,0:T(8,128)(2,1)S(1)}, bf16[4,128,128]{2,1,0:T(8,128)(2,1)S(1)}, u32[]{:S(2)}, u32[]{:S(2)}) collective-permute-start(bf16[4,128,128]{2,1,0:T(8,128)(2,1)S(1)} %get-tuple-element.46), channel_id=1, source_target_pairs={{0,2},{1,3},{2,0},{3,1},{4,6},{5,7},{6,4},{7,5},{8,10},{9,11},{10,... | collective-permute-start | bytes 393224 | tf_op jit(solution)/shard_map/ppermute | solution.py:519
  129.0 11.9 %collective-permute-start.46 = (bf16[4,128,128]{2,1,0:T(8,128)(2,1)S(1)}, bf16[4,128,128]{2,1,0:T(8,128)(2,1)S(1)}, u32[]{:S(2)}, u32[]{:S(2)}) collective-permute-start(bf16[4,128,128]{2,1,0:T(8,128)(2,1)S(1)} %get-tuple-element.47), channel_id=1, source_target_pairs={{0,3},{1,2},{2,1},{3,0},{4,7},{5,6},{6,5},{7,4},{8,11},{9,10},{10,... | collective-permute-start | bytes 393224 | tf_op jit(solution)/shard_map/ppermute | solution.py:519
  130.5 1.3 collective-permute-start.21
  (1 other events, 0.6 us)

commit v5 on v4

--- a/solution.py
+++ b/solution.py
@@ -68,7 +68,10 @@
 CLASSES = 5
 
 
-def lists_kernel(strips, tpi, chips, ints_ref, lists_ref):
+def lists_kernel(strips, tpi, chips, given_ref, ints_ref, lists_ref, sem):
+    copy = pltpu.make_async_copy(given_ref, ints_ref, sem)
+    copy.start()
+    copy.wait()
     ints = Ints(ints_ref, strips, tpi)
     chip = ints.me() // 2
     far = far_chip(chip, chips)
@@ -107,21 +110,21 @@
 
         lax.fori_loop(0, self.count, begin, jnp.int32(0))
 
-    def in_batches(self, tiles_ref, buf_ref, sems, work):
+    def in_batches(self, tiles_ref, buf_ref, sems, work, batch=BATCH):
         def trip(b, carry):
-            for i in range(BATCH):
-                at = b * BATCH + i
+            for i in range(batch):
+                at = b * batch + i
 
                 @pl.when(at < self.count)
                 def _():
                     pltpu.make_async_copy(tiles_ref.at[0], buf_ref.at[at], sems.at[at]).wait()
 
-            for i in range(BATCH):
-                at = jnp.minimum(b * BATCH + i, self.count - 1)
-                work(self.strip(at), at, (b * BATCH + i < self.count).astype(F32))
+            for i in range(batch):
+                at = jnp.minimum(b * batch + i, self.count - 1)
+                work(self.strip(at), at, (b * batch + i < self.count).astype(F32))
             return carry
 
-        lax.fori_loop(0, (self.count + BATCH - 1) // BATCH, trip, jnp.int32(0))
+        lax.fori_loop(0, (self.count + batch - 1) // batch, trip, jnp.int32(0))
 
 
 def sketch_kernel(far_only, chips, blocks, n_src, ints_ref, lists_ref, tiles_ref, *rest):
@@ -154,7 +157,7 @@
         right = jnp.concatenate([omega_ref[ints.column(strip, j)] for j in range(tpi)], axis=0)
         both_ref[block] += jnp.dot(left, right, preferred_element_type=F32) * valid
 
-    picked.in_batches(tiles_ref, buf_ref, sems, work)
+    picked.in_batches(tiles_ref, buf_ref, sems, work, BATCH if far_only else 2 * BATCH)
     size = half // len(theirs)
     for p, out in enumerate(theirs):
         out[...] = both_ref[pl.ds(half + p * size, size)].astype(BF16)
@@ -418,10 +421,14 @@
                            + [tile_col[:, j] for j in range(tpi)]).astype(jnp.int32)
     ints = far_off(ints)
 
-    lists = far_off(pl.pallas_call(
+    ints, lists = pl.pallas_call(
         functools.partial(lists_kernel, strips, tpi, chips),
-        out_shape=jax.ShapeDtypeStruct((CLASSES * (strips + 1),), jnp.int32), in_specs=[SM],
-        out_specs=SM, compiler_params=params(1), name="lists")(ints))
+        out_shape=(pltpu.SMEM(ints.shape, jnp.int32),
+                   pltpu.SMEM((CLASSES * (strips + 1),), jnp.int32)),
+        in_specs=[HB], out_specs=(SM, SM), scratch_shapes=[pltpu.SemaphoreType.DMA],
+        compiler_params=params(1), name="lists")(ints)
+    ints = pltpu.with_memory_space_constraint(ints, pltpu.SMEM)
+    lists = pltpu.with_memory_space_constraint(lists, pltpu.SMEM)
     scalars = (ints, lists)
     swap_links = [(i, i ^ 1) for i in range(n_group)]
 

time: 142 us -> 136 us (0.958)
  Pallas kernels: 43.4 us -> 34.3 us
  waiting for transfers between devices: 60.2 us -> 64.7 us
    pallas_call x12, Pallas kernels: 16.9 us -> 12.6 us  [on_chip(): pl.pallas_call(kernel, out_shape=out_shape, in_specs=specs, out_specs=jax...]
    ppermute x20, waiting for transfers between devices: 52.7 us -> 56.2 us  [over(): return lax.ppermute(x, 'group', links)]
    pallas_call x3, Pallas kernels: 13.5 us -> 11.1 us  [project(): pl.pallas_call(functools.partial(project_kernel, own_class, chips, owned,...]
    pallas_call x2, Pallas kernels: 10.5 us -> 8.61 us  [partial_sketch(): pl.pallas_call(functools.partial(sketch_kernel, far_only, chips, blocks,...]
  transfers between devices with their start and end apart: 47 -> 47, of which waited for: 16 -> 15; matrix products, arithmetic and copies ran while one was open for 2% -> 2% of each run, Pallas kernels for 21% -> 18%
where the time goes in v5:
time: 136 us
  waiting for transfers between devices  64.7 us (48%)
  Pallas kernels  34.3 us (25%)
  starting transfers between devices  32.9 us (24%)
  local copies, waits for them, and re-layouts  2.22 us (2%)
  between operations  1.58 us (1%)
    ppermute x20, waiting for transfers between devices, over(): return lax.ppermute(x, 'group', links)  56.2 us
    ppermute x20, starting transfers between devices, over(): return lax.ppermute(x, 'group', links)  13.6 us
    pallas_call x12, Pallas kernels, on_chip(): pl.pallas_call(kernel, out_shape=out_shape, in_specs=specs, out_specs=jax...  12.6 us
    pallas_call x3, Pallas kernels, project(): pl.pallas_call(functools.partial(project_kernel, own_class, chips, owned,...  11.1 us
    pallas_call x2, Pallas kernels, partial_sketch(): pl.pallas_call(functools.partial(sketch_kernel, far_only, chips, blocks,...  8.61 us
    ppermute x3, starting transfers between devices, on_device(): lax.ppermute(parts[s], 'dev', partners(n_dev, s))  4.8 us
    ppermute x3, starting transfers between devices, on_device(): lax.ppermute(own_omega, 'dev', partners(n_dev, s))  4.57 us
    ppermute x3, starting transfers between devices, exchanges(): lax.ppermute(x, axis, [(i, i // span * span + (i + k * s) % span) for i i...  3.72 us
  transfers between devices with their start and end apart: 47, of which 15 were waited for; matrix products, arithmetic and copies ran while one was open for 2% of the time, Pallas kernels for 18%

profile of v5, /device:TPU:0, one launch (start us, length us, event | category | flops | bytes accessed | tf_op | source)
XLA Modules:
  0.0 135.6 jit_solution(4739712420451474552)
XLA Ops:
  0.6 3.0 %collective-permute-start = (bf16[4,128,128]{2,1,0:T(8,128)(2,1)}, bf16[4,128,128]{2,1,0:T(8,128)(2,1)S(1)}, u32[]{:S(2)}, u32[]{:S(2)}) collective-permute-start(bf16[4,128,128]{2,1,0:T(8,128)(2,1)} %bitcast.18), channel_id=1, source_target_pairs={{0,1},{1,0},{2,3},{3,2},{4,5},{5,4},{6,7},{7,6},{8,9},{9,8},{10,11... | collective-permute-start | bytes 393224 | tf_op jit(solution)/shard_map/ppermute | solution.py:450
  3.7 1.5 %collective-permute-start.1 = (bf16[4,128,128]{2,1,0:T(8,128)(2,1)}, bf16[4,128,128]{2,1,0:T(8,128)(2,1)S(1)}, u32[]{:S(2)}, u32[]{:S(2)}) collective-permute-start(bf16[4,128,128]{2,1,0:T(8,128)(2,1)} %bitcast.19), channel_id=1, source_target_pairs={{0,2},{1,3},{2,0},{3,1},{4,6},{5,7},{6,4},{7,5},{8,10},{9,11},{10,... | collective-permute-start | bytes 393224 | tf_op jit(solution)/shard_map/ppermute | solution.py:450
  5.9 0.9 slice_bitcast_fusion
  6.7 1.3 concatenate.3.given_ref
  8.1 1.9 %lists.1 = (s32[507]{0:T(512)S(4)}, s32[365]{0:T(512)S(4)}) custom-call(s32[507]{0:T(512)} %concatenate.3.given_ref), custom_call_target="tpu_custom_call" | custom-call | tf_op jit(solution)/shard_map/lists/pallas_call | solution.py:424
  10.0 1.6 %collective-permute-done.1.rest_2_ = bf16[4,128,128]{2,1,0:T(8,128)(2,1)S(1)} collective-permute-done((bf16[4,128,128]{2,1,0:T(8,128)(2,1)}, bf16[4,128,128]{2,1,0:T(8,128)(2,1)S(1)}, u32[]{:S(2)}, u32[]{:S(2)}) %collective-permute-start.1) | collective-permute-done | bytes 131104 | tf_op jit(solution)/shard_map/ppermute | solution.py:450
  11.7 3.3 %sketch_far.1 = (f32[32,128,128]{2,1,0:T(8,128)S(1)}, bf16[16,128,128]{2,1,0:T(8,128)(2,1)S(1)}) custom-call(s32[507]{0:T(512)S(4)} %get-tuple-element.27.ints_ref, s32[365]{0:T(512)S(4)} %get-tuple-element.28.lists_ref, bf16[72,5,128,128]{3,2,1,0:T(8,128)(2,1)} %tiles_ref.9, bf16[4,128,128]{2,1,0:T(8,128)(2,1)} %bitcast.21, ...), custom_call_target="tpu_custom_call" | custom-call | flops 4831838208 | bytes 9437184 | tf_op jit(solution)/shard_map/sketch_far/pallas_call | solution.py:171
  15.0 1.9 %collective-permute-done.3.pair_ref.far_pair = bf16[16,128,128]{2,1,0:T(8,128)(2,1)S(1)} collective-permute-done((bf16[16,128,128]{2,1,0:T(8,128)(2,1)S(1)}, bf16[16,128,128]{2,1,0:T(8,128)(2,1)S(1)}, u32[]{:S(2)}, u32[]{:S(2)}) %collective-permute-start.3) | collective-permute-done | bytes 524320 | tf_op jit(solution)/shard_map/ppermute | solution.py:436
  17.0 5.3 %sketch_rest.1 = (f32[96,128,128]{2,1,0:T(8,128)S(1)}, bf16[24,128,128]{2,1,0:T(8,128)(2,1)S(1)}, bf16[24,128,128]{2,1,0:T(8,128)(2,1)S(1)}) custom-call(s32[507]{0:T(512)S(4)} %get-tuple-element.27.ints_ref, s32[365]{0:T(512)S(4)} %get-tuple-element.28.lists_ref, bf16[72,5,128,128]{3,2,1,0:T(8,128)(2,1)} %tiles_ref.9, bf16[4,128,128]{2,1,0:T(8,128)(2,1)} %bitcast.22, ...), custom_call_target="tpu_custom_call" | custom-call | flops 19327352832 | bytes 37748736 | tf_op jit(solution)/shard_map/sketch_rest/pallas_call | solution.py:171
  22.4 0.7 collective-permute-start.10
  23.2 0.7 collective-permute-start.11
  23.9 1.3 collective-permute-start.5
  25.2 7.2 %collective-permute-done.11.even_in.odd_in = bf16[8,128,128]{2,1,0:T(8,128)(2,1)S(1)} collective-permute-done((bf16[8,128,128]{2,1,0:T(8,128)(2,1)S(1)}, bf16[8,128,128]{2,1,0:T(8,128)(2,1)S(1)}, u32[]{:S(2)}, u32[]{:S(2)}) %collective-permute-start.11) | collective-permute-done | bytes 262176 | tf_op jit(solution)/shard_map/ppermute | solution.py:446
  32.6 0.8 collective-permute-start.12
  33.3 4.6 %collective-permute-done.5.even_in.odd_in = bf16[8,128,128]{2,1,0:T(8,128)(2,1)S(1)} collective-permute-done((bf16[8,128,128]{2,1,0:T(8,128)(2,1)S(1)}, bf16[8,128,128]{2,1,0:T(8,128)(2,1)S(1)}, u32[]{:S(2)}, u32[]{:S(2)}) %collective-permute-start.5) | collective-permute-done | bytes 262176 | tf_op jit(solution)/shard_map/ppermute | solution.py:446
  38.2 0.8 collective-permute-start.6
  39.0 4.6 %collective-permute-done.12.even_in = bf16[8,128,128]{2,1,0:T(8,128)(2,1)S(1)} collective-permute-done((bf16[8,128,128]{2,1,0:T(8,128)(2,1)S(1)}, bf16[8,128,128]{2,1,0:T(8,128)(2,1)S(1)}, u32[]{:S(2)}, u32[]{:S(2)}) %collective-permute-start.12) | collective-permute-done | bytes 262176 | tf_op jit(solution)/shard_map/ppermute | solution.py:446
  43.8 0.8 collective-permute-start.14
  44.6 4.6 %collective-permute-done.6.even_in = bf16[8,128,128]{2,1,0:T(8,128)(2,1)S(1)} collective-permute-done((bf16[8,128,128]{2,1,0:T(8,128)(2,1)S(1)}, bf16[8,128,128]{2,1,0:T(8,128)(2,1)S(1)}, u32[]{:S(2)}, u32[]{:S(2)}) %collective-permute-start.6) | collective-permute-done | bytes 262176 | tf_op jit(solution)/shard_map/ppermute | solution.py:446
  49.4 0.8 collective-permute-start.8
  50.2 4.6 %collective-permute-done.14.even_ref = bf16[8,128,128]{2,1,0:T(8,128)(2,1)S(1)} collective-permute-done((bf16[8,128,128]{2,1,0:T(8,128)(2,1)S(1)}, bf16[8,128,128]{2,1,0:T(8,128)(2,1)S(1)}, u32[]{:S(2)}, u32[]{:S(2)}) %collective-permute-start.14) | collective-permute-done | bytes 262176 | tf_op jit(solution)/shard_map/ppermute | solution.py:446
  54.8 0.8 shard_map.92
  55.6 4.3 %collective-permute-done.8.even_ref = bf16[8,128,128]{2,1,0:T(8,128)(2,1)S(1)} collective-permute-done((bf16[8,128,128]{2,1,0:T(8,128)(2,1)S(1)}, bf16[8,128,128]{2,1,0:T(8,128)(2,1)S(1)}, u32[]{:S(2)}, u32[]{:S(2)}) %collective-permute-start.8) | collective-permute-done | bytes 262176 | tf_op jit(solution)/shard_map/ppermute | solution.py:446
  59.9 0.8 shard_map.93
  60.7 0.8 collective-permute-start.16
  61.5 3.6 %collective-permute-done.16 = f32[128,128]{1,0:T(8,128)S(1)} collective-permute-done((f32[128,128]{1,0:T(8,128)S(1)}, f32[128,128]{1,0:T(8,128)S(1)}, u32[]{:S(2)}, u32[]{:S(2)}) %collective-permute-start.16) | collective-permute-done | bytes 65568 | tf_op jit(solution)/shard_map/ppermute | solution.py:507
  65.0 2.8 %collective-permute-start.17 = (f32[128,128]{1,0:T(8,128)S(1)}, f32[128,128]{1,0:T(8,128)S(1)}, u32[]{:S(2)}, u32[]{:S(2)}) collective-permute-start(f32[128,128]{1,0:T(8,128)S(1)} %add.18), channel_id=1, source_target_pairs={{0,16},{4,20},{8,24},{12,28},{16,0},{20,4},{24,8},{28,12},{1,17},{... | collective-permute-start | bytes 196616 | tf_op jit(solution)/shard_map/ppermute | solution.py:507
  67.8 1.7 %collective-permute-start.22 = (bf16[8,128,128]{2,1,0:T(8,128)(2,1)S(1)}, bf16[8,128,128]{2,1,0:T(8,128)(2,1)S(1)}, u32[]{:S(2)}, u32[]{:S(2)}) collective-permute-start(bf16[8,128,128]{2,1,0:T(8,128)(2,1)S(1)} %get-tuple-element.46.rest_0_), channel_id=1, source_target_pairs={{0,8},{4,12},{8,0},{12,4},{16,24},{20,28},{24,16},{28,20},{1,9},{5... | collective-permute-start | bytes 786440 | tf_op jit(solution)/shard_map/ppermute | solution.py:446
  70.4 6.6 %collective-permute-done.22.rest_4_ = bf16[8,128,128]{2,1,0:T(8,128)(2,1)S(1)} collective-permute-done((bf16[8,128,128]{2,1,0:T(8,128)(2,1)S(1)}, bf16[8,128,128]{2,1,0:T(8,128)(2,1)S(1)}, u32[]{:S(2)}, u32[]{:S(2)}) %collective-permute-start.22) | collective-permute-done | bytes 262176 | tf_op jit(solution)/shard_map/ppermute | solution.py:446
  77.0 3.4 %collective-permute-done.26.rest_8_ = bf16[8,128,128]{2,1,0:T(8,128)(2,1)S(1)} collective-permute-done((bf16[8,128,128]{2,1,0:T(8,128)(2,1)S(1)}, bf16[8,128,128]{2,1,0:T(8,128)(2,1)S(1)}, u32[]{:S(2)}, u32[]{:S(2)}) %collective-permute-start.26) | collective-permute-done | bytes 262176 | tf_op jit(solution)/shard_map/ppermute | solution.py:446
  80.4 0.5 collective-permute-start.27
  80.9 3.3 %collective-permute-start.31 = (bf16[8,128,128]{2,1,0:T(8,128)(2,1)S(1)}, bf16[8,128,128]{2,1,0:T(8,128)(2,1)S(1)}, u32[]{:S(2)}, u32[]{:S(2)}) collective-permute-start(bf16[8,128,128]{2,1,0:T(8,128)(2,1)S(1)} %collective-permute-done.30.rest_6_), channel_id=1, source_target_pairs={{0,8},{4,12},{8,0},{12,4},{16,24},{20,28},{24,16},{28,20},{1,9},{5... | collective-permute-start | bytes 786440 | tf_op jit(solution)/shard_map/ppermute | solution.py:446
  84.9 6.5 %collective-permute-done.31.rest_0_ = bf16[8,128,128]{2,1,0:T(8,128)(2,1)S(1)} collective-permute-done((bf16[8,128,128]{2,1,0:T(8,128)(2,1)S(1)}, bf16[8,128,128]{2,1,0:T(8,128)(2,1)S(1)}, u32[]{:S(2)}, u32[]{:S(2)}) %collective-permute-start.31) | collective-permute-done | bytes 262176 | tf_op jit(solution)/shard_map/ppermute | solution.py:446
  91.4 3.4 %collective-permute-done.35.rest_4_ = bf16[8,128,128]{2,1,0:T(8,128)(2,1)S(1)} collective-permute-done((bf16[8,128,128]{2,1,0:T(8,128)(2,1)S(1)}, bf16[8,128,128]{2,1,0:T(8,128)(2,1)S(1)}, u32[]{:S(2)}, u32[]{:S(2)}) %collective-permute-start.35) | collective-permute-done | bytes 262176 | tf_op jit(solution)/shard_map/ppermute | solution.py:446
  95.2 1.8 %collective-permute-start.28 = (bf16[8,128,128]{2,1,0:T(8,128)(2,1)S(1)}, bf16[8,128,128]{2,1,0:T(8,128)(2,1)S(1)}, u32[]{:S(2)}, u32[]{:S(2)}) collective-permute-start(bf16[8,128,128]{2,1,0:T(8,128)(2,1)S(1)} %collective-permute-done.27.rest_6_), channel_id=1, source_target_pairs={{0,8},{4,12},{8,0},{12,4},{16,24},{20,28},{24,16},{28,20},{1,9},{5... | collective-permute-start | bytes 786440 | tf_op jit(solution)/shard_map/ppermute | solution.py:446
  97.5 6.5 %collective-permute-done.24.rest_0_ = bf16[8,128,128]{2,1,0:T(8,128)(2,1)S(1)} collective-permute-done((bf16[8,128,128]{2,1,0:T(8,128)(2,1)S(1)}, bf16[8,128,128]{2,1,0:T(8,128)(2,1)S(1)}, u32[]{:S(2)}, u32[]{:S(2)}) %collective-permute-start.24) | collective-permute-done | bytes 262176 | tf_op jit(solution)/shard_map/ppermute | solution.py:446
  104.0 4.6 %shard_map.97.rest_8_ = f32[16,128,128]{2,1,0:T(8,128)S(1)} custom-call(s32[507]{0:T(512)S(4)} %get-tuple-element.27.ints_ref, s32[365]{0:T(512)S(4)} %get-tuple-element.28.lists_ref, bf16[72,5,128,128]{3,2,1,0:T(8,128)(2,1)} %tiles_ref.9, bf16[8,128,128]{2,1,0:T(8,128)(2,1)S(1)} %get-tuple-element.46.rest_0_, ...), custom_call_target="tpu_custom_call" | custom-call | flops 6442450944 | bytes 12582912 | tf_op jit(solution)/shard_map/pallas_call | solution.py:350
  108.6 3.1 %collective-permute-start.20 = (f32[128,128]{1,0:T(8,128)S(1)}, f32[128,128]{1,0:T(8,128)S(1)}, u32[]{:S(2)}, u32[]{:S(2)}) collective-permute-start(f32[128,128]{1,0:T(8,128)S(1)} %add.19), channel_id=1, source_target_pairs={{0,3},{1,0},{2,1},{3,2},{4,7},{5,4},{6,5},{7,6},{8,11},{9,8},{10,9... | collective-permute-start | bytes 196616 | tf_op jit(solution)/shard_map/ppermute | solution.py:403
  111.7 0.6 collective-permute-start.18
  112.9 3.2 %shard_map.98.rest_4_ = f32[16,128,128]{2,1,0:T(8,128)S(1)} custom-call(s32[507]{0:T(512)S(4)} %get-tuple-element.27.ints_ref, s32[365]{0:T(512)S(4)} %get-tuple-element.28.lists_ref, bf16[72,5,128,128]{3,2,1,0:T(8,128)(2,1)} %tiles_ref.9, bf16[8,128,128]{2,1,0:T(8,128)(2,1)S(1)} %collective-permute-done.31.rest_0_, ...), custom_call_target="tpu_custom_call" | custom-call | flops 6442450944 | bytes 12582912 | tf_op jit(solution)/shard_map/pallas_call | solution.py:350
  116.2 3.3 %shard_map.99 = (f32[4,128,128]{2,1,0:T(8,128)S(1)}, bf16[4,128,128]{2,1,0:T(8,128)(2,1)S(1)}, bf16[4,128,128]{2,1,0:T(8,128)(2,1)S(1)}, bf16[4,128,128]{2,1,0:T(8,128)(2,1)S(1)}) custom-call(s32[507]{0:T(512)S(4)} %get-tuple-element.27.ints_ref, s32[365]{0:T(512)S(4)} %get-tuple-element.28.lists_ref, bf16[72,5,128,128]{3,2,1,0:T(8,128)(2,1)} %tiles_ref.9, ...), custom_call_target="tpu_custom_call" | custom-call | flops 6442450944 | bytes 12582912 | tf_op jit(solution)/shard_map/pallas_call | solution.py:350
  119.4 3.3 %collective-permute-start.44 = (bf16[4,128,128]{2,1,0:T(8,128)(2,1)S(1)}, bf16[4,128,128]{2,1,0:T(8,128)(2,1)S(1)}, u32[]{:S(2)}, u32[]{:S(2)}) collective-permute-start(bf16[4,128,128]{2,1,0:T(8,128)(2,1)S(1)} %get-tuple-element.49), channel_id=1, source_target_pairs={{0,1},{1,0},{2,3},{3,2},{4,5},{5,4},{6,7},{7,6},{8,9},{9,8},{10,11... | collective-permute-start | bytes 393224 | tf_op jit(solution)/shard_map/ppermute | solution.py:526
  122.7 1.5 %collective-permute-start.46 = (bf16[4,128,128]{2,1,0:T(8,128)(2,1)S(1)}, bf16[4,128,128]{2,1,0:T(8,128)(2,1)S(1)}, u32[]{:S(2)}, u32[]{:S(2)}) collective-permute-start(bf16[4,128,128]{2,1,0:T(8,128)(2,1)S(1)} %get-tuple-element.51), channel_id=1, source_target_pairs={{0,3},{1,2},{2,1},{3,0},{4,7},{5,6},{6,5},{7,4},{8,11},{9,10},{10,... | collective-permute-start | bytes 393224 | tf_op jit(solution)/shard_map/ppermute | solution.py:526
  124.3 1.2 collective-permute-done.21
  125.6 3.4 %shard_map.94.refs_0_ = f32[128,128]{1,0:T(8,128)S(1)} custom-call(f32[128,128]{1,0:T(8,128)S(1)} %add.23.refs_0_), custom_call_target="tpu_custom_call" | custom-call | tf_op jit(solution)/shard_map/pallas_call | solution.py:379
  129.0 3.4 %shard_map.95.inverse_ref = f32[128,128]{1,0:T(8,128)S(1)} custom-call(f32[128,128]{1,0:T(8,128)S(1)} %shard_map.94.refs_0_), custom_call_target="tpu_custom_call" | custom-call | tf_op jit(solution)/shard_map/pallas_call | solution.py:379
  132.4 2.2 %shard_map.96 = f32[16,128,128]{2,1,0:T(8,128)} custom-call(f32[128,128]{1,0:T(8,128)S(1)} %shard_map.95.inverse_ref, f32[8,128,128]{2,1,0:T(8,128)S(1)} %get-tuple-element.44.rest_0_, f32[8,128,128]{2,1,0:T(8,128)S(1)} %get-tuple-element.45.rest_1_), custom_call_target="tpu_custom_call" | custom-call | tf_op jit(solution)/shard_map/pallas_call | solution.py:379
  134.6 1.0 shard_map.100
  (73 shorter events, 4.3 us)
Async XLA Ops:
  0.6 9.4 %collective-permute-start = (bf16[4,128,128]{2,1,0:T(8,128)(2,1)}, bf16[4,128,128]{2,1,0:T(8,128)(2,1)S(1)}, u32[]{:S(2)}, u32[]{:S(2)}) collective-permute-start(bf16[4,128,128]{2,1,0:T(8,128)(2,1)} %bitcast.18), channel_id=1, source_target_pairs={{0,1},{1,0},{2,3},{3,2},{4,5},{5,4},{6,7},{7,6},{8,9},{9,8},{10,11... | collective-permute-start | bytes 393224 | tf_op jit(solution)/shard_map/ppermute | solution.py:450
  3.7 8.0 %collective-permute-start.1 = (bf16[4,128,128]{2,1,0:T(8,128)(2,1)}, bf16[4,128,128]{2,1,0:T(8,128)(2,1)S(1)}, u32[]{:S(2)}, u32[]{:S(2)}) collective-permute-start(bf16[4,128,128]{2,1,0:T(8,128)(2,1)} %bitcast.19), channel_id=1, source_target_pairs={{0,2},{1,3},{2,0},{3,1},{4,6},{5,7},{6,4},{7,5},{8,10},{9,11},{10,... | collective-permute-start | bytes 393224 | tf_op jit(solution)/shard_map/ppermute | solution.py:450
  5.2 6.5 %collective-permute-start.2 = (bf16[4,128,128]{2,1,0:T(8,128)(2,1)}, bf16[4,128,128]{2,1,0:T(8,128)(2,1)S(1)}, u32[]{:S(2)}, u32[]{:S(2)}) collective-permute-start(bf16[4,128,128]{2,1,0:T(8,128)(2,1)} %bitcast.20), channel_id=1, source_target_pairs={{0,3},{1,2},{2,1},{3,0},{4,7},{5,6},{6,5},{7,4},{8,11},{9,10},{10,... | collective-permute-start | bytes 393224 | tf_op jit(solution)/shard_map/ppermute | solution.py:450
  14.9 2.0 %collective-permute-start.3 = (bf16[16,128,128]{2,1,0:T(8,128)(2,1)S(1)}, bf16[16,128,128]{2,1,0:T(8,128)(2,1)S(1)}, u32[]{:S(2)}, u32[]{:S(2)}) collective-permute-start(bf16[16,128,128]{2,1,0:T(8,128)(2,1)S(1)} %get-tuple-element.30), channel_id=1, source_target_pairs={{0,4},{4,0},{8,12},{12,8},{16,20},{20,16},{24,28},{28,24},{1,5},{5... | collective-permute-start | bytes 1572872 | tf_op jit(solution)/shard_map/ppermute | solution.py:436
  22.4 10.0 %collective-permute-start.10 = (bf16[24,128,128]{2,1,0:T(8,128)(2,1)S(1)}, bf16[24,128,128]{2,1,0:T(8,128)(2,1)S(1)}, u32[]{:S(2)}, u32[]{:S(2)}) collective-permute-start(bf16[24,128,128]{2,1,0:T(8,128)(2,1)S(1)} %get-tuple-element.37), channel_id=1, source_target_pairs={{0,4},{4,0},{8,12},{12,8},{16,20},{20,16},{24,28},{28,24},{1,5},{5... | collective-permute-start | bytes 2359304 | tf_op jit(solution)/shard_map/ppermute | solution.py:436
  23.1 14.9 %collective-permute-start.4 = (bf16[24,128,128]{2,1,0:T(8,128)(2,1)S(1)}, bf16[24,128,128]{2,1,0:T(8,128)(2,1)S(1)}, u32[]{:S(2)}, u32[]{:S(2)}) collective-permute-start(bf16[24,128,128]{2,1,0:T(8,128)(2,1)S(1)} %get-tuple-element.32), channel_id=1, source_target_pairs={{0,4},{4,0},{8,12},{12,8},{16,20},{20,16},{24,28},{28,24},{1,5},{5... | collective-permute-start | bytes 2359304 | tf_op jit(solution)/shard_map/ppermute | solution.py:436
  23.2 9.2 %collective-permute-start.11 = (bf16[8,128,128]{2,1,0:T(8,128)(2,1)S(1)}, bf16[8,128,128]{2,1,0:T(8,128)(2,1)S(1)}, u32[]{:S(2)}, u32[]{:S(2)}) collective-permute-start(bf16[8,128,128]{2,1,0:T(8,128)(2,1)S(1)} %shard_map.86.rest_4_), channel_id=1, source_target_pairs={{0,8},{4,12},{8,0},{12,4},{16,24},{20,28},{24,16},{28,20},{1,9},{5... | collective-permute-start | bytes 786440 | tf_op jit(solution)/shard_map/ppermute | solution.py:446
  23.9 14.1 %collective-permute-start.5 = (bf16[8,128,128]{2,1,0:T(8,128)(2,1)S(1)}, bf16[8,128,128]{2,1,0:T(8,128)(2,1)S(1)}, u32[]{:S(2)}, u32[]{:S(2)}) collective-permute-start(bf16[8,128,128]{2,1,0:T(8,128)(2,1)S(1)} %shard_map.87.rest_5_), channel_id=1, source_target_pairs={{0,8},{4,12},{8,0},{12,4},{16,24},{20,28},{24,16},{28,20},{1,9},{5... | collective-permute-start | bytes 786440 | tf_op jit(solution)/shard_map/ppermute | solution.py:446
  32.6 11.0 %collective-permute-start.12 = (bf16[8,128,128]{2,1,0:T(8,128)(2,1)S(1)}, bf16[8,128,128]{2,1,0:T(8,128)(2,1)S(1)}, u32[]{:S(2)}, u32[]{:S(2)}) collective-permute-start(bf16[8,128,128]{2,1,0:T(8,128)(2,1)S(1)} %get-tuple-element.38), channel_id=1, source_target_pairs={{0,8},{4,12},{8,0},{12,4},{16,24},{20,28},{24,16},{28,20},{1,9},{5... | collective-permute-start | bytes 786440 | tf_op jit(solution)/shard_map/ppermute | solution.py:446
  33.3 10.2 %collective-permute-start.13 = (bf16[8,128,128]{2,1,0:T(8,128)(2,1)S(1)}, bf16[8,128,128]{2,1,0:T(8,128)(2,1)S(1)}, u32[]{:S(2)}, u32[]{:S(2)}) collective-permute-start(bf16[8,128,128]{2,1,0:T(8,128)(2,1)S(1)} %get-tuple-element.39), channel_id=1, source_target_pairs={{0,4},{4,0},{8,16},{12,20},{16,8},{20,12},{24,28},{28,24},{1,5},{5... | collective-permute-start | bytes 786440 | tf_op jit(solution)/shard_map/ppermute | solution.py:446
  38.2 11.0 %collective-permute-start.6 = (bf16[8,128,128]{2,1,0:T(8,128)(2,1)S(1)}, bf16[8,128,128]{2,1,0:T(8,128)(2,1)S(1)}, u32[]{:S(2)}, u32[]{:S(2)}) collective-permute-start(bf16[8,128,128]{2,1,0:T(8,128)(2,1)S(1)} %get-tuple-element.33), channel_id=1, source_target_pairs={{0,8},{4,12},{8,0},{12,4},{16,24},{20,28},{24,16},{28,20},{1,9},{5... | collective-permute-start | bytes 786440 | tf_op jit(solution)/shard_map/ppermute | solution.py:446
  39.0 10.2 %collective-permute-start.7 = (bf16[8,128,128]{2,1,0:T(8,128)(2,1)S(1)}, bf16[8,128,128]{2,1,0:T(8,128)(2,1)S(1)}, u32[]{:S(2)}, u32[]{:S(2)}) collective-permute-start(bf16[8,128,128]{2,1,0:T(8,128)(2,1)S(1)} %get-tuple-element.34), channel_id=1, source_target_pairs={{0,4},{4,0},{8,16},{12,20},{16,8},{20,12},{24,28},{28,24},{1,5},{5... | collective-permute-start | bytes 786440 | tf_op jit(solution)/shard_map/ppermute | solution.py:446
  43.8 11.0 %copy-start = (f32[2048]{0:T(1024)S(1)}, f32[2048]{0:T(1024)}, u32[]{:S(2)}) copy-start(f32[2048]{0:T(1024)} %param.13) | copy-start | bytes 24580
  43.8 11.0 %collective-permute-start.14 = (bf16[8,128,128]{2,1,0:T(8,128)(2,1)S(1)}, bf16[8,128,128]{2,1,0:T(8,128)(2,1)S(1)}, u32[]{:S(2)}, u32[]{:S(2)}) collective-permute-start(bf16[8,128,128]{2,1,0:T(8,128)(2,1)S(1)} %get-tuple-element.40), channel_id=1, source_target_pairs={{0,8},{4,12},{8,0},{12,4},{16,24},{20,28},{24,16},{28,20},{1,9},{5... | collective-permute-start | bytes 786440 | tf_op jit(solution)/shard_map/ppermute | solution.py:446
  44.6 10.2 %collective-permute-start.15 = (bf16[8,128,128]{2,1,0:T(8,128)(2,1)S(1)}, bf16[8,128,128]{2,1,0:T(8,128)(2,1)S(1)}, u32[]{:S(2)}, u32[]{:S(2)}) collective-permute-start(bf16[8,128,128]{2,1,0:T(8,128)(2,1)S(1)} %get-tuple-element.41), channel_id=1, source_target_pairs={{0,4},{4,0},{8,16},{12,20},{16,8},{20,12},{24,28},{28,24},{1,5},{5... | collective-permute-start | bytes 786440 | tf_op jit(solution)/shard_map/ppermute | solution.py:446
  49.4 10.5 %collective-permute-start.8 = (bf16[8,128,128]{2,1,0:T(8,128)(2,1)S(1)}, bf16[8,128,128]{2,1,0:T(8,128)(2,1)S(1)}, u32[]{:S(2)}, u32[]{:S(2)}) collective-permute-start(bf16[8,128,128]{2,1,0:T(8,128)(2,1)S(1)} %get-tuple-element.35), channel_id=1, source_target_pairs={{0,8},{4,12},{8,0},{12,4},{16,24},{20,28},{24,16},{28,20},{1,9},{5... | collective-permute-start | bytes 786440 | tf_op jit(solution)/shard_map/ppermute | solution.py:446
  50.2 9.7 %collective-permute-start.9 = (bf16[8,128,128]{2,1,0:T(8,128)(2,1)S(1)}, bf16[8,128,128]{2,1,0:T(8,128)(2,1)S(1)}, u32[]{:S(2)}, u32[]{:S(2)}) collective-permute-start(bf16[8,128,128]{2,1,0:T(8,128)(2,1)S(1)} %get-tuple-element.36), channel_id=1, source_target_pairs={{0,4},{4,0},{8,16},{12,20},{16,8},{20,12},{24,28},{28,24},{1,5},{5... | collective-permute-start | bytes 786440 | tf_op jit(solution)/shard_map/ppermute | solution.py:446
  60.7 4.3 %collective-permute-start.16 = (f32[128,128]{1,0:T(8,128)S(1)}, f32[128,128]{1,0:T(8,128)S(1)}, u32[]{:S(2)}, u32[]{:S(2)}) collective-permute-start(f32[128,128]{1,0:T(8,128)S(1)} %get-tuple-element.43), channel_id=1, source_target_pairs={{0,8},{4,12},{8,0},{12,4},{16,24},{20,28},{24,16},{28,20},{1,9},{5... | collective-permute-start | bytes 196616 | tf_op jit(solution)/shard_map/ppermute | solution.py:507
  65.0 5.3 %collective-permute-start.17 = (f32[128,128]{1,0:T(8,128)S(1)}, f32[128,128]{1,0:T(8,128)S(1)}, u32[]{:S(2)}, u32[]{:S(2)}) collective-permute-start(f32[128,128]{1,0:T(8,128)S(1)} %add.18), channel_id=1, source_target_pairs={{0,16},{4,20},{8,24},{12,28},{16,0},{20,4},{24,8},{28,12},{1,17},{... | collective-permute-start | bytes 196616 | tf_op jit(solution)/shard_map/ppermute | solution.py:507
  67.8 9.2 %collective-permute-start.22 = (bf16[8,128,128]{2,1,0:T(8,128)(2,1)S(1)}, bf16[8,128,128]{2,1,0:T(8,128)(2,1)S(1)}, u32[]{:S(2)}, u32[]{:S(2)}) collective-permute-start(bf16[8,128,128]{2,1,0:T(8,128)(2,1)S(1)} %get-tuple-element.46.rest_0_), channel_id=1, source_target_pairs={{0,8},{4,12},{8,0},{12,4},{16,24},{20,28},{24,16},{28,20},{1,9},{5... | collective-permute-start | bytes 786440 | tf_op jit(solution)/shard_map/ppermute | solution.py:446
  69.5 10.9 %collective-permute-start.26 = (bf16[8,128,128]{2,1,0:T(8,128)(2,1)S(1)}, bf16[8,128,128]{2,1,0:T(8,128)(2,1)S(1)}, u32[]{:S(2)}, u32[]{:S(2)}) collective-permute-start(bf16[8,128,128]{2,1,0:T(8,128)(2,1)S(1)} %get-tuple-element.47.rest_2_), channel_id=1, source_target_pairs={{0,8},{4,12},{8,0},{12,4},{16,24},{20,28},{24,16},{28,20},{1,9},{5... | collective-permute-start | bytes 786440 | tf_op jit(solution)/shard_map/ppermute | solution.py:446
  69.8 10.6 %collective-permute-start.30 = (bf16[8,128,128]{2,1,0:T(8,128)(2,1)S(1)}, bf16[8,128,128]{2,1,0:T(8,128)(2,1)S(1)}, u32[]{:S(2)}, u32[]{:S(2)}) collective-permute-start(bf16[8,128,128]{2,1,0:T(8,128)(2,1)S(1)} %get-tuple-element.46.rest_0_), channel_id=1, source_target_pairs={{0,4},{4,0},{8,16},{12,20},{16,8},{20,12},{24,28},{28,24},{1,5},{5... | collective-permute-start | bytes 786440 | tf_op jit(solution)/shard_map/ppermute | solution.py:446
  69.8 11.1 %collective-permute-start.34 = (bf16[8,128,128]{2,1,0:T(8,128)(2,1)S(1)}, bf16[8,128,128]{2,1,0:T(8,128)(2,1)S(1)}, u32[]{:S(2)}, u32[]{:S(2)}) collective-permute-start(bf16[8,128,128]{2,1,0:T(8,128)(2,1)S(1)} %get-tuple-element.47.rest_2_), channel_id=1, source_target_pairs={{0,4},{4,0},{8,16},{12,20},{16,8},{20,12},{24,28},{28,24},{1,5},{5... | collective-permute-start | bytes 786440 | tf_op jit(solution)/shard_map/ppermute | solution.py:446
  70.4 13.9 %collective-permute-start.38 = (bf16[8,128,128]{2,1,0:T(8,128)(2,1)S(1)}, bf16[8,128,128]{2,1,0:T(8,128)(2,1)S(1)}, u32[]{:S(2)}, u32[]{:S(2)}) collective-permute-start(bf16[8,128,128]{2,1,0:T(8,128)(2,1)S(1)} %get-tuple-element.46.rest_0_), channel_id=1, source_target_pairs={{0,4},{4,0},{8,12},{12,8},{16,20},{20,16},{24,28},{28,24},{1,5},{5... | collective-permute-start | bytes 786440 | tf_op jit(solution)/shard_map/ppermute | solution.py:436
  77.0 7.3 %collective-permute-start.39 = (bf16[8,128,128]{2,1,0:T(8,128)(2,1)S(1)}, bf16[8,128,128]{2,1,0:T(8,128)(2,1)S(1)}, u32[]{:S(2)}, u32[]{:S(2)}) collective-permute-start(bf16[8,128,128]{2,1,0:T(8,128)(2,1)S(1)} %get-tuple-element.47.rest_2_), channel_id=1, source_target_pairs={{0,4},{4,0},{8,12},{12,8},{16,20},{20,16},{24,28},{28,24},{1,5},{5... | collective-permute-start | bytes 786440 | tf_op jit(solution)/shard_map/ppermute | solution.py:436
  80.4 4.0 %collective-permute-start.23 = (bf16[8,128,128]{2,1,0:T(8,128)(2,1)S(1)}, bf16[8,128,128]{2,1,0:T(8,128)(2,1)S(1)}, u32[]{:S(2)}, u32[]{:S(2)}) collective-permute-start(bf16[8,128,128]{2,1,0:T(8,128)(2,1)S(1)} %collective-permute-done.22.rest_4_), channel_id=1, source_target_pairs={{0,4},{4,0},{8,16},{12,20},{16,8},{20,12},{24,28},{28,24},{1,5},{5... | collective-permute-start | bytes 786440 | tf_op jit(solution)/shard_map/ppermute | solution.py:446
  80.4 4.4 %collective-permute-start.27 = (bf16[8,128,128]{2,1,0:T(8,128)(2,1)S(1)}, bf16[8,128,128]{2,1,0:T(8,128)(2,1)S(1)}, u32[]{:S(2)}, u32[]{:S(2)}) collective-permute-start(bf16[8,128,128]{2,1,0:T(8,128)(2,1)S(1)} %collective-permute-done.26.rest_8_), channel_id=1, source_target_pairs={{0,4},{4,0},{8,16},{12,20},{16,8},{20,12},{24,28},{28,24},{1,5},{5... | collective-permute-start | bytes 786440 | tf_op jit(solution)/shard_map/ppermute | solution.py:446
  80.9 10.5 %collective-permute-start.31 = (bf16[8,128,128]{2,1,0:T(8,128)(2,1)S(1)}, bf16[8,128,128]{2,1,0:T(8,128)(2,1)S(1)}, u32[]{:S(2)}, u32[]{:S(2)}) collective-permute-start(bf16[8,128,128]{2,1,0:T(8,128)(2,1)S(1)} %collective-permute-done.30.rest_6_), channel_id=1, source_target_pairs={{0,8},{4,12},{8,0},{12,4},{16,24},{20,28},{24,16},{28,20},{1,9},{5... | collective-permute-start | bytes 786440 | tf_op jit(solution)/shard_map/ppermute | solution.py:446
  84.3 10.6 %collective-permute-start.35 = (bf16[8,128,128]{2,1,0:T(8,128)(2,1)S(1)}, bf16[8,128,128]{2,1,0:T(8,128)(2,1)S(1)}, u32[]{:S(2)}, u32[]{:S(2)}) collective-permute-start(bf16[8,128,128]{2,1,0:T(8,128)(2,1)S(1)} %collective-permute-done.34.rest_10_), channel_id=1, source_target_pairs={{0,8},{4,12},{8,0},{12,4},{16,24},{20,28},{24,16},{28,20},{1,9},{5... | collective-permute-start | bytes 786440 | tf_op jit(solution)/shard_map/ppermute | solution.py:446
  84.3 10.8 %collective-permute-start.40 = (bf16[8,128,128]{2,1,0:T(8,128)(2,1)S(1)}, bf16[8,128,128]{2,1,0:T(8,128)(2,1)S(1)}, u32[]{:S(2)}, u32[]{:S(2)}) collective-permute-start(bf16[8,128,128]{2,1,0:T(8,128)(2,1)S(1)} %collective-permute-done.22.rest_4_), channel_id=1, source_target_pairs={{0,4},{4,0},{8,12},{12,8},{16,20},{20,16},{24,28},{28,24},{1,5},{5... | collective-permute-start | bytes 786440 | tf_op jit(solution)/shard_map/ppermute | solution.py:436
  84.4 10.8 %collective-permute-start.41 = (bf16[8,128,128]{2,1,0:T(8,128)(2,1)S(1)}, bf16[8,128,128]{2,1,0:T(8,128)(2,1)S(1)}, u32[]{:S(2)}, u32[]{:S(2)}) collective-permute-start(bf16[8,128,128]{2,1,0:T(8,128)(2,1)S(1)} %collective-permute-done.30.rest_6_), channel_id=1, source_target_pairs={{0,4},{4,0},{8,12},{12,8},{16,20},{20,16},{24,28},{28,24},{1,5},{5... | collective-permute-start | bytes 786440 | tf_op jit(solution)/shard_map/ppermute | solution.py:436
  84.8 12.2 %collective-permute-start.42 = (bf16[8,128,128]{2,1,0:T(8,128)(2,1)S(1)}, bf16[8,128,128]{2,1,0:T(8,128)(2,1)S(1)}, u32[]{:S(2)}, u32[]{:S(2)}) collective-permute-start(bf16[8,128,128]{2,1,0:T(8,128)(2,1)S(1)} %collective-permute-done.26.rest_8_), channel_id=1, source_target_pairs={{0,4},{4,0},{8,12},{12,8},{16,20},{20,16},{24,28},{28,24},{1,5},{5... | collective-permute-start | bytes 786440 | tf_op jit(solution)/shard_map/ppermute | solution.py:436
  91.4 5.8 %collective-permute-start.43 = (bf16[8,128,128]{2,1,0:T(8,128)(2,1)S(1)}, bf16[8,128,128]{2,1,0:T(8,128)(2,1)S(1)}, u32[]{:S(2)}, u32[]{:S(2)}) collective-permute-start(bf16[8,128,128]{2,1,0:T(8,128)(2,1)S(1)} %collective-permute-done.34.rest_10_), channel_id=1, source_target_pairs={{0,4},{4,0},{8,12},{12,8},{16,20},{20,16},{24,28},{28,24},{1,5},{5... | collective-permute-start | bytes 786440 | tf_op jit(solution)/shard_map/ppermute | solution.py:436
  94.8 9.2 %collective-permute-start.24 = (bf16[8,128,128]{2,1,0:T(8,128)(2,1)S(1)}, bf16[8,128,128]{2,1,0:T(8,128)(2,1)S(1)}, u32[]{:S(2)}, u32[]{:S(2)}) collective-permute-start(bf16[8,128,128]{2,1,0:T(8,128)(2,1)S(1)} %collective-permute-done.23.rest_2_), channel_id=1, source_target_pairs={{0,8},{4,12},{8,0},{12,4},{16,24},{20,28},{24,16},{28,20},{1,9},{5... | collective-permute-start | bytes 786440 | tf_op jit(solution)/shard_map/ppermute | solution.py:446
  95.1 16.6 %collective-permute-start.33 = (bf16[8,128,128]{2,1,0:T(8,128)(2,1)S(1)}, bf16[8,128,128]{2,1,0:T(8,128)(2,1)S(1)}, u32[]{:S(2)}, u32[]{:S(2)}) collective-permute-start(bf16[8,128,128]{2,1,0:T(8,128)(2,1)S(1)} %collective-permute-done.23.rest_2_), channel_id=1, source_target_pairs={{0,4},{4,0},{8,12},{12,8},{16,20},{20,16},{24,28},{28,24},{1,5},{5... | collective-permute-start | bytes 786440 | tf_op jit(solution)/shard_map/ppermute | solution.py:436
  95.2 13.4 %collective-permute-start.28 = (bf16[8,128,128]{2,1,0:T(8,128)(2,1)S(1)}, bf16[8,128,128]{2,1,0:T(8,128)(2,1)S(1)}, u32[]{:S(2)}, u32[]{:S(2)}) collective-permute-start(bf16[8,128,128]{2,1,0:T(8,128)(2,1)S(1)} %collective-permute-done.27.rest_6_), channel_id=1, source_target_pairs={{0,8},{4,12},{8,0},{12,4},{16,24},{20,28},{24,16},{28,20},{1,9},{5... | collective-permute-start | bytes 786440 | tf_op jit(solution)/shard_map/ppermute | solution.py:446
  97.0 15.4 %collective-permute-start.37 = (bf16[8,128,128]{2,1,0:T(8,128)(2,1)S(1)}, bf16[8,128,128]{2,1,0:T(8,128)(2,1)S(1)}, u32[]{:S(2)}, u32[]{:S(2)}) collective-permute-start(bf16[8,128,128]{2,1,0:T(8,128)(2,1)S(1)} %collective-permute-done.27.rest_6_), channel_id=1, source_target_pairs={{0,4},{4,0},{8,12},{12,8},{16,20},{20,16},{24,28},{28,24},{1,5},{5... | collective-permute-start | bytes 786440 | tf_op jit(solution)/shard_map/ppermute | solution.py:436
  97.2 14.5 %collective-permute-start.32 = (bf16[8,128,128]{2,1,0:T(8,128)(2,1)S(1)}, bf16[8,128,128]{2,1,0:T(8,128)(2,1)S(1)}, u32[]{:S(2)}, u32[]{:S(2)}) collective-permute-start(bf16[8,128,128]{2,1,0:T(8,128)(2,1)S(1)} %collective-permute-done.31.rest_0_), channel_id=1, source_target_pairs={{0,4},{4,0},{8,12},{12,8},{16,20},{20,16},{24,28},{28,24},{1,5},{5... | collective-permute-start | bytes 786440 | tf_op jit(solution)/shard_map/ppermute | solution.py:436
  104.0 8.4 %collective-permute-start.36 = (bf16[8,128,128]{2,1,0:T(8,128)(2,1)S(1)}, bf16[8,128,128]{2,1,0:T(8,128)(2,1)S(1)}, u32[]{:S(2)}, u32[]{:S(2)}) collective-permute-start(bf16[8,128,128]{2,1,0:T(8,128)(2,1)S(1)} %collective-permute-done.35.rest_4_), channel_id=1, source_target_pairs={{0,4},{4,0},{8,12},{12,8},{16,20},{20,16},{24,28},{28,24},{1,5},{5... | collective-permute-start | bytes 786440 | tf_op jit(solution)/shard_map/ppermute | solution.py:436
  108.6 14.1 %collective-permute-start.20 = (f32[128,128]{1,0:T(8,128)S(1)}, f32[128,128]{1,0:T(8,128)S(1)}, u32[]{:S(2)}, u32[]{:S(2)}) collective-permute-start(f32[128,128]{1,0:T(8,128)S(1)} %add.19), channel_id=1, source_target_pairs={{0,3},{1,0},{2,1},{3,2},{4,7},{5,4},{6,5},{7,6},{8,11},{9,8},{10,9... | collective-permute-start | bytes 196616 | tf_op jit(solution)/shard_map/ppermute | solution.py:403
  111.7 12.5 %collective-permute-start.19 = (f32[128,128]{1,0:T(8,128)S(1)}, f32[128,128]{1,0:T(8,128)S(1)}, u32[]{:S(2)}, u32[]{:S(2)}) collective-permute-start(f32[128,128]{1,0:T(8,128)S(1)} %add.19), channel_id=1, source_target_pairs={{0,2},{1,3},{2,0},{3,1},{4,6},{5,7},{6,4},{7,5},{8,10},{9,11},{10,... | collective-permute-start | bytes 196616 | tf_op jit(solution)/shard_map/ppermute | solution.py:403
  111.7 12.5 %collective-permute-start.18 = (f32[128,128]{1,0:T(8,128)S(1)}, f32[128,128]{1,0:T(8,128)S(1)}, u32[]{:S(2)}, u32[]{:S(2)}) collective-permute-start(f32[128,128]{1,0:T(8,128)S(1)} %add.19), channel_id=1, source_target_pairs={{0,1},{1,2},{2,3},{3,0},{4,5},{5,6},{6,7},{7,4},{8,9},{9,10},{10,1... | collective-permute-start | bytes 196616 | tf_op jit(solution)/shard_map/ppermute | solution.py:403
  112.4 3.8 %collective-permute-start.25 = (bf16[8,128,128]{2,1,0:T(8,128)(2,1)S(1)}, bf16[8,128,128]{2,1,0:T(8,128)(2,1)S(1)}, u32[]{:S(2)}, u32[]{:S(2)}) collective-permute-start(bf16[8,128,128]{2,1,0:T(8,128)(2,1)S(1)} %collective-permute-done.24.rest_0_), channel_id=1, source_target_pairs={{0,4},{4,0},{8,12},{12,8},{16,20},{20,16},{24,28},{28,24},{1,5},{5... | collective-permute-start | bytes 786440 | tf_op jit(solution)/shard_map/ppermute | solution.py:436
  112.4 3.8 %collective-permute-start.29 = (bf16[8,128,128]{2,1,0:T(8,128)(2,1)S(1)}, bf16[8,128,128]{2,1,0:T(8,128)(2,1)S(1)}, u32[]{:S(2)}, u32[]{:S(2)}) collective-permute-start(bf16[8,128,128]{2,1,0:T(8,128)(2,1)S(1)} %collective-permute-done.28.rest_2_), channel_id=1, source_target_pairs={{0,4},{4,0},{8,12},{12,8},{16,20},{20,16},{24,28},{28,24},{1,5},{5... | collective-permute-start | bytes 786440 | tf_op jit(solution)/shard_map/ppermute | solution.py:436
  119.4 15.2 %collective-permute-start.44 = (bf16[4,128,128]{2,1,0:T(8,128)(2,1)S(1)}, bf16[4,128,128]{2,1,0:T(8,128)(2,1)S(1)}, u32[]{:S(2)}, u32[]{:S(2)}) collective-permute-start(bf16[4,128,128]{2,1,0:T(8,128)(2,1)S(1)} %get-tuple-element.49), channel_id=1, source_target_pairs={{0,1},{1,0},{2,3},{3,2},{4,5},{5,4},{6,7},{7,6},{8,9},{9,8},{10,11... | collective-permute-start | bytes 393224 | tf_op jit(solution)/shard_map/ppermute | solution.py:526
  122.7 11.9 %collective-permute-start.45 = (bf16[4,128,128]{2,1,0:T(8,128)(2,1)S(1)}, bf16[4,128,128]{2,1,0:T(8,128)(2,1)S(1)}, u32[]{:S(2)}, u32[]{:S(2)}) collective-permute-start(bf16[4,128,128]{2,1,0:T(8,128)(2,1)S(1)} %get-tuple-element.50), channel_id=1, source_target_pairs={{0,2},{1,3},{2,0},{3,1},{4,6},{5,7},{6,4},{7,5},{8,10},{9,11},{10,... | collective-permute-start | bytes 393224 | tf_op jit(solution)/shard_map/ppermute | solution.py:526
  122.7 11.9 %collective-permute-start.46 = (bf16[4,128,128]{2,1,0:T(8,128)(2,1)S(1)}, bf16[4,128,128]{2,1,0:T(8,128)(2,1)S(1)}, u32[]{:S(2)}, u32[]{:S(2)}) collective-permute-start(bf16[4,128,128]{2,1,0:T(8,128)(2,1)S(1)} %get-tuple-element.51), channel_id=1, source_target_pairs={{0,3},{1,2},{2,1},{3,0},{4,7},{5,6},{6,5},{7,4},{8,11},{9,10},{10,... | collective-permute-start | bytes 393224 | tf_op jit(solution)/shard_map/ppermute | solution.py:526
  124.2 1.3 collective-permute-start.21

commit v6 on v5

--- a/solution.py
+++ b/solution.py
@@ -447,8 +447,11 @@
 
     col_own = omega.shape[0] // edge
     own_omega = omega.reshape(col_own, edge, cols)
-    omegas = [own_omega] + [lax.ppermute(own_omega, "dev", partners(n_dev, s))
-                            for s in range(1, n_dev)]
+
+    def to_dev(x, k):
+        return lax.ppermute(x, "dev", partners(n_dev, k))
+
+    omegas = [own_omega] + [to_dev(own_omega, k) for k in range(1, n_dev)]
 
     far_mine, far_theirs = partial_sketch(True, scalars, tiles, omegas, chips, blocks)
     far_pair = swap(far_theirs)
@@ -523,7 +526,7 @@
                        col_own)
         docs = docs if own_class == 2 else docs[0]
     parts = docs
-    arrived = [lax.ppermute(parts[s], "dev", partners(n_dev, s)) for s in range(1, n_dev)]
+    arrived = [to_dev(parts[k], k) for k in range(1, n_dev)]
     doc_factor = on_chip(finish_kernel, jax.ShapeDtypeStruct((cols, col_own * edge), BF16),
                          inverse, parts[0], *arrived)
     return (q_basis, doc_factor)

time: 136 us -> 136 us (level)
  no operation moved by 1% of the time
where the time goes in v6:
time: 136 us
  waiting for transfers between devices  64.7 us (48%)
  Pallas kernels  34.3 us (25%)
  starting transfers between devices  32.9 us (24%)
  local copies, waits for them, and re-layouts  2.22 us (2%)
  between operations  1.58 us (1%)
    ppermute x20, waiting for transfers between devices, over(): return lax.ppermute(x, 'group', links)  56.2 us
    ppermute x20, starting transfers between devices, over(): return lax.ppermute(x, 'group', links)  13.6 us
    pallas_call x12, Pallas kernels, on_chip(): pl.pallas_call(kernel, out_shape=out_shape, in_specs=specs, out_specs=jax...  12.6 us
    pallas_call x3, Pallas kernels, project(): pl.pallas_call(functools.partial(project_kernel, own_class, chips, owned,...  11.1 us
    ppermute x6, starting transfers between devices, to_dev(): return lax.ppermute(x, 'dev', partners(n_dev, k))  9.38 us
    pallas_call x2, Pallas kernels, partial_sketch(): pl.pallas_call(functools.partial(sketch_kernel, far_only, chips, blocks,...  8.61 us
    ppermute x3, starting transfers between devices, exchanges(): lax.ppermute(x, axis, [(i, i // span * span + (i + k * s) % span) for i i...  3.72 us
    ppermute x2, waiting for transfers between devices, on_device(): gram = gram + lax.ppermute(gram, 'group', partners(n_group, step))  3.58 us
  transfers between devices with their start and end apart: 47, of which 15 were waited for; matrix products, arithmetic and copies ran while one was open for 2% of the time, Pallas kernels for 18%

profile of v6, /device:TPU:0, one launch (start us, length us, event | category | flops | bytes accessed | tf_op | source)
XLA Modules:
  0.0 135.6 jit_solution(4739712420451474552)
XLA Ops:
  0.6 3.0 %collective-permute-start = (bf16[4,128,128]{2,1,0:T(8,128)(2,1)}, bf16[4,128,128]{2,1,0:T(8,128)(2,1)S(1)}, u32[]{:S(2)}, u32[]{:S(2)}) collective-permute-start(bf16[4,128,128]{2,1,0:T(8,128)(2,1)} %bitcast.18), channel_id=1, source_target_pairs={{0,1},{1,0},{2,3},{3,2},{4,5},{5,4},{6,7},{7,6},{8,9},{9,8},{10,11... | collective-permute-start | bytes 393224 | tf_op jit(solution)/shard_map/ppermute | solution.py:452
  3.7 1.5 %collective-permute-start.1 = (bf16[4,128,128]{2,1,0:T(8,128)(2,1)}, bf16[4,128,128]{2,1,0:T(8,128)(2,1)S(1)}, u32[]{:S(2)}, u32[]{:S(2)}) collective-permute-start(bf16[4,128,128]{2,1,0:T(8,128)(2,1)} %bitcast.19), channel_id=1, source_target_pairs={{0,2},{1,3},{2,0},{3,1},{4,6},{5,7},{6,4},{7,5},{8,10},{9,11},{10,... | collective-permute-start | bytes 393224 | tf_op jit(solution)/shard_map/ppermute | solution.py:452
  5.9 0.9 slice_bitcast_fusion
  6.7 1.3 concatenate.3.given_ref
  8.1 1.9 %lists.1 = (s32[507]{0:T(512)S(4)}, s32[365]{0:T(512)S(4)}) custom-call(s32[507]{0:T(512)} %concatenate.3.given_ref), custom_call_target="tpu_custom_call" | custom-call | tf_op jit(solution)/shard_map/lists/pallas_call | solution.py:424
  10.0 1.6 %collective-permute-done.1.rest_2_ = bf16[4,128,128]{2,1,0:T(8,128)(2,1)S(1)} collective-permute-done((bf16[4,128,128]{2,1,0:T(8,128)(2,1)}, bf16[4,128,128]{2,1,0:T(8,128)(2,1)S(1)}, u32[]{:S(2)}, u32[]{:S(2)}) %collective-permute-start.1) | collective-permute-done | bytes 131104 | tf_op jit(solution)/shard_map/ppermute | solution.py:452
  11.7 3.3 %sketch_far.1 = (f32[32,128,128]{2,1,0:T(8,128)S(1)}, bf16[16,128,128]{2,1,0:T(8,128)(2,1)S(1)}) custom-call(s32[507]{0:T(512)S(4)} %get-tuple-element.27.ints_ref, s32[365]{0:T(512)S(4)} %get-tuple-element.28.lists_ref, bf16[72,5,128,128]{3,2,1,0:T(8,128)(2,1)} %tiles_ref.9, bf16[4,128,128]{2,1,0:T(8,128)(2,1)} %bitcast.21, ...), custom_call_target="tpu_custom_call" | custom-call | flops 4831838208 | bytes 9437184 | tf_op jit(solution)/shard_map/sketch_far/pallas_call | solution.py:171
  15.0 1.9 %collective-permute-done.3.pair_ref.far_pair = bf16[16,128,128]{2,1,0:T(8,128)(2,1)S(1)} collective-permute-done((bf16[16,128,128]{2,1,0:T(8,128)(2,1)S(1)}, bf16[16,128,128]{2,1,0:T(8,128)(2,1)S(1)}, u32[]{:S(2)}, u32[]{:S(2)}) %collective-permute-start.3) | collective-permute-done | bytes 524320 | tf_op jit(solution)/shard_map/ppermute | solution.py:436
  17.0 5.3 %sketch_rest.1 = (f32[96,128,128]{2,1,0:T(8,128)S(1)}, bf16[24,128,128]{2,1,0:T(8,128)(2,1)S(1)}, bf16[24,128,128]{2,1,0:T(8,128)(2,1)S(1)}) custom-call(s32[507]{0:T(512)S(4)} %get-tuple-element.27.ints_ref, s32[365]{0:T(512)S(4)} %get-tuple-element.28.lists_ref, bf16[72,5,128,128]{3,2,1,0:T(8,128)(2,1)} %tiles_ref.9, bf16[4,128,128]{2,1,0:T(8,128)(2,1)} %bitcast.22, ...), custom_call_target="tpu_custom_call" | custom-call | flops 19327352832 | bytes 37748736 | tf_op jit(solution)/shard_map/sketch_rest/pallas_call | solution.py:171
  22.4 0.7 collective-permute-start.10
  23.2 0.7 collective-permute-start.11
  23.9 1.3 collective-permute-start.5
  25.2 7.2 %collective-permute-done.11.even_in.odd_in = bf16[8,128,128]{2,1,0:T(8,128)(2,1)S(1)} collective-permute-done((bf16[8,128,128]{2,1,0:T(8,128)(2,1)S(1)}, bf16[8,128,128]{2,1,0:T(8,128)(2,1)S(1)}, u32[]{:S(2)}, u32[]{:S(2)}) %collective-permute-start.11) | collective-permute-done | bytes 262176 | tf_op jit(solution)/shard_map/ppermute | solution.py:446
  32.6 0.8 collective-permute-start.12
  33.3 4.6 %collective-permute-done.5.even_in.odd_in = bf16[8,128,128]{2,1,0:T(8,128)(2,1)S(1)} collective-permute-done((bf16[8,128,128]{2,1,0:T(8,128)(2,1)S(1)}, bf16[8,128,128]{2,1,0:T(8,128)(2,1)S(1)}, u32[]{:S(2)}, u32[]{:S(2)}) %collective-permute-start.5) | collective-permute-done | bytes 262176 | tf_op jit(solution)/shard_map/ppermute | solution.py:446
  38.2 0.8 collective-permute-start.6
  39.0 4.6 %collective-permute-done.12.even_in = bf16[8,128,128]{2,1,0:T(8,128)(2,1)S(1)} collective-permute-done((bf16[8,128,128]{2,1,0:T(8,128)(2,1)S(1)}, bf16[8,128,128]{2,1,0:T(8,128)(2,1)S(1)}, u32[]{:S(2)}, u32[]{:S(2)}) %collective-permute-start.12) | collective-permute-done | bytes 262176 | tf_op jit(solution)/shard_map/ppermute | solution.py:446
  43.8 0.8 collective-permute-start.14
  44.6 4.6 %collective-permute-done.6.even_in = bf16[8,128,128]{2,1,0:T(8,128)(2,1)S(1)} collective-permute-done((bf16[8,128,128]{2,1,0:T(8,128)(2,1)S(1)}, bf16[8,128,128]{2,1,0:T(8,128)(2,1)S(1)}, u32[]{:S(2)}, u32[]{:S(2)}) %collective-permute-start.6) | collective-permute-done | bytes 262176 | tf_op jit(solution)/shard_map/ppermute | solution.py:446
  49.4 0.8 collective-permute-start.8
  50.2 4.6 %collective-permute-done.14.even_ref = bf16[8,128,128]{2,1,0:T(8,128)(2,1)S(1)} collective-permute-done((bf16[8,128,128]{2,1,0:T(8,128)(2,1)S(1)}, bf16[8,128,128]{2,1,0:T(8,128)(2,1)S(1)}, u32[]{:S(2)}, u32[]{:S(2)}) %collective-permute-start.14) | collective-permute-done | bytes 262176 | tf_op jit(solution)/shard_map/ppermute | solution.py:446
  54.8 0.8 shard_map.92
  55.6 4.3 %collective-permute-done.8.even_ref = bf16[8,128,128]{2,1,0:T(8,128)(2,1)S(1)} collective-permute-done((bf16[8,128,128]{2,1,0:T(8,128)(2,1)S(1)}, bf16[8,128,128]{2,1,0:T(8,128)(2,1)S(1)}, u32[]{:S(2)}, u32[]{:S(2)}) %collective-permute-start.8) | collective-permute-done | bytes 262176 | tf_op jit(solution)/shard_map/ppermute | solution.py:446
  59.9 0.8 shard_map.93
  60.7 0.8 collective-permute-start.16
  61.5 3.6 %collective-permute-done.16 = f32[128,128]{1,0:T(8,128)S(1)} collective-permute-done((f32[128,128]{1,0:T(8,128)S(1)}, f32[128,128]{1,0:T(8,128)S(1)}, u32[]{:S(2)}, u32[]{:S(2)}) %collective-permute-start.16) | collective-permute-done | bytes 65568 | tf_op jit(solution)/shard_map/ppermute | solution.py:510
  65.0 2.8 %collective-permute-start.17 = (f32[128,128]{1,0:T(8,128)S(1)}, f32[128,128]{1,0:T(8,128)S(1)}, u32[]{:S(2)}, u32[]{:S(2)}) collective-permute-start(f32[128,128]{1,0:T(8,128)S(1)} %add.18), channel_id=1, source_target_pairs={{0,16},{4,20},{8,24},{12,28},{16,0},{20,4},{24,8},{28,12},{1,17},{... | collective-permute-start | bytes 196616 | tf_op jit(solution)/shard_map/ppermute | solution.py:510
  67.8 1.7 %collective-permute-start.22 = (bf16[8,128,128]{2,1,0:T(8,128)(2,1)S(1)}, bf16[8,128,128]{2,1,0:T(8,128)(2,1)S(1)}, u32[]{:S(2)}, u32[]{:S(2)}) collective-permute-start(bf16[8,128,128]{2,1,0:T(8,128)(2,1)S(1)} %get-tuple-element.46.rest_0_), channel_id=1, source_target_pairs={{0,8},{4,12},{8,0},{12,4},{16,24},{20,28},{24,16},{28,20},{1,9},{5... | collective-permute-start | bytes 786440 | tf_op jit(solution)/shard_map/ppermute | solution.py:446
  70.4 6.6 %collective-permute-done.22.rest_4_ = bf16[8,128,128]{2,1,0:T(8,128)(2,1)S(1)} collective-permute-done((bf16[8,128,128]{2,1,0:T(8,128)(2,1)S(1)}, bf16[8,128,128]{2,1,0:T(8,128)(2,1)S(1)}, u32[]{:S(2)}, u32[]{:S(2)}) %collective-permute-start.22) | collective-permute-done | bytes 262176 | tf_op jit(solution)/shard_map/ppermute | solution.py:446
  77.0 3.4 %collective-permute-done.26.rest_8_ = bf16[8,128,128]{2,1,0:T(8,128)(2,1)S(1)} collective-permute-done((bf16[8,128,128]{2,1,0:T(8,128)(2,1)S(1)}, bf16[8,128,128]{2,1,0:T(8,128)(2,1)S(1)}, u32[]{:S(2)}, u32[]{:S(2)}) %collective-permute-start.26) | collective-permute-done | bytes 262176 | tf_op jit(solution)/shard_map/ppermute | solution.py:446
  80.4 0.5 collective-permute-start.27
  80.9 3.3 %collective-permute-start.31 = (bf16[8,128,128]{2,1,0:T(8,128)(2,1)S(1)}, bf16[8,128,128]{2,1,0:T(8,128)(2,1)S(1)}, u32[]{:S(2)}, u32[]{:S(2)}) collective-permute-start(bf16[8,128,128]{2,1,0:T(8,128)(2,1)S(1)} %collective-permute-done.30.rest_6_), channel_id=1, source_target_pairs={{0,8},{4,12},{8,0},{12,4},{16,24},{20,28},{24,16},{28,20},{1,9},{5... | collective-permute-start | bytes 786440 | tf_op jit(solution)/shard_map/ppermute | solution.py:446
  84.9 6.5 %collective-permute-done.31.rest_0_ = bf16[8,128,128]{2,1,0:T(8,128)(2,1)S(1)} collective-permute-done((bf16[8,128,128]{2,1,0:T(8,128)(2,1)S(1)}, bf16[8,128,128]{2,1,0:T(8,128)(2,1)S(1)}, u32[]{:S(2)}, u32[]{:S(2)}) %collective-permute-start.31) | collective-permute-done | bytes 262176 | tf_op jit(solution)/shard_map/ppermute | solution.py:446
  91.4 3.4 %collective-permute-done.35.rest_4_ = bf16[8,128,128]{2,1,0:T(8,128)(2,1)S(1)} collective-permute-done((bf16[8,128,128]{2,1,0:T(8,128)(2,1)S(1)}, bf16[8,128,128]{2,1,0:T(8,128)(2,1)S(1)}, u32[]{:S(2)}, u32[]{:S(2)}) %collective-permute-start.35) | collective-permute-done | bytes 262176 | tf_op jit(solution)/shard_map/ppermute | solution.py:446
  95.2 1.8 %collective-permute-start.28 = (bf16[8,128,128]{2,1,0:T(8,128)(2,1)S(1)}, bf16[8,128,128]{2,1,0:T(8,128)(2,1)S(1)}, u32[]{:S(2)}, u32[]{:S(2)}) collective-permute-start(bf16[8,128,128]{2,1,0:T(8,128)(2,1)S(1)} %collective-permute-done.27.rest_6_), channel_id=1, source_target_pairs={{0,8},{4,12},{8,0},{12,4},{16,24},{20,28},{24,16},{28,20},{1,9},{5... | collective-permute-start | bytes 786440 | tf_op jit(solution)/shard_map/ppermute | solution.py:446
  97.5 6.5 %collective-permute-done.24.rest_0_ = bf16[8,128,128]{2,1,0:T(8,128)(2,1)S(1)} collective-permute-done((bf16[8,128,128]{2,1,0:T(8,128)(2,1)S(1)}, bf16[8,128,128]{2,1,0:T(8,128)(2,1)S(1)}, u32[]{:S(2)}, u32[]{:S(2)}) %collective-permute-start.24) | collective-permute-done | bytes 262176 | tf_op jit(solution)/shard_map/ppermute | solution.py:446
  104.0 4.6 %shard_map.97.rest_8_ = f32[16,128,128]{2,1,0:T(8,128)S(1)} custom-call(s32[507]{0:T(512)S(4)} %get-tuple-element.27.ints_ref, s32[365]{0:T(512)S(4)} %get-tuple-element.28.lists_ref, bf16[72,5,128,128]{3,2,1,0:T(8,128)(2,1)} %tiles_ref.9, bf16[8,128,128]{2,1,0:T(8,128)(2,1)S(1)} %get-tuple-element.46.rest_0_, ...), custom_call_target="tpu_custom_call" | custom-call | flops 6442450944 | bytes 12582912 | tf_op jit(solution)/shard_map/pallas_call | solution.py:350
  108.6 3.1 %collective-permute-start.20 = (f32[128,128]{1,0:T(8,128)S(1)}, f32[128,128]{1,0:T(8,128)S(1)}, u32[]{:S(2)}, u32[]{:S(2)}) collective-permute-start(f32[128,128]{1,0:T(8,128)S(1)} %add.19), channel_id=1, source_target_pairs={{0,3},{1,0},{2,1},{3,2},{4,7},{5,4},{6,5},{7,6},{8,11},{9,8},{10,9... | collective-permute-start | bytes 196616 | tf_op jit(solution)/shard_map/ppermute | solution.py:403
  111.7 0.6 collective-permute-start.18
  112.9 3.2 %shard_map.98.rest_4_ = f32[16,128,128]{2,1,0:T(8,128)S(1)} custom-call(s32[507]{0:T(512)S(4)} %get-tuple-element.27.ints_ref, s32[365]{0:T(512)S(4)} %get-tuple-element.28.lists_ref, bf16[72,5,128,128]{3,2,1,0:T(8,128)(2,1)} %tiles_ref.9, bf16[8,128,128]{2,1,0:T(8,128)(2,1)S(1)} %collective-permute-done.31.rest_0_, ...), custom_call_target="tpu_custom_call" | custom-call | flops 6442450944 | bytes 12582912 | tf_op jit(solution)/shard_map/pallas_call | solution.py:350
  116.2 3.3 %shard_map.99 = (f32[4,128,128]{2,1,0:T(8,128)S(1)}, bf16[4,128,128]{2,1,0:T(8,128)(2,1)S(1)}, bf16[4,128,128]{2,1,0:T(8,128)(2,1)S(1)}, bf16[4,128,128]{2,1,0:T(8,128)(2,1)S(1)}) custom-call(s32[507]{0:T(512)S(4)} %get-tuple-element.27.ints_ref, s32[365]{0:T(512)S(4)} %get-tuple-element.28.lists_ref, bf16[72,5,128,128]{3,2,1,0:T(8,128)(2,1)} %tiles_ref.9, ...), custom_call_target="tpu_custom_call" | custom-call | flops 6442450944 | bytes 12582912 | tf_op jit(solution)/shard_map/pallas_call | solution.py:350
  119.4 3.3 %collective-permute-start.44 = (bf16[4,128,128]{2,1,0:T(8,128)(2,1)S(1)}, bf16[4,128,128]{2,1,0:T(8,128)(2,1)S(1)}, u32[]{:S(2)}, u32[]{:S(2)}) collective-permute-start(bf16[4,128,128]{2,1,0:T(8,128)(2,1)S(1)} %get-tuple-element.49), channel_id=1, source_target_pairs={{0,1},{1,0},{2,3},{3,2},{4,5},{5,4},{6,7},{7,6},{8,9},{9,8},{10,11... | collective-permute-start | bytes 393224 | tf_op jit(solution)/shard_map/ppermute | solution.py:452
  122.7 1.5 %collective-permute-start.46 = (bf16[4,128,128]{2,1,0:T(8,128)(2,1)S(1)}, bf16[4,128,128]{2,1,0:T(8,128)(2,1)S(1)}, u32[]{:S(2)}, u32[]{:S(2)}) collective-permute-start(bf16[4,128,128]{2,1,0:T(8,128)(2,1)S(1)} %get-tuple-element.51), channel_id=1, source_target_pairs={{0,3},{1,2},{2,1},{3,0},{4,7},{5,6},{6,5},{7,4},{8,11},{9,10},{10,... | collective-permute-start | bytes 393224 | tf_op jit(solution)/shard_map/ppermute | solution.py:452
  124.3 1.2 collective-permute-done.21
  125.6 3.4 %shard_map.94.refs_0_ = f32[128,128]{1,0:T(8,128)S(1)} custom-call(f32[128,128]{1,0:T(8,128)S(1)} %add.23.refs_0_), custom_call_target="tpu_custom_call" | custom-call | tf_op jit(solution)/shard_map/pallas_call | solution.py:379
  129.0 3.4 %shard_map.95.inverse_ref = f32[128,128]{1,0:T(8,128)S(1)} custom-call(f32[128,128]{1,0:T(8,128)S(1)} %shard_map.94.refs_0_), custom_call_target="tpu_custom_call" | custom-call | tf_op jit(solution)/shard_map/pallas_call | solution.py:379
  132.4 2.2 %shard_map.96 = f32[16,128,128]{2,1,0:T(8,128)} custom-call(f32[128,128]{1,0:T(8,128)S(1)} %shard_map.95.inverse_ref, f32[8,128,128]{2,1,0:T(8,128)S(1)} %get-tuple-element.44.rest_0_, f32[8,128,128]{2,1,0:T(8,128)S(1)} %get-tuple-element.45.rest_1_), custom_call_target="tpu_custom_call" | custom-call | tf_op jit(solution)/shard_map/pallas_call | solution.py:379
  134.6 1.0 shard_map.100
  (73 shorter events, 4.3 us)
Async XLA Ops:
  0.6 9.4 %collective-permute-start = (bf16[4,128,128]{2,1,0:T(8,128)(2,1)}, bf16[4,128,128]{2,1,0:T(8,128)(2,1)S(1)}, u32[]{:S(2)}, u32[]{:S(2)}) collective-permute-start(bf16[4,128,128]{2,1,0:T(8,128)(2,1)} %bitcast.18), channel_id=1, source_target_pairs={{0,1},{1,0},{2,3},{3,2},{4,5},{5,4},{6,7},{7,6},{8,9},{9,8},{10,11... | collective-permute-start | bytes 393224 | tf_op jit(solution)/shard_map/ppermute | solution.py:452
  3.7 8.0 %collective-permute-start.1 = (bf16[4,128,128]{2,1,0:T(8,128)(2,1)}, bf16[4,128,128]{2,1,0:T(8,128)(2,1)S(1)}, u32[]{:S(2)}, u32[]{:S(2)}) collective-permute-start(bf16[4,128,128]{2,1,0:T(8,128)(2,1)} %bitcast.19), channel_id=1, source_target_pairs={{0,2},{1,3},{2,0},{3,1},{4,6},{5,7},{6,4},{7,5},{8,10},{9,11},{10,... | collective-permute-start | bytes 393224 | tf_op jit(solution)/shard_map/ppermute | solution.py:452
  5.2 6.5 %collective-permute-start.2 = (bf16[4,128,128]{2,1,0:T(8,128)(2,1)}, bf16[4,128,128]{2,1,0:T(8,128)(2,1)S(1)}, u32[]{:S(2)}, u32[]{:S(2)}) collective-permute-start(bf16[4,128,128]{2,1,0:T(8,128)(2,1)} %bitcast.20), channel_id=1, source_target_pairs={{0,3},{1,2},{2,1},{3,0},{4,7},{5,6},{6,5},{7,4},{8,11},{9,10},{10,... | collective-permute-start | bytes 393224 | tf_op jit(solution)/shard_map/ppermute | solution.py:452
  14.9 2.0 %collective-permute-start.3 = (bf16[16,128,128]{2,1,0:T(8,128)(2,1)S(1)}, bf16[16,128,128]{2,1,0:T(8,128)(2,1)S(1)}, u32[]{:S(2)}, u32[]{:S(2)}) collective-permute-start(bf16[16,128,128]{2,1,0:T(8,128)(2,1)S(1)} %get-tuple-element.30), channel_id=1, source_target_pairs={{0,4},{4,0},{8,12},{12,8},{16,20},{20,16},{24,28},{28,24},{1,5},{5... | collective-permute-start | bytes 1572872 | tf_op jit(solution)/shard_map/ppermute | solution.py:436
  22.4 10.0 %collective-permute-start.10 = (bf16[24,128,128]{2,1,0:T(8,128)(2,1)S(1)}, bf16[24,128,128]{2,1,0:T(8,128)(2,1)S(1)}, u32[]{:S(2)}, u32[]{:S(2)}) collective-permute-start(bf16[24,128,128]{2,1,0:T(8,128)(2,1)S(1)} %get-tuple-element.37), channel_id=1, source_target_pairs={{0,4},{4,0},{8,12},{12,8},{16,20},{20,16},{24,28},{28,24},{1,5},{5... | collective-permute-start | bytes 2359304 | tf_op jit(solution)/shard_map/ppermute | solution.py:436
  23.1 14.9 %collective-permute-start.4 = (bf16[24,128,128]{2,1,0:T(8,128)(2,1)S(1)}, bf16[24,128,128]{2,1,0:T(8,128)(2,1)S(1)}, u32[]{:S(2)}, u32[]{:S(2)}) collective-permute-start(bf16[24,128,128]{2,1,0:T(8,128)(2,1)S(1)} %get-tuple-element.32), channel_id=1, source_target_pairs={{0,4},{4,0},{8,12},{12,8},{16,20},{20,16},{24,28},{28,24},{1,5},{5... | collective-permute-start | bytes 2359304 | tf_op jit(solution)/shard_map/ppermute | solution.py:436
  23.2 9.2 %collective-permute-start.11 = (bf16[8,128,128]{2,1,0:T(8,128)(2,1)S(1)}, bf16[8,128,128]{2,1,0:T(8,128)(2,1)S(1)}, u32[]{:S(2)}, u32[]{:S(2)}) collective-permute-start(bf16[8,128,128]{2,1,0:T(8,128)(2,1)S(1)} %shard_map.86.rest_4_), channel_id=1, source_target_pairs={{0,8},{4,12},{8,0},{12,4},{16,24},{20,28},{24,16},{28,20},{1,9},{5... | collective-permute-start | bytes 786440 | tf_op jit(solution)/shard_map/ppermute | solution.py:446
  23.9 14.1 %collective-permute-start.5 = (bf16[8,128,128]{2,1,0:T(8,128)(2,1)S(1)}, bf16[8,128,128]{2,1,0:T(8,128)(2,1)S(1)}, u32[]{:S(2)}, u32[]{:S(2)}) collective-permute-start(bf16[8,128,128]{2,1,0:T(8,128)(2,1)S(1)} %shard_map.87.rest_5_), channel_id=1, source_target_pairs={{0,8},{4,12},{8,0},{12,4},{16,24},{20,28},{24,16},{28,20},{1,9},{5... | collective-permute-start | bytes 786440 | tf_op jit(solution)/shard_map/ppermute | solution.py:446
  32.6 11.0 %collective-permute-start.12 = (bf16[8,128,128]{2,1,0:T(8,128)(2,1)S(1)}, bf16[8,128,128]{2,1,0:T(8,128)(2,1)S(1)}, u32[]{:S(2)}, u32[]{:S(2)}) collective-permute-start(bf16[8,128,128]{2,1,0:T(8,128)(2,1)S(1)} %get-tuple-element.38), channel_id=1, source_target_pairs={{0,8},{4,12},{8,0},{12,4},{16,24},{20,28},{24,16},{28,20},{1,9},{5... | collective-permute-start | bytes 786440 | tf_op jit(solution)/shard_map/ppermute | solution.py:446
  33.3 10.2 %collective-permute-start.13 = (bf16[8,128,128]{2,1,0:T(8,128)(2,1)S(1)}, bf16[8,128,128]{2,1,0:T(8,128)(2,1)S(1)}, u32[]{:S(2)}, u32[]{:S(2)}) collective-permute-start(bf16[8,128,128]{2,1,0:T(8,128)(2,1)S(1)} %get-tuple-element.39), channel_id=1, source_target_pairs={{0,4},{4,0},{8,16},{12,20},{16,8},{20,12},{24,28},{28,24},{1,5},{5... | collective-permute-start | bytes 786440 | tf_op jit(solution)/shard_map/ppermute | solution.py:446
  38.2 11.0 %collective-permute-start.6 = (bf16[8,128,128]{2,1,0:T(8,128)(2,1)S(1)}, bf16[8,128,128]{2,1,0:T(8,128)(2,1)S(1)}, u32[]{:S(2)}, u32[]{:S(2)}) collective-permute-start(bf16[8,128,128]{2,1,0:T(8,128)(2,1)S(1)} %get-tuple-element.33), channel_id=1, source_target_pairs={{0,8},{4,12},{8,0},{12,4},{16,24},{20,28},{24,16},{28,20},{1,9},{5... | collective-permute-start | bytes 786440 | tf_op jit(solution)/shard_map/ppermute | solution.py:446
  39.0 10.2 %collective-permute-start.7 = (bf16[8,128,128]{2,1,0:T(8,128)(2,1)S(1)}, bf16[8,128,128]{2,1,0:T(8,128)(2,1)S(1)}, u32[]{:S(2)}, u32[]{:S(2)}) collective-permute-start(bf16[8,128,128]{2,1,0:T(8,128)(2,1)S(1)} %get-tuple-element.34), channel_id=1, source_target_pairs={{0,4},{4,0},{8,16},{12,20},{16,8},{20,12},{24,28},{28,24},{1,5},{5... | collective-permute-start | bytes 786440 | tf_op jit(solution)/shard_map/ppermute | solution.py:446
  43.8 11.0 %copy-start = (f32[2048]{0:T(1024)S(1)}, f32[2048]{0:T(1024)}, u32[]{:S(2)}) copy-start(f32[2048]{0:T(1024)} %param.13) | copy-start | bytes 24580
  43.8 11.0 %collective-permute-start.14 = (bf16[8,128,128]{2,1,0:T(8,128)(2,1)S(1)}, bf16[8,128,128]{2,1,0:T(8,128)(2,1)S(1)}, u32[]{:S(2)}, u32[]{:S(2)}) collective-permute-start(bf16[8,128,128]{2,1,0:T(8,128)(2,1)S(1)} %get-tuple-element.40), channel_id=1, source_target_pairs={{0,8},{4,12},{8,0},{12,4},{16,24},{20,28},{24,16},{28,20},{1,9},{5... | collective-permute-start | bytes 786440 | tf_op jit(solution)/shard_map/ppermute | solution.py:446
  44.6 10.2 %collective-permute-start.15 = (bf16[8,128,128]{2,1,0:T(8,128)(2,1)S(1)}, bf16[8,128,128]{2,1,0:T(8,128)(2,1)S(1)}, u32[]{:S(2)}, u32[]{:S(2)}) collective-permute-start(bf16[8,128,128]{2,1,0:T(8,128)(2,1)S(1)} %get-tuple-element.41), channel_id=1, source_target_pairs={{0,4},{4,0},{8,16},{12,20},{16,8},{20,12},{24,28},{28,24},{1,5},{5... | collective-permute-start | bytes 786440 | tf_op jit(solution)/shard_map/ppermute | solution.py:446
  49.4 10.5 %collective-permute-start.8 = (bf16[8,128,128]{2,1,0:T(8,128)(2,1)S(1)}, bf16[8,128,128]{2,1,0:T(8,128)(2,1)S(1)}, u32[]{:S(2)}, u32[]{:S(2)}) collective-permute-start(bf16[8,128,128]{2,1,0:T(8,128)(2,1)S(1)} %get-tuple-element.35), channel_id=1, source_target_pairs={{0,8},{4,12},{8,0},{12,4},{16,24},{20,28},{24,16},{28,20},{1,9},{5... | collective-permute-start | bytes 786440 | tf_op jit(solution)/shard_map/ppermute | solution.py:446
  50.2 9.7 %collective-permute-start.9 = (bf16[8,128,128]{2,1,0:T(8,128)(2,1)S(1)}, bf16[8,128,128]{2,1,0:T(8,128)(2,1)S(1)}, u32[]{:S(2)}, u32[]{:S(2)}) collective-permute-start(bf16[8,128,128]{2,1,0:T(8,128)(2,1)S(1)} %get-tuple-element.36), channel_id=1, source_target_pairs={{0,4},{4,0},{8,16},{12,20},{16,8},{20,12},{24,28},{28,24},{1,5},{5... | collective-permute-start | bytes 786440 | tf_op jit(solution)/shard_map/ppermute | solution.py:446
  60.7 4.3 %collective-permute-start.16 = (f32[128,128]{1,0:T(8,128)S(1)}, f32[128,128]{1,0:T(8,128)S(1)}, u32[]{:S(2)}, u32[]{:S(2)}) collective-permute-start(f32[128,128]{1,0:T(8,128)S(1)} %get-tuple-element.43), channel_id=1, source_target_pairs={{0,8},{4,12},{8,0},{12,4},{16,24},{20,28},{24,16},{28,20},{1,9},{5... | collective-permute-start | bytes 196616 | tf_op jit(solution)/shard_map/ppermute | solution.py:510
  65.0 5.3 %collective-permute-start.17 = (f32[128,128]{1,0:T(8,128)S(1)}, f32[128,128]{1,0:T(8,128)S(1)}, u32[]{:S(2)}, u32[]{:S(2)}) collective-permute-start(f32[128,128]{1,0:T(8,128)S(1)} %add.18), channel_id=1, source_target_pairs={{0,16},{4,20},{8,24},{12,28},{16,0},{20,4},{24,8},{28,12},{1,17},{... | collective-permute-start | bytes 196616 | tf_op jit(solution)/shard_map/ppermute | solution.py:510
  67.8 9.2 %collective-permute-start.22 = (bf16[8,128,128]{2,1,0:T(8,128)(2,1)S(1)}, bf16[8,128,128]{2,1,0:T(8,128)(2,1)S(1)}, u32[]{:S(2)}, u32[]{:S(2)}) collective-permute-start(bf16[8,128,128]{2,1,0:T(8,128)(2,1)S(1)} %get-tuple-element.46.rest_0_), channel_id=1, source_target_pairs={{0,8},{4,12},{8,0},{12,4},{16,24},{20,28},{24,16},{28,20},{1,9},{5... | collective-permute-start | bytes 786440 | tf_op jit(solution)/shard_map/ppermute | solution.py:446
  69.5 10.9 %collective-permute-start.26 = (bf16[8,128,128]{2,1,0:T(8,128)(2,1)S(1)}, bf16[8,128,128]{2,1,0:T(8,128)(2,1)S(1)}, u32[]{:S(2)}, u32[]{:S(2)}) collective-permute-start(bf16[8,128,128]{2,1,0:T(8,128)(2,1)S(1)} %get-tuple-element.47.rest_2_), channel_id=1, source_target_pairs={{0,8},{4,12},{8,0},{12,4},{16,24},{20,28},{24,16},{28,20},{1,9},{5... | collective-permute-start | bytes 786440 | tf_op jit(solution)/shard_map/ppermute | solution.py:446
  69.8 10.6 %collective-permute-start.30 = (bf16[8,128,128]{2,1,0:T(8,128)(2,1)S(1)}, bf16[8,128,128]{2,1,0:T(8,128)(2,1)S(1)}, u32[]{:S(2)}, u32[]{:S(2)}) collective-permute-start(bf16[8,128,128]{2,1,0:T(8,128)(2,1)S(1)} %get-tuple-element.46.rest_0_), channel_id=1, source_target_pairs={{0,4},{4,0},{8,16},{12,20},{16,8},{20,12},{24,28},{28,24},{1,5},{5... | collective-permute-start | bytes 786440 | tf_op jit(solution)/shard_map/ppermute | solution.py:446
  69.8 11.1 %collective-permute-start.34 = (bf16[8,128,128]{2,1,0:T(8,128)(2,1)S(1)}, bf16[8,128,128]{2,1,0:T(8,128)(2,1)S(1)}, u32[]{:S(2)}, u32[]{:S(2)}) collective-permute-start(bf16[8,128,128]{2,1,0:T(8,128)(2,1)S(1)} %get-tuple-element.47.rest_2_), channel_id=1, source_target_pairs={{0,4},{4,0},{8,16},{12,20},{16,8},{20,12},{24,28},{28,24},{1,5},{5... | collective-permute-start | bytes 786440 | tf_op jit(solution)/shard_map/ppermute | solution.py:446
  70.4 13.9 %collective-permute-start.38 = (bf16[8,128,128]{2,1,0:T(8,128)(2,1)S(1)}, bf16[8,128,128]{2,1,0:T(8,128)(2,1)S(1)}, u32[]{:S(2)}, u32[]{:S(2)}) collective-permute-start(bf16[8,128,128]{2,1,0:T(8,128)(2,1)S(1)} %get-tuple-element.46.rest_0_), channel_id=1, source_target_pairs={{0,4},{4,0},{8,12},{12,8},{16,20},{20,16},{24,28},{28,24},{1,5},{5... | collective-permute-start | bytes 786440 | tf_op jit(solution)/shard_map/ppermute | solution.py:436
  77.0 7.3 %collective-permute-start.39 = (bf16[8,128,128]{2,1,0:T(8,128)(2,1)S(1)}, bf16[8,128,128]{2,1,0:T(8,128)(2,1)S(1)}, u32[]{:S(2)}, u32[]{:S(2)}) collective-permute-start(bf16[8,128,128]{2,1,0:T(8,128)(2,1)S(1)} %get-tuple-element.47.rest_2_), channel_id=1, source_target_pairs={{0,4},{4,0},{8,12},{12,8},{16,20},{20,16},{24,28},{28,24},{1,5},{5... | collective-permute-start | bytes 786440 | tf_op jit(solution)/shard_map/ppermute | solution.py:436
  80.4 4.0 %collective-permute-start.23 = (bf16[8,128,128]{2,1,0:T(8,128)(2,1)S(1)}, bf16[8,128,128]{2,1,0:T(8,128)(2,1)S(1)}, u32[]{:S(2)}, u32[]{:S(2)}) collective-permute-start(bf16[8,128,128]{2,1,0:T(8,128)(2,1)S(1)} %collective-permute-done.22.rest_4_), channel_id=1, source_target_pairs={{0,4},{4,0},{8,16},{12,20},{16,8},{20,12},{24,28},{28,24},{1,5},{5... | collective-permute-start | bytes 786440 | tf_op jit(solution)/shard_map/ppermute | solution.py:446
  80.4 4.4 %collective-permute-start.27 = (bf16[8,128,128]{2,1,0:T(8,128)(2,1)S(1)}, bf16[8,128,128]{2,1,0:T(8,128)(2,1)S(1)}, u32[]{:S(2)}, u32[]{:S(2)}) collective-permute-start(bf16[8,128,128]{2,1,0:T(8,128)(2,1)S(1)} %collective-permute-done.26.rest_8_), channel_id=1, source_target_pairs={{0,4},{4,0},{8,16},{12,20},{16,8},{20,12},{24,28},{28,24},{1,5},{5... | collective-permute-start | bytes 786440 | tf_op jit(solution)/shard_map/ppermute | solution.py:446
  80.9 10.5 %collective-permute-start.31 = (bf16[8,128,128]{2,1,0:T(8,128)(2,1)S(1)}, bf16[8,128,128]{2,1,0:T(8,128)(2,1)S(1)}, u32[]{:S(2)}, u32[]{:S(2)}) collective-permute-start(bf16[8,128,128]{2,1,0:T(8,128)(2,1)S(1)} %collective-permute-done.30.rest_6_), channel_id=1, source_target_pairs={{0,8},{4,12},{8,0},{12,4},{16,24},{20,28},{24,16},{28,20},{1,9},{5... | collective-permute-start | bytes 786440 | tf_op jit(solution)/shard_map/ppermute | solution.py:446
  84.3 10.6 %collective-permute-start.35 = (bf16[8,128,128]{2,1,0:T(8,128)(2,1)S(1)}, bf16[8,128,128]{2,1,0:T(8,128)(2,1)S(1)}, u32[]{:S(2)}, u32[]{:S(2)}) collective-permute-start(bf16[8,128,128]{2,1,0:T(8,128)(2,1)S(1)} %collective-permute-done.34.rest_10_), channel_id=1, source_target_pairs={{0,8},{4,12},{8,0},{12,4},{16,24},{20,28},{24,16},{28,20},{1,9},{5... | collective-permute-start | bytes 786440 | tf_op jit(solution)/shard_map/ppermute | solution.py:446
  84.3 10.8 %collective-permute-start.40 = (bf16[8,128,128]{2,1,0:T(8,128)(2,1)S(1)}, bf16[8,128,128]{2,1,0:T(8,128)(2,1)S(1)}, u32[]{:S(2)}, u32[]{:S(2)}) collective-permute-start(bf16[8,128,128]{2,1,0:T(8,128)(2,1)S(1)} %collective-permute-done.22.rest_4_), channel_id=1, source_target_pairs={{0,4},{4,0},{8,12},{12,8},{16,20},{20,16},{24,28},{28,24},{1,5},{5... | collective-permute-start | bytes 786440 | tf_op jit(solution)/shard_map/ppermute | solution.py:436
  84.4 10.8 %collective-permute-start.41 = (bf16[8,128,128]{2,1,0:T(8,128)(2,1)S(1)}, bf16[8,128,128]{2,1,0:T(8,128)(2,1)S(1)}, u32[]{:S(2)}, u32[]{:S(2)}) collective-permute-start(bf16[8,128,128]{2,1,0:T(8,128)(2,1)S(1)} %collective-permute-done.30.rest_6_), channel_id=1, source_target_pairs={{0,4},{4,0},{8,12},{12,8},{16,20},{20,16},{24,28},{28,24},{1,5},{5... | collective-permute-start | bytes 786440 | tf_op jit(solution)/shard_map/ppermute | solution.py:436
  84.8 12.2 %collective-permute-start.42 = (bf16[8,128,128]{2,1,0:T(8,128)(2,1)S(1)}, bf16[8,128,128]{2,1,0:T(8,128)(2,1)S(1)}, u32[]{:S(2)}, u32[]{:S(2)}) collective-permute-start(bf16[8,128,128]{2,1,0:T(8,128)(2,1)S(1)} %collective-permute-done.26.rest_8_), channel_id=1, source_target_pairs={{0,4},{4,0},{8,12},{12,8},{16,20},{20,16},{24,28},{28,24},{1,5},{5... | collective-permute-start | bytes 786440 | tf_op jit(solution)/shard_map/ppermute | solution.py:436
  91.4 5.8 %collective-permute-start.43 = (bf16[8,128,128]{2,1,0:T(8,128)(2,1)S(1)}, bf16[8,128,128]{2,1,0:T(8,128)(2,1)S(1)}, u32[]{:S(2)}, u32[]{:S(2)}) collective-permute-start(bf16[8,128,128]{2,1,0:T(8,128)(2,1)S(1)} %collective-permute-done.34.rest_10_), channel_id=1, source_target_pairs={{0,4},{4,0},{8,12},{12,8},{16,20},{20,16},{24,28},{28,24},{1,5},{5... | collective-permute-start | bytes 786440 | tf_op jit(solution)/shard_map/ppermute | solution.py:436
  94.8 9.2 %collective-permute-start.24 = (bf16[8,128,128]{2,1,0:T(8,128)(2,1)S(1)}, bf16[8,128,128]{2,1,0:T(8,128)(2,1)S(1)}, u32[]{:S(2)}, u32[]{:S(2)}) collective-permute-start(bf16[8,128,128]{2,1,0:T(8,128)(2,1)S(1)} %collective-permute-done.23.rest_2_), channel_id=1, source_target_pairs={{0,8},{4,12},{8,0},{12,4},{16,24},{20,28},{24,16},{28,20},{1,9},{5... | collective-permute-start | bytes 786440 | tf_op jit(solution)/shard_map/ppermute | solution.py:446
  95.1 16.6 %collective-permute-start.33 = (bf16[8,128,128]{2,1,0:T(8,128)(2,1)S(1)}, bf16[8,128,128]{2,1,0:T(8,128)(2,1)S(1)}, u32[]{:S(2)}, u32[]{:S(2)}) collective-permute-start(bf16[8,128,128]{2,1,0:T(8,128)(2,1)S(1)} %collective-permute-done.23.rest_2_), channel_id=1, source_target_pairs={{0,4},{4,0},{8,12},{12,8},{16,20},{20,16},{24,28},{28,24},{1,5},{5... | collective-permute-start | bytes 786440 | tf_op jit(solution)/shard_map/ppermute | solution.py:436
  95.2 13.4 %collective-permute-start.28 = (bf16[8,128,128]{2,1,0:T(8,128)(2,1)S(1)}, bf16[8,128,128]{2,1,0:T(8,128)(2,1)S(1)}, u32[]{:S(2)}, u32[]{:S(2)}) collective-permute-start(bf16[8,128,128]{2,1,0:T(8,128)(2,1)S(1)} %collective-permute-done.27.rest_6_), channel_id=1, source_target_pairs={{0,8},{4,12},{8,0},{12,4},{16,24},{20,28},{24,16},{28,20},{1,9},{5... | collective-permute-start | bytes 786440 | tf_op jit(solution)/shard_map/ppermute | solution.py:446
  97.0 15.4 %collective-permute-start.37 = (bf16[8,128,128]{2,1,0:T(8,128)(2,1)S(1)}, bf16[8,128,128]{2,1,0:T(8,128)(2,1)S(1)}, u32[]{:S(2)}, u32[]{:S(2)}) collective-permute-start(bf16[8,128,128]{2,1,0:T(8,128)(2,1)S(1)} %collective-permute-done.27.rest_6_), channel_id=1, source_target_pairs={{0,4},{4,0},{8,12},{12,8},{16,20},{20,16},{24,28},{28,24},{1,5},{5... | collective-permute-start | bytes 786440 | tf_op jit(solution)/shard_map/ppermute | solution.py:436
  97.2 14.5 %collective-permute-start.32 = (bf16[8,128,128]{2,1,0:T(8,128)(2,1)S(1)}, bf16[8,128,128]{2,1,0:T(8,128)(2,1)S(1)}, u32[]{:S(2)}, u32[]{:S(2)}) collective-permute-start(bf16[8,128,128]{2,1,0:T(8,128)(2,1)S(1)} %collective-permute-done.31.rest_0_), channel_id=1, source_target_pairs={{0,4},{4,0},{8,12},{12,8},{16,20},{20,16},{24,28},{28,24},{1,5},{5... | collective-permute-start | bytes 786440 | tf_op jit(solution)/shard_map/ppermute | solution.py:436
  104.0 8.4 %collective-permute-start.36 = (bf16[8,128,128]{2,1,0:T(8,128)(2,1)S(1)}, bf16[8,128,128]{2,1,0:T(8,128)(2,1)S(1)}, u32[]{:S(2)}, u32[]{:S(2)}) collective-permute-start(bf16[8,128,128]{2,1,0:T(8,128)(2,1)S(1)} %collective-permute-done.35.rest_4_), channel_id=1, source_target_pairs={{0,4},{4,0},{8,12},{12,8},{16,20},{20,16},{24,28},{28,24},{1,5},{5... | collective-permute-start | bytes 786440 | tf_op jit(solution)/shard_map/ppermute | solution.py:436
  108.6 14.1 %collective-permute-start.20 = (f32[128,128]{1,0:T(8,128)S(1)}, f32[128,128]{1,0:T(8,128)S(1)}, u32[]{:S(2)}, u32[]{:S(2)}) collective-permute-start(f32[128,128]{1,0:T(8,128)S(1)} %add.19), channel_id=1, source_target_pairs={{0,3},{1,0},{2,1},{3,2},{4,7},{5,4},{6,5},{7,6},{8,11},{9,8},{10,9... | collective-permute-start | bytes 196616 | tf_op jit(solution)/shard_map/ppermute | solution.py:403
  111.7 12.5 %collective-permute-start.19 = (f32[128,128]{1,0:T(8,128)S(1)}, f32[128,128]{1,0:T(8,128)S(1)}, u32[]{:S(2)}, u32[]{:S(2)}) collective-permute-start(f32[128,128]{1,0:T(8,128)S(1)} %add.19), channel_id=1, source_target_pairs={{0,2},{1,3},{2,0},{3,1},{4,6},{5,7},{6,4},{7,5},{8,10},{9,11},{10,... | collective-permute-start | bytes 196616 | tf_op jit(solution)/shard_map/ppermute | solution.py:403
  111.7 12.5 %collective-permute-start.18 = (f32[128,128]{1,0:T(8,128)S(1)}, f32[128,128]{1,0:T(8,128)S(1)}, u32[]{:S(2)}, u32[]{:S(2)}) collective-permute-start(f32[128,128]{1,0:T(8,128)S(1)} %add.19), channel_id=1, source_target_pairs={{0,1},{1,2},{2,3},{3,0},{4,5},{5,6},{6,7},{7,4},{8,9},{9,10},{10,1... | collective-permute-start | bytes 196616 | tf_op jit(solution)/shard_map/ppermute | solution.py:403
  112.4 3.8 %collective-permute-start.25 = (bf16[8,128,128]{2,1,0:T(8,128)(2,1)S(1)}, bf16[8,128,128]{2,1,0:T(8,128)(2,1)S(1)}, u32[]{:S(2)}, u32[]{:S(2)}) collective-permute-start(bf16[8,128,128]{2,1,0:T(8,128)(2,1)S(1)} %collective-permute-done.24.rest_0_), channel_id=1, source_target_pairs={{0,4},{4,0},{8,12},{12,8},{16,20},{20,16},{24,28},{28,24},{1,5},{5... | collective-permute-start | bytes 786440 | tf_op jit(solution)/shard_map/ppermute | solution.py:436
  112.4 3.8 %collective-permute-start.29 = (bf16[8,128,128]{2,1,0:T(8,128)(2,1)S(1)}, bf16[8,128,128]{2,1,0:T(8,128)(2,1)S(1)}, u32[]{:S(2)}, u32[]{:S(2)}) collective-permute-start(bf16[8,128,128]{2,1,0:T(8,128)(2,1)S(1)} %collective-permute-done.28.rest_2_), channel_id=1, source_target_pairs={{0,4},{4,0},{8,12},{12,8},{16,20},{20,16},{24,28},{28,24},{1,5},{5... | collective-permute-start | bytes 786440 | tf_op jit(solution)/shard_map/ppermute | solution.py:436
  119.4 15.2 %collective-permute-start.44 = (bf16[4,128,128]{2,1,0:T(8,128)(2,1)S(1)}, bf16[4,128,128]{2,1,0:T(8,128)(2,1)S(1)}, u32[]{:S(2)}, u32[]{:S(2)}) collective-permute-start(bf16[4,128,128]{2,1,0:T(8,128)(2,1)S(1)} %get-tuple-element.49), channel_id=1, source_target_pairs={{0,1},{1,0},{2,3},{3,2},{4,5},{5,4},{6,7},{7,6},{8,9},{9,8},{10,11... | collective-permute-start | bytes 393224 | tf_op jit(solution)/shard_map/ppermute | solution.py:452
  122.7 11.9 %collective-permute-start.45 = (bf16[4,128,128]{2,1,0:T(8,128)(2,1)S(1)}, bf16[4,128,128]{2,1,0:T(8,128)(2,1)S(1)}, u32[]{:S(2)}, u32[]{:S(2)}) collective-permute-start(bf16[4,128,128]{2,1,0:T(8,128)(2,1)S(1)} %get-tuple-element.50), channel_id=1, source_target_pairs={{0,2},{1,3},{2,0},{3,1},{4,6},{5,7},{6,4},{7,5},{8,10},{9,11},{10,... | collective-permute-start | bytes 393224 | tf_op jit(solution)/shard_map/ppermute | solution.py:452
  122.7 11.9 %collective-permute-start.46 = (bf16[4,128,128]{2,1,0:T(8,128)(2,1)S(1)}, bf16[4,128,128]{2,1,0:T(8,128)(2,1)S(1)}, u32[]{:S(2)}, u32[]{:S(2)}) collective-permute-start(bf16[4,128,128]{2,1,0:T(8,128)(2,1)S(1)} %get-tuple-element.51), channel_id=1, source_target_pairs={{0,3},{1,2},{2,1},{3,0},{4,7},{5,6},{6,5},{7,4},{8,11},{9,10},{10,... | collective-permute-start | bytes 393224 | tf_op jit(solution)/shard_map/ppermute | solution.py:452
  124.2 1.3 collective-permute-start.21
